TPU v7x, 32 devices: a whole 2x2x4 slice. The times are simulated.
32 devices in a mesh: dp: 4 (over y, x), seq: 8 (over z, core).
Axes of the slice: x: 2, y: 2, z: 4, core: 2. Of those that a mesh axis runs over, the one named last changes fastest.
Arguments:
- hidden: float32 [4, 2048, 768], P('dp', 'seq'), may hold values from -6 to 6
- cotangent: float32 [4, 2048, 768], P('dp', 'seq'), may hold values from -6 to 6
- lengths: int32 [4], P('dp'), may hold values from 1024 to 2048, as said below
- norm_gain: float32 [2, 768], P(None, 'dp'), may hold values from 0.5 to 1.5
- gate_weight: float32 [2, 768, 1536], P(None, 'dp'), may hold values from -0.21875 to 0.21875
- mix_weight: float32 [2, 768, 1792], P(None, 'dp'), may hold values from -0.21875 to 0.21875
- step_weight: float32 [2, 768, 24], P(None, 'dp'), may hold values from -0.21875 to 0.21875
- conv_kernel: float32 [2, 4, 1792], P(None, None, 'dp'), may hold values from -0.5 to 0.5
- conv_bias: float32 [2, 1792], P(None, 'dp'), may hold values from -0.5 to 0.5
- gated_gain: float32 [2, 1536], P(None, 'dp'), may hold values from 0.5 to 1.5
- out_weight: float32 [2, 1536, 768], P(None, 'dp'), may hold values from -0.15625 to 0.15625
- skip_gain: float32 [2, 24], replicated, may hold values from 0.5 to 1.5
- log_rate: float32 [2, 24], replicated, may hold values from -4 to 1
- step_bias: float32 [2, 24], replicated, may hold values from -9 to -4
Outputs:
- result: float32 [4, 2048, 768], P('dp', 'seq')
- hidden_grad: float32 [4, 2048, 768], P('dp', 'seq')
- norm_gain_grad: float32 [2, 768], P(None, 'dp')
- gate_weight_grad: float32 [2, 768, 1536], P(None, 'dp')
- mix_weight_grad: float32 [2, 768, 1792], P(None, 'dp')
- step_weight_grad: float32 [2, 768, 24], P(None, 'dp')
- conv_kernel_grad: float32 [2, 4, 1792], P(None, None, 'dp')
- conv_bias_grad: float32 [2, 1792], P(None, 'dp')
- gated_gain_grad: float32 [2, 1536], P(None, 'dp')
- out_weight_grad: float32 [2, 1536, 768], P(None, 'dp')
- skip_gain_grad: float32 [2, 24], replicated
Inputs may be any that keep to these rules, and one draw needn't show every extreme that they name: `lengths`: positions at or past a slot's length are padding; some slot has length 2048 and some slot the least length.
All inputs are finite; a program needn't handle non-finite values.
Results may differ from a plain program's by a relative error of at most 0.0003.
Values sent between devices are 32-bit elements; how exact they have to be, the bound alone decides.
A program may use at most 192 MiB of HBM per device.

v0:
```python
import jax
import jax.numpy as jnp
from jax import lax
from jax.sharding import PartitionSpec as P

EPSILON = 1e-05
HIGHEST = lax.Precision.HIGHEST


def from_behind(value, axis, steps):
    count = lax.axis_size(axis)
    first, last = (max(0, -steps), min(count, count - steps))
    return lax.ppermute(value, axis, [(source, source + steps) for source in range(first, last)])


def matmul(left, right):
    return jnp.dot(left, right, precision=HIGHEST)


def rms_scale(values):
    return lax.rsqrt(jnp.mean(values * values, axis=-1, keepdims=True) + EPSILON)


def carry_forward(totals, state_local):

    def relay_turn(turn_index, incoming):
        return from_behind(totals[:, :, None, None] * incoming + state_local, "seq", 1)

    return lax.fori_loop(0, lax.axis_size("seq") - 1, relay_turn, jnp.zeros_like(state_local))


def carry_backward(totals, state_in_grad):

    def relay_back(turn_index, incoming):
        return from_behind(totals[:, :, None, None] * incoming + state_in_grad, "seq", -1)

    return lax.fori_loop(0, lax.axis_size("seq") - 1, relay_back, jnp.zeros_like(state_in_grad))


def layer_forward(stream, weights, skip_gain, log_rate, step_bias):
    (
        norm_gain,
        gate_weight,
        mix_weight,
        step_weight,
        conv_kernel,
        conv_bias,
        gated_gain,
        out_weight,
    ) = weights
    slots, group, width = stream.shape
    inner = gated_gain.shape[0]
    heads = skip_gain.shape[0]
    head_size = inner // heads
    taps = conv_kernel.shape[0]
    flat = stream.reshape(slots * group, width)
    inv_in = rms_scale(flat)
    normed = flat * inv_in * norm_gain
    gate_pre = matmul(normed, gate_weight)
    mixed_raw = matmul(normed, mix_weight).reshape(slots, group, -1)
    step_raw = matmul(normed, step_weight).reshape(slots, group, heads)
    channels = mixed_raw.shape[-1]
    states = (channels - inner) // 2
    edge = from_behind(mixed_raw[:, group - taps + 1 :, :], "seq", 1)
    extended = jnp.concatenate([edge, mixed_raw], axis=1)
    conv_pre = conv_bias
    for tap_index in range(taps):
        conv_pre = conv_pre + conv_kernel[tap_index] * extended[:, tap_index : tap_index + group, :]
    mixed = jax.nn.silu(conv_pre)
    heads_in = mixed[..., :inner].reshape(slots, group, heads, head_size)
    input_map = mixed[..., inner : inner + states]
    output_map = mixed[..., inner + states :]
    step_size = jax.nn.softplus(step_raw + step_bias)
    rates = jnp.exp(log_rate)
    log_decay = jnp.cumsum(-rates * step_size, axis=1)
    scaled_in = heads_in * step_size[..., None]
    position = lax.iota(jnp.int32, group)
    causal = (position[:, None] >= position[None, :])[None, :, :, None]
    gaps = log_decay[:, :, None, :] - log_decay[:, None, :, :]
    decays = jnp.where(causal, jnp.exp(jnp.where(causal, gaps, 0.0)), 0.0)
    intersection = jnp.einsum("btn,bsn->bts", output_map, input_map, precision=HIGHEST)
    mixing = intersection[..., None] * decays
    diag_out = jnp.einsum("btsh,bshp->bthp", mixing, scaled_in, precision=HIGHEST)
    end_weight = jnp.exp(log_decay[:, -1:, :] - log_decay)
    state_local = jnp.einsum(
        "bshp,bsn->bhpn", scaled_in * end_weight[..., None], input_map, precision=HIGHEST
    )
    totals = jnp.exp(log_decay[:, -1, :])
    state_in = carry_forward(totals, state_local)
    lift = jnp.exp(log_decay)
    off_out = lift[..., None] * jnp.einsum(
        "btn,bhpn->bthp", output_map, state_in, precision=HIGHEST
    )
    mixed_out = diag_out + off_out + skip_gain[:, None] * heads_in
    out_flat = mixed_out.reshape(slots * group, inner)
    gate_sig = jax.nn.sigmoid(gate_pre)
    gated = out_flat * (gate_pre * gate_sig)
    inv_out = rms_scale(gated)
    normed_out = gated * inv_out * gated_gain
    branch = matmul(normed_out, out_weight)
    saved = {
        "flat": flat,
        "inv_in": inv_in,
        "normed": normed,
        "gate_pre": gate_pre,
        "gate_sig": gate_sig,
        "step_raw": step_raw,
        "extended": extended,
        "conv_pre": conv_pre,
        "heads_in": heads_in,
        "input_map": input_map,
        "output_map": output_map,
        "step_size": step_size,
        "scaled_in": scaled_in,
        "decays": decays,
        "mixing": mixing,
        "end_weight": end_weight,
        "totals": totals,
        "state_in": state_in,
        "lift": lift,
        "off_out": off_out,
        "out_flat": out_flat,
        "gated": gated,
        "inv_out": inv_out,
        "normed_out": normed_out,
    }
    return (stream + branch.reshape(slots, group, width), saved)


def layer_backward(grad, saved, weights, skip_gain, log_rate, step_bias):
    (
        norm_gain,
        gate_weight,
        mix_weight,
        step_weight,
        conv_kernel,
        conv_bias,
        gated_gain,
        out_weight,
    ) = weights
    slots, group, width = grad.shape
    inner = gated_gain.shape[0]
    heads = skip_gain.shape[0]
    head_size = inner // heads
    taps = conv_kernel.shape[0]
    flat = saved["flat"]
    inv_in = saved["inv_in"]
    normed = saved["normed"]
    gate_pre = saved["gate_pre"]
    gate_sig = saved["gate_sig"]
    heads_in = saved["heads_in"]
    input_map = saved["input_map"]
    output_map = saved["output_map"]
    scaled_in = saved["scaled_in"]
    end_weight = saved["end_weight"]
    totals = saved["totals"]
    state_in = saved["state_in"]
    mixing = saved["mixing"]
    gated = saved["gated"]
    inv_out = saved["inv_out"]
    conv_pre = saved["conv_pre"]
    extended = saved["extended"]
    channels = extended.shape[-1]
    grad_flat = grad.reshape(slots * group, width)
    out_weight_grad = matmul(saved["normed_out"].T, grad_flat)
    normed_out_grad = matmul(grad_flat, out_weight.T)
    gated_gain_grad = jnp.sum(normed_out_grad * gated * inv_out, axis=0)
    scaled = normed_out_grad * gated_gain
    gated_grad = inv_out * scaled - gated * (inv_out * inv_out * inv_out) * jnp.mean(
        scaled * gated, axis=-1, keepdims=True
    )
    gate_grad = gated_grad * saved["out_flat"] * gate_sig * (1.0 + gate_pre * (1.0 - gate_sig))
    out_grad = (gated_grad * (gate_pre * gate_sig)).reshape(slots, group, heads, head_size)
    skip_grad = jnp.sum(out_grad * heads_in, axis=(0, 1, 3))
    heads_grad = skip_gain[:, None] * out_grad
    lifted_grad = out_grad * saved["lift"][..., None]
    state_in_grad = jnp.einsum("bthp,btn->bhpn", lifted_grad, output_map, precision=HIGHEST)
    output_map_grad = jnp.einsum("bthp,bhpn->btn", lifted_grad, state_in, precision=HIGHEST)
    decay_grad = jnp.sum(out_grad * saved["off_out"], axis=-1)
    pairing = jnp.einsum("bthp,bshp->btsh", out_grad, scaled_in, precision=HIGHEST)
    scaled_grad = jnp.einsum("btsh,bthp->bshp", mixing, out_grad, precision=HIGHEST)
    intersection_grad = jnp.sum(saved["decays"] * pairing, axis=-1)
    output_map_grad = output_map_grad + jnp.einsum(
        "bts,bsn->btn", intersection_grad, input_map, precision=HIGHEST
    )
    input_map_grad = jnp.einsum("bts,btn->bsn", intersection_grad, output_map, precision=HIGHEST)
    weighted = mixing * pairing
    decay_grad = decay_grad + jnp.sum(weighted, axis=2) - jnp.sum(weighted, axis=1)
    state_out_grad = carry_backward(totals, state_in_grad)
    end_grad = jnp.sum(state_out_grad * state_in, axis=(2, 3)) * totals
    reach = jnp.einsum("bhpn,bsn->bshp", state_out_grad, input_map, precision=HIGHEST)
    scaled_grad = scaled_grad + reach * end_weight[..., None]
    input_map_grad = input_map_grad + jnp.einsum(
        "bshp,bhpn->bsn", scaled_in * end_weight[..., None], state_out_grad, precision=HIGHEST
    )
    weight_pull = jnp.sum(reach * scaled_in, axis=-1) * end_weight
    end_grad = end_grad + jnp.sum(weight_pull, axis=1)
    decay_grad = decay_grad - weight_pull
    decay_grad = jnp.concatenate(
        [decay_grad[:, :-1, :], decay_grad[:, -1:, :] + end_grad[:, None, :]], axis=1
    )
    rate_grad = jnp.flip(jnp.cumsum(jnp.flip(decay_grad, axis=1), axis=1), axis=1)
    step_grad = -jnp.exp(log_rate) * rate_grad + jnp.sum(scaled_grad * heads_in, axis=-1)
    heads_grad = heads_grad + scaled_grad * saved["step_size"][..., None]
    step_raw_grad = step_grad * jax.nn.sigmoid(saved["step_raw"] + step_bias)
    mixed_grad = jnp.concatenate(
        [heads_grad.reshape(slots, group, inner), input_map_grad, output_map_grad], axis=-1
    )
    conv_sig = jax.nn.sigmoid(conv_pre)
    pre_grad = mixed_grad * conv_sig * (1.0 + conv_pre * (1.0 - conv_sig))
    conv_bias_grad = jnp.sum(pre_grad, axis=(0, 1))
    conv_kernel_grad = jnp.stack(
        [
            jnp.sum(pre_grad * extended[:, tap_index : tap_index + group, :], axis=(0, 1))
            for tap_index in range(taps)
        ]
    )
    border = jnp.zeros((slots, taps - 1, channels), jnp.float32)
    padded_grad = jnp.concatenate([border, pre_grad, border], axis=1)
    extended_grad = conv_kernel[0] * padded_grad[:, taps - 1 : taps - 1 + group + taps - 1, :]
    for tap_index in range(1, taps):
        offset = taps - 1 - tap_index
        extended_grad = (
            extended_grad
            + conv_kernel[tap_index] * padded_grad[:, offset : offset + group + taps - 1, :]
        )
    edge_back = from_behind(extended_grad[:, : taps - 1, :], "seq", -1)
    raw_grad = extended_grad[:, taps - 1 :, :]
    raw_grad = jnp.concatenate(
        [raw_grad[:, : group - taps + 1, :], raw_grad[:, group - taps + 1 :, :] + edge_back], axis=1
    )
    raw_flat = raw_grad.reshape(slots * group, channels)
    step_flat = step_raw_grad.reshape(slots * group, heads)
    gate_weight_grad = matmul(normed.T, gate_grad)
    mix_weight_grad = matmul(normed.T, raw_flat)
    step_weight_grad = matmul(normed.T, step_flat)
    normed_grad = (
        matmul(gate_grad, gate_weight.T)
        + matmul(raw_flat, mix_weight.T)
        + matmul(step_flat, step_weight.T)
    )
    norm_gain_grad = jnp.sum(normed_grad * flat * inv_in, axis=0)
    scaled_norm = normed_grad * norm_gain
    stream_grad = (
        grad_flat
        + inv_in * scaled_norm
        - flat * (inv_in * inv_in * inv_in) * jnp.mean(scaled_norm * flat, axis=-1, keepdims=True)
    )
    weight_grads = (
        norm_gain_grad,
        gate_weight_grad,
        mix_weight_grad,
        step_weight_grad,
        conv_kernel_grad,
        conv_bias_grad,
        gated_gain_grad,
        out_weight_grad,
    )
    return (stream_grad.reshape(slots, group, width), weight_grads, skip_grad)


def on_device(
    hidden,
    cotangent,
    lengths,
    norm_gain,
    gate_weight,
    mix_weight,
    step_weight,
    conv_kernel,
    conv_bias,
    gated_gain,
    out_weight,
    skip_gain,
    log_rate,
    step_bias,
):
    slots, group, width = hidden.shape
    layers = norm_gain.shape[0]
    position = lax.axis_index("seq") * group + lax.iota(jnp.int32, group)
    mask = (position[None, :] < lengths[:, None]).astype(jnp.float32)[:, :, None]
    stream = hidden
    saved_all = []
    for layer_index in range(layers):
        weights = (
            lax.all_gather(norm_gain[layer_index], "dp", axis=0, tiled=True),
            lax.all_gather(gate_weight[layer_index], "dp", axis=0, tiled=True),
            lax.all_gather(mix_weight[layer_index], "dp", axis=0, tiled=True),
            lax.all_gather(step_weight[layer_index], "dp", axis=0, tiled=True),
            lax.all_gather(conv_kernel[layer_index], "dp", axis=1, tiled=True),
            lax.all_gather(conv_bias[layer_index], "dp", axis=0, tiled=True),
            lax.all_gather(gated_gain[layer_index], "dp", axis=0, tiled=True),
            lax.all_gather(out_weight[layer_index], "dp", axis=0, tiled=True),
        )
        stream, saved = layer_forward(
            stream, weights, skip_gain[layer_index], log_rate[layer_index], step_bias[layer_index]
        )
        saved_all.append(saved)
    result = stream * mask
    grad = cotangent * mask
    reduced_all = []
    skip_all = []
    for layer_index in reversed(range(layers)):
        weights = (
            lax.all_gather(norm_gain[layer_index], "dp", axis=0, tiled=True),
            lax.all_gather(gate_weight[layer_index], "dp", axis=0, tiled=True),
            lax.all_gather(mix_weight[layer_index], "dp", axis=0, tiled=True),
            lax.all_gather(step_weight[layer_index], "dp", axis=0, tiled=True),
            lax.all_gather(conv_kernel[layer_index], "dp", axis=1, tiled=True),
            lax.all_gather(conv_bias[layer_index], "dp", axis=0, tiled=True),
            lax.all_gather(gated_gain[layer_index], "dp", axis=0, tiled=True),
            lax.all_gather(out_weight[layer_index], "dp", axis=0, tiled=True),
        )
        grad, weight_grads, skip_grad = layer_backward(
            grad,
            saved_all[layer_index],
            weights,
            skip_gain[layer_index],
            log_rate[layer_index],
            step_bias[layer_index],
        )
        reduced = (
            lax.psum_scatter(weight_grads[0], "dp", scatter_dimension=0, tiled=True),
            lax.psum_scatter(weight_grads[1], "dp", scatter_dimension=0, tiled=True),
            lax.psum_scatter(weight_grads[2], "dp", scatter_dimension=0, tiled=True),
            lax.psum_scatter(weight_grads[3], "dp", scatter_dimension=0, tiled=True),
            lax.psum_scatter(weight_grads[4], "dp", scatter_dimension=1, tiled=True),
            lax.psum_scatter(weight_grads[5], "dp", scatter_dimension=0, tiled=True),
            lax.psum_scatter(weight_grads[6], "dp", scatter_dimension=0, tiled=True),
            lax.psum_scatter(weight_grads[7], "dp", scatter_dimension=0, tiled=True),
        )
        reduced = lax.psum(
            (
                reduced[0],
                reduced[1],
                reduced[2],
                reduced[3],
                reduced[4],
                reduced[5],
                reduced[6],
                reduced[7],
            ),
            "seq",
        )
        skip_total = lax.psum(skip_grad, ("dp", "seq"))
        reduced_all.insert(0, reduced)
        skip_all.insert(0, skip_total)
    stacked = tuple((jnp.stack([entry[member] for entry in reduced_all]) for member in range(8)))
    return (result, grad) + stacked + (jnp.stack(skip_all),)


def solution(mesh):
    return jax.shard_map(
        on_device,
        mesh=mesh,
        in_specs=(
            P("dp", "seq", None),
            P("dp", "seq", None),
            P("dp"),
            P(None, "dp"),
            P(None, "dp", None),
            P(None, "dp", None),
            P(None, "dp", None),
            P(None, None, "dp"),
            P(None, "dp"),
            P(None, "dp"),
            P(None, "dp", None),
            P(),
            P(),
            P(),
        ),
        out_specs=(
            P("dp", "seq", None),
            P("dp", "seq", None),
            P(None, "dp"),
            P(None, "dp", None),
            P(None, "dp", None),
            P(None, "dp", None),
            P(None, None, "dp"),
            P(None, "dp"),
            P(None, "dp"),
            P(None, "dp", None),
            P(),
        ),
        check_vma=False,
    )
```

profile of v0, /device:TPU:0, one launch (start us, length us, event | category | flops | bytes accessed | tf_op | source)
XLA Modules:
  0.0 1350.0 jit_solution(13960874902507613550)
XLA Ops:
  17.8 14.1 %all-gather.4 = f32[1,768,24]{2,0,1:T(1,128)S(1)} all-gather(f32[1,192,24]{2,0,1:T(1,128)S(1)} %copy.514), channel_id=6, replica_groups=mesh['dp'=4,'seq'=8] {'dp'}, dimensions={1}, use_global_device_ids=true | all-gather | bytes 92160 | tf_op jit(solution)/shard_map/all_gather | solution.py:289
  36.6 16.4 %all-reduce.18 = (f32[768]{0:T(1024)S(1)}, f32[1792]{0:T(1024)}, f32[768]{0:T(1024)S(1)}, f32[1792]{0:T(1024)}) all-reduce(f32[768]{0:T(1024)S(1)} %dynamic-update-slice.1, f32[1792]{0:T(1024)S(1)} %dynamic-update-slice, f32[768]{0:T(1024)S(1)} %dynamic-update-slice.3, ...), channel_id=4, replica_groups=mesh['dp'=4,'seq'=8] {'dp'}, use_global_device_ids=true, to_apply=%add.5 | all-reduce | flops 5120 | bytes 40960 | tf_op jit(solution)/shard_map/all_gather | solution.py:286
  56.2 20.2 %all-gather.1 = f32[1,4,1792]{1,0,2:T(1,128)S(1)} all-gather(f32[1,4,448]{1,0,2:T(1,128)S(1)} %copy.513), channel_id=3, replica_groups=mesh['dp'=4,'seq'=8] {'dp'}, dimensions={2}, use_global_device_ids=true | all-gather | bytes 35840 | tf_op jit(solution)/shard_map/all_gather | solution.py:290
  76.5 37.7 %slice_reduce_fusion.7 = (f32[1792]{0:T(1024)}, f32[1792]{0:T(1024)}, f32[1792]{0:T(1024)}, f32[1792]{0:T(1024)}) fusion(f32[1,4,1792]{1,0,2:T(1,128)S(1)} %all-gather.1), kind=kLoop, calls=%fused_computation.195 | loop fusion | bytes 57344 | tf_op jit(solution)/shard_map/slice | solution.py:68
  115.0 16.2 %all-gather.9 = f32[1,4,1792]{1,0,2:T(1,128)S(1)} all-gather(f32[1,4,448]{1,0,2:T(1,128)S(1)} %copy.515), channel_id=11, replica_groups=mesh['dp'=4,'seq'=8] {'dp'}, dimensions={2}, use_global_device_ids=true | all-gather | bytes 35840 | tf_op jit(solution)/shard_map/all_gather | solution.py:290
  131.2 38.1 %slice_reduce_fusion.3 = (f32[1792]{0:T(1024)}, f32[1792]{0:T(1024)}, f32[1792]{0:T(1024)}, f32[1792]{0:T(1024)}) fusion(f32[1,4,1792]{1,0,2:T(1,128)S(1)} %all-gather.9), kind=kLoop, calls=%fused_computation.191 | loop fusion | bytes 57344 | tf_op jit(solution)/shard_map/slice | solution.py:68
  207.0 9.7 all-gather.12
  230.0 89.3 %while.40 = (s32[]{:T(128)}, f32[1,24,64,128]{3,2,1,0:T(8,128)S(1)}, f32[1,24]{1,0:T(1,128)}, f32[1,24,64,128]{3,2,1,0:T(8,128)S(1)}, s32[]{:T(128)}) while((s32[]{:T(128)}, f32[1,24,64,128]{3,2,1,0:T(8,128)S(1)}, f32[1,24]{1,0:T(1,128)}, f32[1,24,64,128]{3,2,1,0:T(8,128)S(1)}, s32[]{:T(128)}) %tuple.134), condition=%wide.region_4.5_spmd, body=%wide.region_3.4_spmd.sunk | while | flops 393218 | bytes 5505221 | solution.py:29
  235.0 11.8 collective-permute-start
  249.5 11.5 collective-permute-start
  263.7 11.5 collective-permute-start
  277.8 11.5 collective-permute-start
  291.9 11.5 collective-permute-start
  306.0 11.5 collective-permute-start
  362.1 11.3 collective-permute-start.5
  405.0 100.9 %while.41 = (s32[]{:T(128)}, f32[1,24,64,128]{3,2,1,0:T(8,128)S(1)}, f32[1,24]{1,0:T(1,128)}, f32[1,24,64,128]{3,2,1,0:T(8,128)}, s32[]{:T(128)}) while((s32[]{:T(128)}, f32[1,24,64,128]{3,2,1,0:T(8,128)S(1)}, f32[1,24]{1,0:T(1,128)}, f32[1,24,64,128]{3,2,1,0:T(8,128)}, s32[]{:T(128)}) %tuple.137), condition=%wide.region_10.11_spmd, body=%wide.region_9.10_spmd.sunk | while | flops 393218 | bytes 5505221 | solution.py:29
  429.8 11.4 collective-permute-start.1
  445.4 11.4 collective-permute-start.1
  461.1 11.4 collective-permute-start.1
  476.8 11.4 collective-permute-start.1
  492.4 11.4 collective-permute-start.1
  520.0 9.5 multiply_reduce_fusion.18
  571.0 114.2 %while.42 = (s32[]{:T(128)}, f32[1,24,64,128]{3,2,1,0:T(8,128)}, f32[1,24]{1,0:T(1,128)}, f32[1,24,64,128]{3,2,1,0:T(8,128)}, s32[]{:T(128)}) while((s32[]{:T(128)}, f32[1,24,64,128]{3,2,1,0:T(8,128)}, f32[1,24]{1,0:T(1,128)}, f32[1,24,64,128]{3,2,1,0:T(8,128)}, s32[]{:T(128)}) %tuple.182), condition=%wide.region_14.15_spmd, body=%wide.region_13.14_spmd.sunk | while | flops 393218 | bytes 5505221 | solution.py:37
  574.8 12.3 collective-permute-done.2
  590.8 13.0 collective-permute-done.2
  607.6 12.6 collective-permute-done.2
  623.9 12.6 collective-permute-done.2
  640.2 12.7 collective-permute-done.2
  656.6 12.6 collective-permute-done.2
  672.9 12.3 collective-permute-done.2
  694.9 9.7 multiply_reduce_fusion.14
  711.9 11.3 fusion.31
  822.5 111.8 %while.43 = (s32[]{:T(128)}, f32[1,24,64,128]{3,2,1,0:T(8,128)S(1)}, f32[1,24]{1,0:T(1,128)S(1)}, f32[1,24,64,128]{3,2,1,0:T(8,128)}, s32[]{:T(128)}) while((s32[]{:T(128)}, f32[1,24,64,128]{3,2,1,0:T(8,128)S(1)}, f32[1,24]{1,0:T(1,128)S(1)}, f32[1,24,64,128]{3,2,1,0:T(8,128)}, s32[]{:T(128)}) %tuple.181), condition=%wide.region_28.29_spmd, body=%wide.region_27.28_spmd.sunk | while | flops 393218 | bytes 5505221 | solution.py:37
  826.1 12.6 collective-permute-done.3
  842.2 12.6 collective-permute-done.3
  858.3 12.2 collective-permute-done.3
  873.9 12.6 collective-permute-done.3
  890.0 12.2 collective-permute-done.3
  905.6 12.6 collective-permute-done.3
  921.7 12.6 collective-permute-done.3
  952.4 10.7 fusion.33
  973.5 11.2 collective-permute-done.7
  1004.5 51.9 %reduce-scatter.23.cloned.1.call-done = f32[192,1792]{1,0:T(8,128)} async-done(((f32[768,1792]{1,0:T(8,128)}), f32[192,1792]{1,0:T(8,128)}) %reduce-scatter.23.cloned.1.call-update) | async-done | bytes 1376272 | tf_op jit(solution)/shard_map/reduce_scatter | solution.py:325
  1066.2 39.5 %all-reduce.14 = (f32[1,24]{1,0:T(1,128)S(1)}, f32[1,24]{1,0:T(1,128)S(1)}) all-reduce(f32[1,24]{1,0:T(1,128)S(1)} %bitcast.663, f32[1,24]{1,0:T(1,128)S(1)} %bitcast.664), channel_id=1, replica_groups=mesh['dp'=4,'seq'=8] {'dp','seq'}, use_global_device_ids=true, to_apply=%region_91.92 | all-reduce | flops 48 | bytes 384 | tf_op jit(solution)/shard_map/psum | solution.py:345
  1122.1 17.5 %all-reduce.17 = (f32[768]{0:T(1024)S(1)}, f32[768]{0:T(1024)S(1)}, f32[1792]{0:T(1024)S(1)}, f32[1792]{0:T(1024)S(1)}, f32[1536]{0:T(1024)S(1)}, /*index=5*/f32[1536]{0:T(1024)S(1)}) all-reduce(f32[768]{0:T(1024)S(1)} %copy-done.142, f32[768]{0:T(1024)S(1)} %get-tuple-element.129, ...), channel_id=19, replica_groups=mesh['dp'=4,'seq'=8] {'dp'}, use_global_device_ids=true, to_apply=%region_44.45.clone | all-reduce | flops 8192 | bytes 65536
  1145.6 26.1 %reduce-scatter.31.cloned.1.call-done = f32[192,24]{1,0:T(8,128)} async-done(((f32[768,24]{1,0:T(8,128)}), f32[192,24]{1,0:T(8,128)}) %reduce-scatter.31.cloned.1.call-update) | async-done | bytes 18448
  1172.7 31.5 %all-reduce.15 = (f32[1,192]{1,0:T(1,128)S(1)}, f32[1,192]{1,0:T(1,128)S(1)}, f32[1,192,24]{1,2,0:T(8,128)S(1)}, f32[1,192,24]{1,2,0:T(8,128)S(1)}, f32[1,4,448]...) all-reduce(f32[1,192]{1,0:T(1,128)S(1)} %bitcast.655, ...), channel_id=1, replica_groups=mesh['dp'=4,'seq'=8] {'seq'}, use_global_device_ids=true, to_apply=%region_45.46 | all-reduce | flops 14848 | bytes 118784 | tf_op jit(solution)/shard_map/psum | solution.py:332
  1207.3 128.5 %all-reduce.21.cloned.1.call-done = (f32[1,192,1536]{2,1,0:T(8,128)}, f32[1,192,1536]{2,1,0:T(8,128)}, f32[1,192,1792]{2,1,0:T(8,128)}, f32[1,192,1792]{2,1,0:T(...) async-done(((f32[1,192,1536]{2,1,0:T(8,128)}, f32[1,192,1536]{2,1,0:T(8,128)}, f32[1,192,1792]{2,1,0:T(8,128)}, f32[1,192,1792]{2,1,0:T(8,128)}, ...) | async-done | bytes 7471120 | tf_op jit(solution)/shard_map/psum | solution.py:332
  (704 shorter events, 515.3 us)
Async XLA Ops:
  7.2 162.8 %all-gather.23.cloned.1.call-start = ((), (), s32[]{:S(2)}) async-start(), calls=%async_computation.16 | async-start | bytes 6881280 | tf_op jit(solution)/shard_map/all_gather | solution.py:288
  10.9 322.5 %all-gather.25.cloned.1.call-start = ((), (), s32[]{:S(2)}) async-start(), calls=%async_computation.17 | async-start | bytes 5898240 | tf_op jit(solution)/shard_map/all_gather | solution.py:287
  12.5 330.7 %all-gather.27.cloned.1.call-start = ((), (), s32[]{:S(2)}) async-start(), calls=%async_computation.18 | async-start | bytes 5898240 | tf_op jit(solution)/shard_map/all_gather | solution.py:293
  15.8 337.7 %all-gather.29.cloned.1.call-start = ((), (), s32[]{:S(2)}) async-start(), calls=%async_computation.19 | async-start | bytes 6881280 | tf_op jit(solution)/shard_map/all_gather | solution.py:288
  16.4 503.5 %all-gather.31.cloned.1.call-start = ((), (), s32[]{:S(2)}) async-start(), calls=%async_computation.20 | async-start | bytes 5898240 | tf_op jit(solution)/shard_map/all_gather | solution.py:287
  17.0 513.0 %all-gather.33.cloned.1.call-start = ((), (), s32[]{:S(2)}) async-start(), calls=%async_computation.21 | async-start | bytes 5898240 | tf_op jit(solution)/shard_map/all_gather | solution.py:293
  17.6 986.8 %reduce-scatter.21.cloned.1.call-start = ((), (), s32[]{:S(2)}) async-start(), calls=%async_computation.11 | async-start | bytes 5898240 | tf_op jit(solution)/shard_map/reduce_scatter | solution.py:324
  178.0 38.6 %collective-permute-start.4 = (f32[1,3,1792]{2,1,0:T(4,128)}, f32[1,3,1792]{2,1,0:T(4,128)S(1)}, u32[]{:S(2)}, u32[]{:S(2)}) collective-permute-start(f32[1,3,1792]{2,1,0:T(4,128)} %slice.331), channel_id=1, source_target_pairs={{0,1},{1,2},{2,3},{3,4},{4,5},{5,6},{6,7},{8,9},{9,10},{10,11},{11... | collective-permute-start | bytes 64520 | tf_op jit(solution)/shard_map/ppermute | solution.py:13
  235.0 13.7 %collective-permute-start = (f32[1,24,64,128]{3,2,1,0:T(8,128)S(1)}, f32[1,24,64,128]{3,2,1,0:T(8,128)S(1)}, u32[]{:S(2)}, u32[]{:S(2)}) collective-permute-start(f32[1,24,64,128]{3,2,1,0:T(8,128)S(1)} %multiply_add_fusion.10), channel_id=1, source_target_pairs={{0,1},{1,2},{2,3},{3,4},{4,5},{5,6},{6,7},{8,9},{9,10},{10,11},{11... | collective-permute-start | bytes 2359304 | tf_op jit(solution)/shard_map/while/body/eval_jaxpr/ppermute | solution.py:13
  249.5 13.3 collective-permute-start
  263.7 13.3 collective-permute-start
  277.8 13.3 collective-permute-start
  291.9 13.3 collective-permute-start
  306.0 13.3 collective-permute-start
  362.1 22.9 %collective-permute-start.5 = (f32[1,3,1792]{2,1,0:T(4,128)S(1)}, f32[1,3,1792]{2,1,0:T(4,128)S(1)}, u32[]{:S(2)}, u32[]{:S(2)}) collective-permute-start(f32[1,3,1792]{2,1,0:T(4,128)S(1)} %slice.345), channel_id=1, source_target_pairs={{0,1},{1,2},{2,3},{3,4},{4,5},{5,6},{6,7},{8,9},{9,10},{10,11},{11... | collective-permute-start | bytes 64520 | tf_op jit(solution)/shard_map/ppermute | solution.py:13
  407.6 6.7 collective-permute-start.1
  416.5 11.1 collective-permute-start.1
  429.8 13.5 %collective-permute-start.1 = (f32[1,24,64,128]{3,2,1,0:T(8,128)}, f32[1,24,64,128]{3,2,1,0:T(8,128)S(1)}, u32[]{:S(2)}, u32[]{:S(2)}) collective-permute-start(f32[1,24,64,128]{3,2,1,0:T(8,128)} %multiply_add_fusion.11), channel_id=1, source_target_pairs={{0,1},{1,2},{2,3},{3,4},{4,5},{5,6},{6,7},{8,9},{9,10},{10,11},{11... | collective-permute-start | bytes 2359304 | tf_op jit(solution)/shard_map/while/body/eval_jaxpr/ppermute | solution.py:13
  445.4 13.5 %collective-permute-start.1 = (f32[1,24,64,128]{3,2,1,0:T(8,128)}, f32[1,24,64,128]{3,2,1,0:T(8,128)S(1)}, u32[]{:S(2)}, u32[]{:S(2)}) collective-permute-start(f32[1,24,64,128]{3,2,1,0:T(8,128)} %multiply_add_fusion.11), channel_id=1, source_target_pairs={{0,1},{1,2},{2,3},{3,4},{4,5},{5,6},{6,7},{8,9},{9,10},{10,11},{11... | collective-permute-start | bytes 2359304 | tf_op jit(solution)/shard_map/while/body/eval_jaxpr/ppermute | solution.py:13
  461.1 13.5 %collective-permute-start.1 = (f32[1,24,64,128]{3,2,1,0:T(8,128)}, f32[1,24,64,128]{3,2,1,0:T(8,128)S(1)}, u32[]{:S(2)}, u32[]{:S(2)}) collective-permute-start(f32[1,24,64,128]{3,2,1,0:T(8,128)} %multiply_add_fusion.11), channel_id=1, source_target_pairs={{0,1},{1,2},{2,3},{3,4},{4,5},{5,6},{6,7},{8,9},{9,10},{10,11},{11... | collective-permute-start | bytes 2359304 | tf_op jit(solution)/shard_map/while/body/eval_jaxpr/ppermute | solution.py:13
  476.8 13.5 %collective-permute-start.1 = (f32[1,24,64,128]{3,2,1,0:T(8,128)}, f32[1,24,64,128]{3,2,1,0:T(8,128)S(1)}, u32[]{:S(2)}, u32[]{:S(2)}) collective-permute-start(f32[1,24,64,128]{3,2,1,0:T(8,128)} %multiply_add_fusion.11), channel_id=1, source_target_pairs={{0,1},{1,2},{2,3},{3,4},{4,5},{5,6},{6,7},{8,9},{9,10},{10,11},{11... | collective-permute-start | bytes 2359304 | tf_op jit(solution)/shard_map/while/body/eval_jaxpr/ppermute | solution.py:13
  492.4 13.5 %collective-permute-start.1 = (f32[1,24,64,128]{3,2,1,0:T(8,128)}, f32[1,24,64,128]{3,2,1,0:T(8,128)S(1)}, u32[]{:S(2)}, u32[]{:S(2)}) collective-permute-start(f32[1,24,64,128]{3,2,1,0:T(8,128)} %multiply_add_fusion.11), channel_id=1, source_target_pairs={{0,1},{1,2},{2,3},{3,4},{4,5},{5,6},{6,7},{8,9},{9,10},{10,11},{11... | collective-permute-start | bytes 2359304 | tf_op jit(solution)/shard_map/while/body/eval_jaxpr/ppermute | solution.py:13
  548.4 456.0 %reduce-scatter.29.cloned.1.call-start = ((), (), s32[]{:S(2)}) async-start(), calls=%async_computation.15 | async-start | bytes 5898240 | tf_op jit(solution)/shard_map/reduce_scatter | solution.py:330
  569.9 434.5 %reduce-scatter.19.cloned.1.call-start = ((), (), s32[]{:S(2)}) async-start(), calls=%async_computation.10 | async-start | bytes 5898240 | tf_op jit(solution)/shard_map/reduce_scatter | solution.py:324
  573.5 13.6 %collective-permute-start.2 = (f32[1,24,64,128]{3,2,1,0:T(8,128)}, f32[1,24,64,128]{3,2,1,0:T(8,128)}, u32[]{:S(2)}, u32[]{:S(2)}) collective-permute-start(f32[1,24,64,128]{3,2,1,0:T(8,128)} %multiply_add_fusion.12), channel_id=1, source_target_pairs={{1,0},{2,1},{3,2},{4,3},{5,4},{6,5},{7,6},{9,8},{10,9},{11,10},{12... | collective-permute-start | bytes 2359304 | tf_op jit(solution)/shard_map/while/body/eval_jaxpr/ppermute | solution.py:13
  589.6 14.3 %collective-permute-start.2 = (f32[1,24,64,128]{3,2,1,0:T(8,128)}, f32[1,24,64,128]{3,2,1,0:T(8,128)}, u32[]{:S(2)}, u32[]{:S(2)}) collective-permute-start(f32[1,24,64,128]{3,2,1,0:T(8,128)} %multiply_add_fusion.12), channel_id=1, source_target_pairs={{1,0},{2,1},{3,2},{4,3},{5,4},{6,5},{7,6},{9,8},{10,9},{11,10},{12... | collective-permute-start | bytes 2359304 | tf_op jit(solution)/shard_map/while/body/eval_jaxpr/ppermute | solution.py:13
  606.3 13.9 %collective-permute-start.2 = (f32[1,24,64,128]{3,2,1,0:T(8,128)}, f32[1,24,64,128]{3,2,1,0:T(8,128)}, u32[]{:S(2)}, u32[]{:S(2)}) collective-permute-start(f32[1,24,64,128]{3,2,1,0:T(8,128)} %multiply_add_fusion.12), channel_id=1, source_target_pairs={{1,0},{2,1},{3,2},{4,3},{5,4},{6,5},{7,6},{9,8},{10,9},{11,10},{12... | collective-permute-start | bytes 2359304 | tf_op jit(solution)/shard_map/while/body/eval_jaxpr/ppermute | solution.py:13
  622.6 13.9 %collective-permute-start.2 = (f32[1,24,64,128]{3,2,1,0:T(8,128)}, f32[1,24,64,128]{3,2,1,0:T(8,128)}, u32[]{:S(2)}, u32[]{:S(2)}) collective-permute-start(f32[1,24,64,128]{3,2,1,0:T(8,128)} %multiply_add_fusion.12), channel_id=1, source_target_pairs={{1,0},{2,1},{3,2},{4,3},{5,4},{6,5},{7,6},{9,8},{10,9},{11,10},{12... | collective-permute-start | bytes 2359304 | tf_op jit(solution)/shard_map/while/body/eval_jaxpr/ppermute | solution.py:13
  638.9 14.0 %collective-permute-start.2 = (f32[1,24,64,128]{3,2,1,0:T(8,128)}, f32[1,24,64,128]{3,2,1,0:T(8,128)}, u32[]{:S(2)}, u32[]{:S(2)}) collective-permute-start(f32[1,24,64,128]{3,2,1,0:T(8,128)} %multiply_add_fusion.12), channel_id=1, source_target_pairs={{1,0},{2,1},{3,2},{4,3},{5,4},{6,5},{7,6},{9,8},{10,9},{11,10},{12... | collective-permute-start | bytes 2359304 | tf_op jit(solution)/shard_map/while/body/eval_jaxpr/ppermute | solution.py:13
  655.3 13.9 %collective-permute-start.2 = (f32[1,24,64,128]{3,2,1,0:T(8,128)}, f32[1,24,64,128]{3,2,1,0:T(8,128)}, u32[]{:S(2)}, u32[]{:S(2)}) collective-permute-start(f32[1,24,64,128]{3,2,1,0:T(8,128)} %multiply_add_fusion.12), channel_id=1, source_target_pairs={{1,0},{2,1},{3,2},{4,3},{5,4},{6,5},{7,6},{9,8},{10,9},{11,10},{12... | collective-permute-start | bytes 2359304 | tf_op jit(solution)/shard_map/while/body/eval_jaxpr/ppermute | solution.py:13
  671.6 13.6 %collective-permute-start.2 = (f32[1,24,64,128]{3,2,1,0:T(8,128)}, f32[1,24,64,128]{3,2,1,0:T(8,128)}, u32[]{:S(2)}, u32[]{:S(2)}) collective-permute-start(f32[1,24,64,128]{3,2,1,0:T(8,128)} %multiply_add_fusion.12), channel_id=1, source_target_pairs={{1,0},{2,1},{3,2},{4,3},{5,4},{6,5},{7,6},{9,8},{10,9},{11,10},{12... | collective-permute-start | bytes 2359304 | tf_op jit(solution)/shard_map/while/body/eval_jaxpr/ppermute | solution.py:13
  736.4 23.1 %collective-permute-start.6 = (f32[1,3,1792]{2,1,0:T(4,128)}, f32[1,3,1792]{2,1,0:T(4,128)}, u32[]{:S(2)}, u32[]{:S(2)}) collective-permute-start(f32[1,3,1792]{2,1,0:T(4,128)} %slice.362), channel_id=1, source_target_pairs={{1,0},{2,1},{3,2},{4,3},{5,4},{6,5},{7,6},{9,8},{10,9},{11,10},{12... | collective-permute-start | bytes 64520 | tf_op jit(solution)/shard_map/ppermute | solution.py:13
  786.4 218.0 %reduce-scatter.27.cloned.1.call-start = ((), (), s32[]{:S(2)}) async-start(), calls=%async_computation.14 | async-start | bytes 5898240 | tf_op jit(solution)/shard_map/reduce_scatter | solution.py:330
  794.0 210.5 %reduce-scatter.25.cloned.1.call-start = ((), (), s32[]{:S(2)}) async-start(), calls=%async_computation.13 | async-start | bytes 6881280 | tf_op jit(solution)/shard_map/reduce_scatter | solution.py:325
  802.8 253.6 %reduce-scatter.23.cloned.1.call-start = ((), (), s32[]{:S(2)}) async-start(), calls=%async_computation.12 | async-start | bytes 6881280 | tf_op jit(solution)/shard_map/reduce_scatter | solution.py:325
  824.9 13.9 %collective-permute-start.3 = (f32[1,24,64,128]{3,2,1,0:T(8,128)}, f32[1,24,64,128]{3,2,1,0:T(8,128)S(1)}, u32[]{:S(2)}, u32[]{:S(2)}) collective-permute-start(f32[1,24,64,128]{3,2,1,0:T(8,128)} %multiply_add_fusion.13), channel_id=1, source_target_pairs={{1,0},{2,1},{3,2},{4,3},{5,4},{6,5},{7,6},{9,8},{10,9},{11,10},{12... | collective-permute-start | bytes 2359304 | tf_op jit(solution)/shard_map/while/body/eval_jaxpr/ppermute | solution.py:13
  840.9 13.9 %collective-permute-start.3 = (f32[1,24,64,128]{3,2,1,0:T(8,128)}, f32[1,24,64,128]{3,2,1,0:T(8,128)S(1)}, u32[]{:S(2)}, u32[]{:S(2)}) collective-permute-start(f32[1,24,64,128]{3,2,1,0:T(8,128)} %multiply_add_fusion.13), channel_id=1, source_target_pairs={{1,0},{2,1},{3,2},{4,3},{5,4},{6,5},{7,6},{9,8},{10,9},{11,10},{12... | collective-permute-start | bytes 2359304 | tf_op jit(solution)/shard_map/while/body/eval_jaxpr/ppermute | solution.py:13
  857.0 13.5 %collective-permute-start.3 = (f32[1,24,64,128]{3,2,1,0:T(8,128)}, f32[1,24,64,128]{3,2,1,0:T(8,128)S(1)}, u32[]{:S(2)}, u32[]{:S(2)}) collective-permute-start(f32[1,24,64,128]{3,2,1,0:T(8,128)} %multiply_add_fusion.13), channel_id=1, source_target_pairs={{1,0},{2,1},{3,2},{4,3},{5,4},{6,5},{7,6},{9,8},{10,9},{11,10},{12... | collective-permute-start | bytes 2359304 | tf_op jit(solution)/shard_map/while/body/eval_jaxpr/ppermute | solution.py:13
  872.6 13.9 %collective-permute-start.3 = (f32[1,24,64,128]{3,2,1,0:T(8,128)}, f32[1,24,64,128]{3,2,1,0:T(8,128)S(1)}, u32[]{:S(2)}, u32[]{:S(2)}) collective-permute-start(f32[1,24,64,128]{3,2,1,0:T(8,128)} %multiply_add_fusion.13), channel_id=1, source_target_pairs={{1,0},{2,1},{3,2},{4,3},{5,4},{6,5},{7,6},{9,8},{10,9},{11,10},{12... | collective-permute-start | bytes 2359304 | tf_op jit(solution)/shard_map/while/body/eval_jaxpr/ppermute | solution.py:13
  888.7 13.5 %collective-permute-start.3 = (f32[1,24,64,128]{3,2,1,0:T(8,128)}, f32[1,24,64,128]{3,2,1,0:T(8,128)S(1)}, u32[]{:S(2)}, u32[]{:S(2)}) collective-permute-start(f32[1,24,64,128]{3,2,1,0:T(8,128)} %multiply_add_fusion.13), channel_id=1, source_target_pairs={{1,0},{2,1},{3,2},{4,3},{5,4},{6,5},{7,6},{9,8},{10,9},{11,10},{12... | collective-permute-start | bytes 2359304 | tf_op jit(solution)/shard_map/while/body/eval_jaxpr/ppermute | solution.py:13
  904.3 13.9 %collective-permute-start.3 = (f32[1,24,64,128]{3,2,1,0:T(8,128)}, f32[1,24,64,128]{3,2,1,0:T(8,128)S(1)}, u32[]{:S(2)}, u32[]{:S(2)}) collective-permute-start(f32[1,24,64,128]{3,2,1,0:T(8,128)} %multiply_add_fusion.13), channel_id=1, source_target_pairs={{1,0},{2,1},{3,2},{4,3},{5,4},{6,5},{7,6},{9,8},{10,9},{11,10},{12... | collective-permute-start | bytes 2359304 | tf_op jit(solution)/shard_map/while/body/eval_jaxpr/ppermute | solution.py:13
  920.4 13.9 %collective-permute-start.3 = (f32[1,24,64,128]{3,2,1,0:T(8,128)}, f32[1,24,64,128]{3,2,1,0:T(8,128)S(1)}, u32[]{:S(2)}, u32[]{:S(2)}) collective-permute-start(f32[1,24,64,128]{3,2,1,0:T(8,128)} %multiply_add_fusion.13), channel_id=1, source_target_pairs={{1,0},{2,1},{3,2},{4,3},{5,4},{6,5},{7,6},{9,8},{10,9},{11,10},{12... | collective-permute-start | bytes 2359304 | tf_op jit(solution)/shard_map/while/body/eval_jaxpr/ppermute | solution.py:13
  972.1 12.6 collective-permute-start.7
  991.3 149.9 %reduce-scatter.37.cloned.1.call-start = ((), (), s32[]{:S(2)}) async-start(), calls=%async_computation.25 | async-start | bytes 1146880
  993.4 148.9 %reduce-scatter.35.cloned.1.call-start = ((), (), s32[]{:S(2)}) async-start(), calls=%async_computation.24 | async-start | bytes 1146880
  994.8 149.9 %reduce-scatter.33.cloned.1.call-start = ((), (), s32[]{:S(2)}) async-start(), calls=%async_computation.23 | async-start | bytes 491520
  997.1 174.6 %reduce-scatter.31.cloned.1.call-start = ((), (), s32[]{:S(2)}) async-start(), calls=%async_computation.22 | async-start | bytes 491520
  1004.3 331.4 %all-reduce.21.cloned.1.call-start = ((), (), s32[]{:S(2)}) async-start(), calls=%async_computation.26 | async-start | bytes 14942208 | tf_op jit(solution)/shard_map/psum | solution.py:332
  (171 other events, 1946.2 us)
Sparse Core Ops, SparseCore 0:
  11.0 76.4 all-gather.22
  89.3 60.2 all-gather.24
  151.5 57.2 all-gather.26
  210.4 65.1 all-gather.28
  277.4 57.0 all-gather.30
  336.1 57.0 all-gather.32
  548.6 67.0 reduce-scatter.20
  618.6 57.0 reduce-scatter.28
  786.5 66.9 reduce-scatter.18
  856.4 57.0 reduce-scatter.26
  916.6 63.6 reduce-scatter.24
  991.4 64.9 reduce-scatter.22
  1059.9 27.1 reduce-scatter.36
  1090.5 27.0 reduce-scatter.34
  1120.2 24.4 reduce-scatter.32
  1147.3 24.3 reduce-scatter.30
  1174.4 161.2 all-reduce.20
where the time goes:
time: 1360 us; the launch traced here: 1350 us
  waiting for transfers between devices  424 us (31%)
  matrix products  247 us (18%)
  local copies, waits for them, and re-layouts  189 us (14%)
  blocking collectives  180 us (13%)
  starting transfers between devices  175 us (13%)
  other arithmetic  112 us (8%)
  between operations  20.4 us (1%)
    ppermute x32, waiting for transfers between devices, from_behind(): lax.ppermute(value, axis, [(source, source + steps) for source in range(f...  214 us
    ppermute x32, starting transfers between devices, from_behind(): lax.ppermute(value, axis, [(source, source + steps) for source in range(f...  174 us
    dot_general x22, matrix products, matmul(): return jnp.dot(left, right, precision=HIGHEST)  136 us
    psum x1, waiting for transfers between devices, on_device(): lax.psum((reduced[0], reduced[1], reduced[2], reduced[3], reduced[4], red...  128 us
    slice x2, local copies, waits for them, and re-layouts, layer_forward(): conv_kernel[tap_index] * extended[:, tap_index:tap_index + group, :]  75.8 us
    reduce_scatter x2, waiting for transfers between devices, on_device(): lax.psum_scatter(weight_grads[2], 'dp', scatter_dimension=0, tiled=True)  51.9 us
    psum x1, blocking collectives, on_device(): skip_total = lax.psum(skip_grad, ('dp', 'seq'))  39.5 us
    all_gather x2, blocking collectives, on_device(): lax.all_gather(conv_kernel[layer_index], 'dp', axis=1, tiled=True)  36.4 us
  transfers between devices with their start and end apart: 49, of which 33 were waited for; matrix products, arithmetic and copies ran while one was open for 38% of the time, Pallas kernels for 0%

commit v1 on v0

v1 whole, which is shorter than its diff:
```python
import functools

import jax
import jax.numpy as jnp
from jax import lax
from jax.experimental import pallas as pl
from jax.experimental.pallas import tpu as pltpu
from jax.sharding import PartitionSpec as P

EPSILON = 1e-05
HIGH = lax.Precision.HIGH
MESH = pl.DeviceIdType.MESH
LANES = 128
F32 = jnp.float32


def mm(left, right, contract=((1,), (0,))):
    return lax.dot_general(left, right, (contract, ((), ())), precision=HIGH, preferred_element_type=F32)


NN = ((1,), (0,))
NT = ((1,), (1,))
TN = ((0,), (0,))


def split(value):
    high = value.astype(jnp.bfloat16)
    return high, (value - high.astype(F32)).astype(jnp.bfloat16)


def split3(value):
    first = value.astype(jnp.bfloat16)
    rest = value - first.astype(F32)
    second = rest.astype(jnp.bfloat16)
    third = (rest - second.astype(F32)).astype(jnp.bfloat16)
    return first, second, third


def exact(select, value, contract=((1,), (0,))):
    total = None
    for part in split3(value):
        term = lax.dot_general(select, part, (contract, ((), ())), preferred_element_type=F32)
        total = term if total is None else total + term
    return total


def exact_right(value, select, contract=((1,), (0,))):
    total = None
    for part in split3(value):
        term = lax.dot_general(part, select, (contract, ((), ())), preferred_element_type=F32)
        total = term if total is None else total + term
    return total


def iota(shape, axis):
    return lax.broadcasted_iota(jnp.int32, shape, axis)


def head_matrix(heads_padded, width, head_size, start=0):
    head = iota((heads_padded, width), 0)
    channel = iota((heads_padded, width), 1) + start
    inside = jnp.logical_and(channel >= head * head_size, channel < (head + 1) * head_size)
    return jnp.where(inside, 1.0, 0.0).astype(jnp.bfloat16)


def tri(size):
    return jnp.where(iota((size, size), 0) >= iota((size, size), 1), 1.0, 0.0)


def sigmoid(v):
    return jax.nn.sigmoid(v)


def softplus(v):
    return jnp.maximum(v, 0.0) + jnp.log1p(jnp.exp(-jnp.abs(v)))


def tiles(count, body):
    lax.fori_loop(0, count, lambda i, c: (body(i), c)[1], 0)


def lanes(i, width):
    return pl.ds(pl.multiple_of(i * width, width), width)


class Place:
    def __init__(self, dp_count, seq_count):
        self.n_dp, self.n_seq = dp_count, seq_count
        self.dp = lax.axis_index("dp")
        self.seq = lax.axis_index("seq")
        self.core = self.seq % 2
        self.z = self.seq // 2
        self.sib = self.z * 2 + (1 - self.core)
        self.parity = self.z % 2
        self.pair = (self.z + 1 - 2 * self.parity) * 2 + self.core
        y, x = self.dp // 2, self.dp % 2
        self.dpx = 2 * y + (1 - x)
        self.dpy = 2 * (1 - y) + x
        self.dpd = 2 * (1 - y) + (1 - x)


def remote(src, dst, send, recv, dp, seq):
    return pltpu.make_async_remote_copy(
        src_ref=src, dst_ref=dst, send_sem=send, recv_sem=recv, device_id=(dp, seq), device_id_type=MESH
    )


def entry_barrier(place):
    barrier = pltpu.get_barrier_semaphore()

    def greet(dp, seq):
        pl.semaphore_signal(barrier, inc=1, device_id=(dp, seq), device_id_type=MESH)

    for step in range(1, place.n_dp):
        greet((place.dp + step) % place.n_dp, place.seq)
    greet(place.dp, place.sib)
    greet(place.dp, place.pair)

    @pl.when(jnp.logical_and(place.core == 1, place.seq < place.n_seq - 1))
    def _():
        greet(place.dp, place.seq + 1)

    @pl.when(jnp.logical_and(place.core == 0, place.seq > 0))
    def _():
        greet(place.dp, place.seq - 1)

    outer = jnp.logical_or(place.seq == 0, place.seq == place.n_seq - 1)

    @pl.when(outer)
    def _():
        pl.semaphore_wait(barrier, place.n_dp + 1)

    @pl.when(jnp.logical_not(outer))
    def _():
        pl.semaphore_wait(barrier, place.n_dp + 2)


def full_barrier(place):
    barrier = pltpu.get_barrier_semaphore()
    for step in range(1, place.n_dp):
        peer = (place.dp + step) % place.n_dp
        pl.semaphore_signal(barrier, inc=1, device_id=(peer, place.seq), device_id_type=MESH)
    for step in range(1, place.n_seq):
        peer = (place.seq + step) % place.n_seq
        pl.semaphore_signal(barrier, inc=1, device_id=(place.dp, peer), device_id_type=MESH)
    pl.semaphore_wait(barrier, place.n_dp + place.n_seq - 2)


class Gather:
    def __init__(self, place, own, dest, stride, row_of, columns, half, sems, index):
        self.p, self.own, self.dest = place, own, dest
        self.stride, self.row_of, self.columns = stride, row_of, columns
        self.send, self.recv = sems
        self.index = index
        self.half = half
        self.third = half // 3
        self.wide = place.n_dp == 4 and half % 24 == 0 and place.n_seq % 4 == 0

    def at(self, owner, core, offset, count):
        start = owner * self.stride + self.row_of(core) + offset
        return self.dest.at[pl.ds(pl.multiple_of(start, 8), count), self.columns]

    def copy(self, kind, src, dst, dp, seq):
        return remote(src, dst, self.send.at[self.index, kind], self.recv.at[self.index, kind], dp, seq)

    def own_part(self, offset, count):
        start = self.row_of(self.p.core) + offset
        return self.own.at[pl.ds(pl.multiple_of(start, 8), count), self.columns]

    def get(self, kind):
        p, t = self.p, self.third
        if not self.wide:
            if kind < p.n_dp:
                peer = (p.dp + kind) % p.n_dp
                return self.copy(
                    kind, self.own_part(0, self.half), self.at(p.dp, p.core, 0, self.half), peer, p.seq
                )
            owner = (p.dp + 2 * p.n_dp - 1 - kind) % p.n_dp
            part = self.at(owner, p.core, 0, self.half)
            return self.copy(kind, part, part, p.dp, p.sib)
        first = p.parity * t
        only = 2 * t * p.parity
        miss = 2 * t * (1 - p.parity)
        if kind < 2:
            return self.copy(
                kind, self.own_part(first, 2 * t), self.at(p.dp, p.core, first, 2 * t),
                p.dpx if kind == 0 else p.dpy, p.seq,
            )
        owner, offset, count, dp, seq = {
            2: (p.dpx, first, t, p.dpy, p.seq),
            3: (p.dpy, first + t, t, p.dpx, p.seq),
            4: (p.dpx, only, t, p.dp, p.pair),
            5: (p.dpy, only, t, p.dp, p.pair),
            6: (p.dpd, only, t, p.dp, p.pair),
            7: (p.dpx, first, 2 * t, p.dp, p.sib),
            8: (p.dpy, first, 2 * t, p.dp, p.sib),
            9: (p.dpd, first, 2 * t, p.dp, p.sib),
            10: (p.dpx, miss, t, p.dp, p.sib),
            11: (p.dpy, miss, t, p.dp, p.sib),
            12: (p.dpd, miss, t, p.dp, p.sib),
        }[kind]
        part = self.at(owner, p.core, offset, count)
        return self.copy(kind, part, part, dp, seq)

    def stage(self, number):
        n = self.p.n_dp
        if not self.wide:
            if number == 0:
                for kind in range(1, n):
                    self.get(kind).start()
            elif number == 1:
                for kind in range(1, n):
                    self.get(kind).wait_recv()
                    self.get(n - 1 + kind).start()
            elif number == 4:
                for kind in range(n, 2 * n - 1):
                    self.get(kind).wait_recv()
            elif number == 5:
                for kind in range(1, 2 * n - 1):
                    self.get(kind).wait_send()
            return
        if number == 0:
            self.get(0).start()
            self.get(1).start()
        elif number == 1:
            self.get(0).wait_recv()
            for kind in (2, 4, 7):
                self.get(kind).start()
            self.get(1).wait_recv()
            for kind in (3, 5, 8):
                self.get(kind).start()
        elif number == 2:
            self.get(2).wait_recv()
            self.get(3).wait_recv()
            for kind in (6, 9):
                self.get(kind).start()
        elif number == 3:
            for kind in (4, 5, 6):
                self.get(kind).wait_recv()
                self.get(kind + 6).start()
        elif number == 4:
            for kind in range(7, 13):
                self.get(kind).wait_recv()
        else:
            for kind in range(13):
                self.get(kind).wait_send()


GATHER_OFFSETS = (0, 2, 4, 6, 7, 9)
PIECE = 384


def kinds_of(n_dp):
    return max(13, 2 * n_dp)


def forward_kernel(n_dp, n_seq, dims, *refs):
    (
        x_hbm, mask_ref, conv_ref, head_ref, wm_own, wg_own, wo_own,
        result_ref, conv_full, xs_out, gate_out, ext_out, step_out, mo_out, sin_out, sout_out, wm_out, wg_out, wo_out,
        WM, WG, WO, xs, gate, ext, step, mo, sin, sout, conv_in, mixed, diag, ldE, dtE, ldT, gm,
        g_send, g_recv, g_local, c_send, c_recv, e_send, e_recv, r_send, r_recv, o_sem,
    ) = refs
    T, D, DI, CW, H, PS, N, K = dims
    layers = 2
    place = Place(n_dp, n_seq)
    h = D // n_dp // 2
    mix_pieces, gate_pieces, across = (CW + LANES) // PIECE, DI // PIECE, D // PIECE
    out_pieces = 2 * across
    per_layer = mix_pieces + gate_pieces + out_pieces
    early = mix_pieces + gate_pieces
    done_at = GATHER_OFFSETS[4]

    def tick(t):
        for number in reversed(range(len(GATHER_OFFSETS))):
            job = t - GATHER_OFFSETS[number]
            layer, q = job // per_layer, job % per_layer
            inside = jnp.logical_and(job >= 0, job < 2 * per_layer)

            def run(own, dest, stride, row_of, column, number=number, job=job, layer=layer):
                piece = Gather(
                    place, own.at[layer], dest.at[layer], stride, row_of, lanes(column, PIECE), h, (g_send, g_recv), job
                )
                piece.stage(number)

            @pl.when(jnp.logical_and(inside, q < mix_pieces))
            def _():
                run(wm_own, WM, 2 * h, lambda core: core * h, q)

            @pl.when(jnp.logical_and(inside, jnp.logical_and(q >= mix_pieces, q < early)))
            def _():
                run(wg_own, WG, 2 * h, lambda core: core * h, q - mix_pieces)

            @pl.when(jnp.logical_and(inside, q >= early))
            def _():
                part = (q - early) // across
                run(wo_own, WO, 4 * h, lambda core: core * 2 * h + part * h, (q - early) % across)

    def own_copy(kind, layer):
        own, dest = ((wm_own, WM), (wg_own, WG), (wo_own, WO))[kind]
        rows = own.shape[1]
        start = pl.multiple_of(place.dp * rows, 8)
        return pltpu.make_async_copy(own.at[layer], dest.at[layer, pl.ds(start, rows)], g_local.at[layer * 3 + kind])

    first_in = pltpu.make_async_copy(x_hbm, xs.at[0], o_sem.at[0])
    first_in.start()
    ext[0, 0:8, :] = jnp.zeros((8, CW), F32)
    ext[1, 0:8, :] = jnp.zeros((8, CW), F32)
    entry_barrier(place)
    tick(0)
    for layer in range(layers):
        for kind in range(3):
            own_copy(kind, layer).start()

    def conv_copy(step_index):
        peer = (place.dp + step_index) % n_dp
        return remote(
            conv_ref, conv_in.at[place.dp], c_send.at[step_index - 1], c_recv.at[step_index - 1], peer, place.seq
        )

    for s in range(1, n_dp):
        conv_copy(s).start()
    conv_in[place.dp] = conv_ref[...]
    first_in.wait()
    tiles(done_at, lambda i: tick(i + 1))
    per_body = mix_pieces + 4 + H // 4 + gate_pieces + across
    ti, tj = iota((T, T), 0), iota((T, T), 1)
    lane_low = iota((T, LANES), 1) < PS
    CHUNK = 256
    chunks = DI // CHUNK

    def saved_copies(layer):
        saved = (
            (gate, gate_out), (ext, ext_out), (step, step_out), (mo, mo_out), (sin, sin_out), (sout, sout_out),
            (WM, wm_out), (WG, wg_out), (WO, wo_out),
        )
        return [
            pltpu.make_async_copy(a.at[layer], b.at[layer], o_sem.at[layer * 9 + k + 1])
            for k, (a, b) in enumerate(saved)
        ]

    def layer_body(layer, carry):
        x_all = xs[layer]
        inv = lax.rsqrt(jnp.mean(x_all * x_all, axis=-1, keepdims=True) + EPSILON)
        diag[:, 0:D] = x_all * inv
        head = head_ref[layer]
        base = done_at + 1 + layer * per_body
        own_copy(0, layer).wait()

        def project_mix(i):
            ext[layer, 8 : T + 8, lanes(i, PIECE)] = mm(diag[:, 0:D], WM[layer, :, lanes(i, PIECE)])
            tick(base + i)

        tiles(mix_pieces - 1, project_mix)
        last = (mix_pieces - 1) * PIECE
        value = mm(diag[:, 0:D], WM[layer, :, last : last + PIECE])
        ext[layer, 8 : T + 8, last:CW] = value[:, 0 : CW - last]
        raw = value[:, CW - last :]
        edge = remote(
            ext.at[layer, pl.ds(T, 8)], ext.at[layer, pl.ds(0, 8)], e_send.at[layer], e_recv.at[layer],
            place.dp, place.seq + 1,
        )

        @pl.when(place.seq < n_seq - 1)
        def _():
            edge.start()

        step[layer] = raw
        tick(base + mix_pieces - 1)
        dt = softplus(raw + head[1:2, :])
        rate = -jnp.exp(head[0:1, :]) * dt
        ld = exact(tri(T).astype(jnp.bfloat16), rate)
        ldT[...] = ld.T
        tick(base + mix_pieces)

        def expand(i):
            select = head_matrix(LANES, 256, PS, i * 256)
            ldE[:, lanes(i, 256)] = exact_right(ld, select)
            dtE[:, lanes(i, 256)] = exact_right(dt, select)

        tiles(DI // 256, expand)
        tick(base + mix_pieces + 1)

        @pl.when(layer == 0)
        def _():
            for s in range(1, n_dp):
                conv_copy(s).wait_recv()

            def sum_taps(i):
                at = lanes(i, 256)
                taps = conv_in[0, :, at]
                for s in range(1, n_dp):
                    taps = taps + conv_in[s, :, at]
                conv_full[:, at] = taps

            tiles(CW // 256, sum_taps)

        @pl.when(place.seq > 0)
        def _():
            edge.wait_recv()

        def conv(i):
            at = lanes(i, 256)
            taps = conv_full[pl.ds(pl.multiple_of(layer * 8, 8), 8), at]
            total = taps[K : K + 1, :]
            for k in range(K):
                total = total + taps[k : k + 1, :] * ext[layer, 8 - K + 1 + k : 8 - K + 1 + k + T, at]
            mixed[:, at] = total * sigmoid(total)

        tiles(CW // 256, conv)
        tick(base + mix_pieces + 2)
        b_map = mixed[:, DI : DI + N]
        c_map = mixed[:, DI + N : DI + 2 * N]
        gm[...] = jnp.where(ti >= tj, mm(c_map, b_map, NT), 0.0)

        def local_state(i):
            at = lanes(i, 256)
            l_tile = ldE[:, at]
            weighted = mixed[:, at] * dtE[:, at] * jnp.exp(l_tile[T - 1 : T, :] - l_tile)
            sout[layer, :, at] = mm(b_map, weighted, TN)

        tiles(DI // 256, local_state)
        tick(base + mix_pieces + 3)

        def relay_copy(chunk):
            at = lanes(chunk, CHUNK)
            return remote(
                sout.at[layer, :, at], sin.at[layer, :, at], r_send.at[layer, chunk], r_recv.at[layer, chunk],
                place.dp, place.seq + 1,
            )

        def relay(chunk):
            at = lanes(chunk, CHUNK)

            @pl.when(place.seq > 0)
            def _():
                relay_copy(chunk).wait_recv()
                total = jnp.exp(ldE[T - 1 : T, at])
                sout[layer, :, at] = sout[layer, :, at] + total * sin[layer, :, at]

            @pl.when(place.seq == 0)
            def _():
                sin[layer, :, at] = jnp.zeros((N, CHUNK), F32)

            @pl.when(place.seq < n_seq - 1)
            def _():
                relay_copy(chunk).start()

        pairs = H // 2

        def diagonal(i):
            @pl.when(i == place.seq * pairs // n_seq)
            def _():
                tiles(chunks, relay)

            at = lanes(i, LANES)
            scaled = mixed[:, at] * dtE[:, at]
            l_tile = ldE[:, at]
            parts = []
            for side in range(2):
                column = l_tile[:, side * PS : side * PS + 1]
                row = ldT[pl.ds(2 * i + side, 1), :]
                weights = gm[...] * jnp.exp(jnp.minimum(column - row, 0.0))
                parts.append(mm(weights, scaled))
            diag[:, at] = jnp.where(lane_low, parts[0], parts[1])

            @pl.when(i % 2 == 1)
            def _():
                tick(base + mix_pieces + 4 + i // 2)

        tiles(pairs, diagonal)

        def skip_row(i):
            return exact_right(head[2:3, :], head_matrix(LANES, 256, PS, i * 256))

        def gate_proj(i):
            at = lanes(i, PIECE)
            gate[layer, :, at] = mm(xs[layer] * inv, WG[layer, :, at])
            tick(base + mix_pieces + 4 + H // 4 + i)

        def off(i):
            at = lanes(i, 256)
            lift = jnp.exp(ldE[:, at])
            out = diag[:, at] + lift * mm(c_map, sin[layer, :, at]) + skip_row(i) * mixed[:, at]
            mo[layer, :, at] = out

        tiles(DI // 256, off)
        own_copy(1, layer).wait()
        tiles(gate_pieces, gate_proj)

        def gating(i, squares):
            at = lanes(i, LANES)
            pre = gate[layer, :, at]
            gated = mo[layer, :, at] * (pre * sigmoid(pre))
            diag[:, at] = gated
            return squares + gated * gated

        squares = lax.fori_loop(0, DI // LANES, gating, jnp.zeros((T, LANES), F32))
        inv_out = lax.rsqrt(jnp.sum(squares, axis=-1, keepdims=True) / DI + EPSILON)
        own_copy(2, layer).wait()

        def project_out(i):
            at = lanes(i, PIECE)
            tick(base + mix_pieces + 4 + H // 4 + gate_pieces + i)
            branch = mm(diag[...] * inv_out, WO[layer, :, at])
            nxt = xs[layer, :, at] + branch
            xs[layer + 1, :, at] = nxt

        tiles(across, project_out)
        for copy in saved_copies(layer):
            copy.start()
        @pl.when(place.seq < n_seq - 1)
        def _():
            edge.wait_send()
            tiles(chunks, lambda c: relay_copy(c).wait_send())

        return carry

    lax.fori_loop(0, layers, layer_body, 0)
    done = done_at + 1 + layers * per_body
    left = layers * per_layer + GATHER_OFFSETS[5] - done
    if left > 0:
        tiles(left, lambda i: tick(done + i))
    result_ref[...] = xs[layers] * mask_ref[...]
    last = pltpu.make_async_copy(xs.at[1], xs_out, o_sem.at[0])
    last.start()
    for s in range(1, n_dp):
        conv_copy(s).wait_send()
    for layer in range(layers):
        for copy in saved_copies(layer):
            copy.wait()
    last.wait()


def forward(x, mask, conv, head, wm, wg, wo, n_dp, n_seq, dims):
    T, D, DI, CW, H, PS, N, K = dims
    any_spec = pl.BlockSpec(memory_space=pl.ANY)
    vmem = pl.BlockSpec(memory_space=pltpu.VMEM)
    CX = CW + LANES
    kinds = kinds_of(n_dp)
    PIECES = 2 * ((CW + LANES) // PIECE + DI // PIECE + 2 * (D // PIECE))
    sd = lambda *s: jax.ShapeDtypeStruct(s, F32)
    v = lambda *s: pltpu.VMEM(s, F32)
    dma = pltpu.SemaphoreType.DMA
    return pl.pallas_call(
        functools.partial(forward_kernel, n_dp, n_seq, dims),
        out_shape=(
            sd(T, D), sd(16, CW), sd(T, D), sd(2, T, DI), sd(2, T + 8, CW), sd(2, T, LANES), sd(2, T, DI), sd(2, N, DI),
            sd(2, N, DI), sd(2, D, CX), sd(2, D, DI), sd(2, DI, D),
        ),
        in_specs=[any_spec, vmem, vmem, vmem, any_spec, any_spec, any_spec],
        out_specs=(vmem, vmem) + (any_spec,) * 10,
        scratch_shapes=[
            v(2, D, CX), v(2, D, DI), v(2, DI, D), v(3, T, D), v(2, T, DI), v(2, T + 8, CW), v(2, T, LANES),
            v(2, T, DI), v(2, N, DI), v(2, N, DI), v(n_dp, 16, CW), v(T, CW), v(T, DI), v(T, DI), v(T, DI),
            v(LANES, T), v(T, T),
            dma((PIECES, kinds)), dma((PIECES, kinds)), dma((6,)), dma((n_dp - 1,)), dma((n_dp - 1,)), dma((2,)), dma((2,)),
            dma((2, DI // 256)), dma((2, DI // 256)), dma((19,)),
        ],
        compiler_params=pltpu.CompilerParams(
            collective_id=0, has_side_effects=True, vmem_limit_bytes=61 << 20
        ),
        name="forward",
    )(x, mask, conv, head, wm, wg, wo)


def prepare(hidden, lengths, norm_gain, gate_weight, mix_weight, step_weight, conv_kernel, conv_bias, gated_gain,
            out_weight, skip_gain, log_rate, step_bias, n_dp):
    T = hidden.shape[1]
    H = skip_gain.shape[1]
    shard = conv_bias.shape[1]
    CW = shard * n_dp
    position = lax.axis_index("seq") * T + lax.iota(jnp.int32, T)
    mask = (position < lengths[0]).astype(F32)[:, None]
    gain = norm_gain[:, :, None]
    step_pad = jnp.pad(step_weight, ((0, 0), (0, 0), (0, LANES - H)))
    wm = jnp.concatenate([mix_weight, step_pad], axis=2) * gain
    wg = gate_weight * gain
    wo = out_weight * gated_gain[:, :, None]
    head = jnp.pad(jnp.stack([log_rate, step_bias, skip_gain], axis=1), ((0, 0), (0, 5), (0, LANES - H)))
    own = jnp.concatenate([conv_kernel, conv_bias[:, None, :]], axis=1)
    own = jnp.pad(own, ((0, 0), (0, 8 - own.shape[1]), (0, 0))).reshape(16, shard)
    conv = lax.dynamic_update_slice(jnp.zeros((16, CW), F32), own, (0, lax.axis_index("dp") * shard))
    return mask, conv, head, wm, wg, wo
CHUNK_N = 384


class Plan:
    def __init__(self, n_dp, n_seq, dims):
        T, D, DI, CW, H, PS, N, K = dims
        self.n_dp, self.n_seq = n_dp, n_seq
        self.n_z = n_seq // 2
        self.h = D // n_dp // 2
        self.out_jobs = 2 * (D // CHUNK_N)
        self.gate_jobs = DI // CHUNK_N
        self.mix_jobs = (CW + LANES) // CHUNK_N
        self.lead, self.bubbles = 2, 3
        self.per_layer = self.out_jobs + self.gate_jobs + self.mix_jobs
        self.early = self.out_jobs + self.gate_jobs
        self.slots = self.lead + self.per_layer + self.bubbles
        self.blocks = 2 * self.mix_jobs
        self.blocks_per_job = self.h // 8
        self.conv_jobs = -(-self.blocks // self.blocks_per_job)
        self.jobs = 2 * self.per_layer + self.conv_jobs
        self.total_slots = 2 * self.slots + self.conv_jobs
        self.wide = n_dp == 4 and self.n_z == 4 and self.h % 32 == 0
        self.rounds = self.n_z.bit_length() - 1
        self.offsets = (0, 1, 2, 4, 6, 8, 10, 12, 14, 15)
        self.o_ring = self.offsets[4] + 1
        self.f_ring = max(self.offsets) + 1
        self.s_ring = self.offsets[2] + 1
        self.kinds = 12 if self.wide else n_dp - 1 + self.rounds + 2
        self.sibling_kind = self.kinds - 1

    def job_of(self, slot):
        layer = slot // self.slots
        q = slot % self.slots - self.lead
        early = jnp.logical_and(q >= 0, q < self.early)
        late = q >= self.early + self.bubbles
        inside = jnp.logical_and(slot >= 0, slot < 2 * self.slots)
        valid = jnp.logical_and(inside, jnp.logical_or(early, late))
        job = layer * self.per_layer + q - jnp.where(early, 0, self.bubbles)
        conv = jnp.logical_and(slot >= 2 * self.slots, slot < self.total_slots)
        job = jnp.where(slot >= 2 * self.slots, 2 * self.per_layer + slot - 2 * self.slots, job)
        return jnp.logical_or(valid, conv), job


class Reducer:
    def __init__(self, place, plan, refs, outs):
        self.p, self.plan = place, plan
        self.S, self.O, self.R, self.rx, self.ry, self.r2x, self.r2y, self.z1, self.z2, self.G, self.F, self.send, self.recv, self.loc, self.fin = refs
        self.outs = outs

    def copy(self, job, kind, src, dst, dp, seq):
        return remote(src, dst, self.send.at[job, kind], self.recv.at[job, kind], dp, seq)

    def own(self, job, owner, start, count):
        ring = lax.rem(job, self.plan.o_ring)
        if not isinstance(start, int):
            start = pl.multiple_of(start, 8)
        return self.O.at[ring, owner, pl.ds(start, count)]

    def mine(self, job, start, count):
        return self.own(job, self.p.dp, start, count)

    def summed(self, job, start, count):
        ring = lax.rem(job, self.plan.f_ring)
        if not isinstance(start, int):
            start = pl.multiple_of(start, 8)
        return self.G.at[ring, pl.ds(start, count)]

    def to_sibling(self, job):
        ring = lax.rem(job, self.plan.s_ring)
        kind = self.plan.kinds - 2
        return self.copy(job, kind, self.S.at[ring], self.R.at[job], self.p.dp, self.p.sib)

    def load(self, job):
        ring = lax.rem(job, self.plan.s_ring)
        return pltpu.make_async_copy(self.R.at[job], self.S.at[ring], self.loc.at[ring])

    def z_peer(self, step):
        return lax.rem(self.p.z + step, self.plan.n_z) * 2 + self.p.core

    def xy(self, job, kind):
        p, half = self.p, self.plan.h // 2
        low, high = (0, half), (half, half)
        return {
            0: lambda: self.copy(job, 0, self.own(job, p.dpx, *low), self.rx.at[job, 0], p.dpx, p.seq),
            1: lambda: self.copy(job, 1, self.own(job, p.dpd, *low), self.rx.at[job, 1], p.dpx, p.seq),
            2: lambda: self.copy(job, 2, self.own(job, p.dpy, *high), self.ry.at[job, 0], p.dpy, p.seq),
            3: lambda: self.copy(job, 3, self.own(job, p.dpd, *high), self.ry.at[job, 1], p.dpy, p.seq),
            4: lambda: self.copy(job, 4, self.own(job, p.dpy, *low), self.r2y.at[job], p.dpy, p.seq),
            5: lambda: self.copy(job, 5, self.own(job, p.dpx, *high), self.r2x.at[job], p.dpx, p.seq),
        }[kind]()

    def keep(self):
        return self.p.parity * (self.plan.h // 2)

    def quarter(self):
        return self.keep() + (self.p.z // 2) * (self.plan.h // 4)

    def zed(self, job, kind):
        p, h = self.p, self.plan.h
        if kind == 6:
            return self.copy(job, 6, self.summed(job, (1 - p.parity) * (h // 2), h // 2), self.z1.at[job], p.dp, p.pair)
        if kind == 7:
            start = self.keep() + (1 - p.z // 2) * (h // 4)
            return self.copy(job, 7, self.summed(job, start, h // 4), self.z2.at[job], p.dp, self.z_peer(2))
        if kind == 8:
            part = self.whole(job, self.quarter(), h // 4)
            return self.copy(job, 8, part, part, p.dp, self.z_peer(2))
        part = self.whole(job, self.keep(), h // 2)
        return self.copy(job, 9, part, part, p.dp, p.pair)

    def whole(self, job, start, count):
        ring = lax.rem(job, self.plan.f_ring)
        return self.F.at[ring, pl.ds(pl.multiple_of(start, 8), count)]

    def direct(self, job, step):
        p, h = self.p, self.plan.h
        peer = lax.rem(p.dp + step, p.n_dp)
        return self.copy(job, step - 1, self.own(job, peer, 0, h), self.rx.at[job, step - 1], peer, p.seq)

    def butterfly(self, job, rnd):
        p, h = self.p, self.plan.h
        bit = (p.z // (1 << rnd)) % 2
        peer = (p.z + (1 << rnd) - 2 * bit * (1 << rnd)) * 2 + p.core
        kind = p.n_dp - 1 + rnd
        return self.copy(job, kind, self.summed(job, 0, h), self.z1.at[job, rnd], p.dp, peer)

    def add(self, dst, src):
        dst[...] = dst[...] + src[...]

    def stage(self, number, job):
        plan, p = self.plan, self.p
        h = plan.h
        half = h // 2
        if number == 0:
            self.to_sibling(job).start()
        elif number == 1:
            copy = self.to_sibling(job)
            copy.wait_recv()
            copy.wait_send()
            self.load(job).start()
        elif number == 2:
            self.load(job).wait()
            ring = lax.rem(job, plan.s_ring)
            o_ring = lax.rem(job, plan.o_ring)

            def add_owner(o):
                self.O[o_ring, o] = self.O[o_ring, o] + self.S[ring, o]

            tiles(plan.n_dp, add_owner)
            if plan.wide:
                for kind in range(4):
                    self.xy(job, kind).start()
            else:
                for step in range(1, plan.n_dp):
                    self.direct(job, step).start()
        elif number == 3:
            if plan.wide:
                self.xy(job, 0).wait_recv()
                self.xy(job, 1).wait_recv()
                self.add(self.own(job, p.dpy, 0, half), self.rx.at[job, 1])
                self.xy(job, 4).start()
                self.add(self.mine(job, 0, half), self.rx.at[job, 0])
                self.xy(job, 2).wait_recv()
                self.xy(job, 3).wait_recv()
                self.add(self.own(job, p.dpx, half, half), self.ry.at[job, 1])
                self.xy(job, 5).start()
                self.add(self.mine(job, half, half), self.ry.at[job, 0])
            else:
                for step in range(1, plan.n_dp):
                    self.direct(job, step).wait_recv()
                    self.add(self.mine(job, 0, h), self.rx.at[job, step - 1])
        elif number == 4:
            if plan.wide:
                self.xy(job, 4).wait_recv()
                self.summed(job, 0, half)[...] = self.mine(job, 0, half)[...] + self.r2y[job]
                self.xy(job, 5).wait_recv()
                self.summed(job, half, half)[...] = self.mine(job, half, half)[...] + self.r2x[job]
                self.zed(job, 6).start()
                for kind in range(6):
                    self.xy(job, kind).wait_send()
            else:
                self.summed(job, 0, h)[...] = self.mine(job, 0, h)[...]
                for step in range(1, plan.n_dp):
                    self.direct(job, step).wait_send()
                if plan.rounds > 0:
                    self.butterfly(job, 0).start()
        elif number == 5:
            if plan.wide:
                self.zed(job, 6).wait_recv()
                self.add(self.summed(job, self.keep(), half), self.z1.at[job])
                self.zed(job, 7).start()
            else:
                self.exchange(job, 0)
        elif number == 6:
            if plan.wide:
                self.zed(job, 7).wait_recv()
                total = self.summed(job, self.quarter(), h // 4)
                self.whole(job, self.quarter(), h // 4)[...] = total[...] + self.z2[job]
                self.zed(job, 8).start()
            else:
                self.exchange(job, 1)
        elif number == 7:
            if plan.wide:
                self.zed(job, 8).wait_recv()
                self.zed(job, 9).start()
        elif number == 8:
            if plan.wide:
                self.zed(job, 9).wait_recv()
            else:
                for rnd in range(2, max(plan.rounds, 3)):
                    self.exchange(job, rnd)
            self.final(job, "start")
        else:
            self.final(job, "wait")
            if plan.wide:
                for kind in range(6, 10):
                    self.zed(job, kind).wait_send()

    def exchange(self, job, rnd):
        if rnd >= self.plan.rounds:
            return
        copy = self.butterfly(job, rnd)
        copy.wait_recv()
        copy.wait_send()
        self.add(self.summed(job, 0, self.plan.h), self.z1.at[job, rnd])
        if rnd + 1 < self.plan.rounds:
            self.butterfly(job, rnd + 1).start()

    def final(self, job, what):
        plan, p = self.plan, self.p
        h = plan.h
        gm, gg, go, gc = self.outs
        layer = 1 - job // plan.per_layer
        q = lax.rem(job, plan.per_layer)
        normal = job < 2 * plan.per_layer
        src = self.whole(job, 0, h) if plan.wide else self.summed(job, 0, h)

        def put(core):
            def rows(start):
                return pl.ds(pl.multiple_of(start, 8), h)

            per_row = plan.out_jobs // 2
            return (
                (
                    jnp.logical_and(normal, q < plan.out_jobs),
                    lambda: go.at[layer, rows(core * 2 * h + (q // per_row) * h), lanes(lax.rem(q, per_row), CHUNK_N)],
                ),
                (
                    jnp.logical_and(normal, jnp.logical_and(q >= plan.out_jobs, q < plan.early)),
                    lambda: gg.at[layer, rows(core * h), lanes(q - plan.out_jobs, CHUNK_N)],
                ),
                (
                    jnp.logical_and(normal, q >= plan.early),
                    lambda: gm.at[layer, rows(core * h), lanes(q - plan.early, CHUNK_N)],
                ),
                (jnp.logical_not(normal), lambda: gc.at[job - 2 * plan.per_layer, core]),
            )

        def go_for(make, which):
            local = pltpu.make_async_copy(src, make(), self.fin.at[lax.rem(job, plan.f_ring)])
            away = self.copy(job, plan.sibling_kind, src, make(), p.dp, p.sib)
            if which == "start":
                local.start()
                away.start()
            else:
                local.wait()
                away.wait_send()

        for when, make in put(p.core):
            pl.when(when)(functools.partial(go_for, make, what))
        if what == "wait":
            for when, make in put(1 - p.core):

                def arrived(make=make):
                    self.copy(job, plan.sibling_kind, src, make(), p.dp, p.sib).wait_recv()

                pl.when(when)(arrived)

    def tick(self, t):
        for number in reversed(range(len(self.plan.offsets))):
            valid, job = self.plan.job_of(t - self.plan.offsets[number])

            @pl.when(valid)
            def _():
                self.stage(number, job)


def backward_kernel(n_dp, n_seq, dims, *refs):
    T, D, DI, CW, H, PS, N, K = dims
    plan = Plan(n_dp, n_seq, dims)
    (
        cot_ref, mask_ref, conv_ref, head_ref, x0_hbm, x1_hbm, gate_hbm, ext_hbm, step_hbm, mo_hbm, sin_hbm,
        sout_hbm, wm_hbm, wg_hbm, wo_hbm,
        hg_ref, gm, gg, go, gc, R,
        grad, x, gate, ext, step, mo, sin, sout, wrow, wcol, U, V, mixed, ldE, dtE, ldT, gmT, dgT, PG, raw, nT, gnT,
        NG, dS, dSin, maps, heads, convg, rows,
        S, O, rx, ry, r2x, r2y, z1, z2, G, F, edge_in,
        j_send, j_recv, s_loc, f_loc, l_sem, w_sem, v_sem, e_send, e_recv, r_send, r_recv,
    ) = refs
    place = Place(n_dp, n_seq)
    h = plan.h
    red = Reducer(
        place, plan, (S, O, R, rx, ry, r2x, r2y, z1, z2, G, F, j_send, j_recv, s_loc, f_loc), (gm, gg, go, gc)
    )
    CX = CW + LANES
    CHUNK = 256
    chunks = DI // CHUNK
    pairs = H // 2

    def loads(layer, is_second):
        items = ((mo_hbm, mo), (gate_hbm, gate), (step_hbm, step), (ext_hbm, ext), (sin_hbm, sin), (sout_hbm, sout))
        return [pltpu.make_async_copy(a.at[layer], b, l_sem.at[k]) for k, (a, b) in enumerate(items)]

    def load_x(layer_value, action):
        @pl.when(layer_value == 1)
        def _():
            getattr(pltpu.make_async_copy(x1_hbm, x, l_sem.at[6]), action)()

        @pl.when(layer_value == 0)
        def _():
            getattr(pltpu.make_async_copy(x0_hbm, x, l_sem.at[6]), action)()

    grad[...] = cot_ref[...] * mask_ref[...]
    PG[T : T + 8, :] = jnp.zeros((8, CW), F32)
    full_barrier(place)
    ti, tj = iota((T, T), 0), iota((T, T), 1)
    lane_low = iota((T, LANES), 1) < PS

    def produce(job, lhs, stride, offset_of, rhs):
        ring_s = lax.rem(job, plan.s_ring)
        ring_o = lax.rem(job, plan.o_ring)
        for target, buffer, ring in ((1 - place.core, S, ring_s), (place.core, O, ring_o)):
            left = jnp.concatenate(
                [lhs[pl.ds(pl.multiple_of(o * stride + offset_of(target), 8), h), :] for o in range(n_dp)], axis=0
            )
            result = mm(left, rhs)
            for o in range(n_dp):
                buffer[ring, o] = result[o * h : (o + 1) * h]

    def column_stream(hbm, count, layer, body):
        def fetch(i, slot):
            return pltpu.make_async_copy(hbm.at[layer, :, lanes(i, CHUNK_N)], wcol.at[slot], w_sem.at[slot])

        fetch(0, 0).start()

        def run(i):
            slot = lax.rem(i, 2)
            fetch(i, slot).wait()

            @pl.when(i + 1 < count)
            def _():
                fetch(i + 1, 1 - slot).start()

            body(i, slot)

        tiles(count, run)

    def layer_body(li, carry):
        layer = 1 - li
        base = li * plan.slots
        first_job = li * plan.per_layer
        head = head_ref[layer]
        items = loads(layer, li)
        for copy in items:
            copy.start()
        load_x(layer, "start")

        def fetch_row(i, slot):
            return pltpu.make_async_copy(wo_hbm.at[layer, lanes(i, 256)], wrow.at[slot], v_sem.at[slot])

        fetch_row(0, 0).start()
        items[0].wait()
        items[1].wait()

        def regate(i, squares):
            at = lanes(i, LANES)
            pre = gate[:, at]
            gated = mo[:, at] * (pre * sigmoid(pre))
            U[:, at] = gated
            return squares + gated * gated

        squares = lax.fori_loop(0, DI // LANES, regate, jnp.zeros((T, LANES), F32))
        inv_out = lax.rsqrt(jnp.sum(squares, axis=-1, keepdims=True) / DI + EPSILON)
        red.tick(base)

        def back_out(i, sums):
            slot = lax.rem(i, 2)
            fetch_row(i, slot).wait()

            @pl.when(i + 1 < DI // 256)
            def _():
                fetch_row(i + 1, 1 - slot).start()

            at = lanes(i, 256)
            q = mm(grad[...], wrow[slot], NT)
            V[:, at] = q
            gated = U[:, at]
            gnT[at, :] = (gated * inv_out).T
            product = q * gated
            return sums + product[:, 0:LANES] + product[:, LANES:256]

        sums = lax.fori_loop(0, DI // 256, back_out, jnp.zeros((T, LANES), F32))
        pull = jnp.sum(sums, axis=-1, keepdims=True) / DI * (inv_out * inv_out * inv_out)

        red.tick(base + 1)

        def out_job(i):
            per_row = plan.out_jobs // 2
            part = i // per_row
            rhs = grad[:, lanes(i % per_row, CHUNK_N)]
            produce(first_job + i, gnT, 4 * h, lambda target: target * 2 * h + part * h, rhs)
            red.tick(base + plan.lead + i)

        def degate(i):
            at = lanes(i, LANES)
            pre = gate[:, at]
            sig = sigmoid(pre)
            gated_grad = inv_out * V[:, at] - U[:, at] * pull
            gate[:, at] = gated_grad * mo[:, at] * (sig * (1.0 + pre * (1.0 - sig)))
            V[:, at] = gated_grad * (pre * sig)

        tiles(DI // LANES, degate)
        out_job(0)
        load_x(layer, "wait")
        inv_in = lax.rsqrt(jnp.mean(x[...] * x[...], axis=-1, keepdims=True) + EPSILON)
        for copy in items[2:]:
            copy.wait()
        raw_step = step[...]
        dt = softplus(raw_step + head[1:2, :])
        ld = exact(tri(T).astype(jnp.bfloat16), -jnp.exp(head[0:1, :]) * dt)
        ldT[...] = ld.T

        def expand(i):
            select = head_matrix(LANES, 256, PS, i * 256)
            ldE[:, lanes(i, 256)] = exact_right(ld, select)
            dtE[:, lanes(i, 256)] = exact_right(dt, select)

        tiles(DI // 256, expand)

        def conv_value(at):
            taps = conv_ref[pl.ds(pl.multiple_of(layer * 8, 8), 8), at]
            total = taps[K : K + 1, :]
            for k in range(K):
                total = total + taps[k : k + 1, :] * ext[8 - K + 1 + k : 8 - K + 1 + k + T, at]
            return taps, total

        def conv(i):
            at = lanes(i, 256)
            total = conv_value(at)[1]
            mixed[:, at] = total * sigmoid(total)

        tiles(CW // 256, conv)
        out_job(1)
        b_map = mixed[:, DI : DI + N]
        c_map = mixed[:, DI + N : DI + 2 * N]
        gmT[...] = jnp.where(ti <= tj, mm(b_map, c_map, NT), 0.0)
        dgT[...] = jnp.zeros((T, T), F32)
        maps[...] = jnp.zeros((T, 2 * N), F32)

        def back_state(i):
            at = lanes(i, 256)
            lifted = V[:, at] * jnp.exp(ldE[:, at])
            dSin[:, at] = mm(c_map, lifted, TN)
            maps[:, N:] = maps[:, N:] + mm(lifted, sin[:, at], NT)

        tiles(DI // 256, back_state)

        def relay_copy(chunk):
            at = lanes(chunk, CHUNK)
            return remote(
                dSin.at[:, at], dS.at[li, :, at], r_send.at[li, chunk], r_recv.at[li, chunk], place.dp, place.seq - 1
            )

        def relay(chunk):
            at = lanes(chunk, CHUNK)

            @pl.when(place.seq < n_seq - 1)
            def _():
                relay_copy(chunk).wait_recv()
                dSin[:, at] = dSin[:, at] + jnp.exp(ldE[T - 1 : T, at]) * dS[li, :, at]

            @pl.when(place.seq == n_seq - 1)
            def _():
                dS[li, :, at] = jnp.zeros((N, CHUNK), F32)

            @pl.when(place.seq > 0)
            def _():
                relay_copy(chunk).start()

        @pl.when(place.seq == n_seq - 1)
        def _():
            tiles(chunks, relay)

        out_job(2)
        nT[...] = (x[...] * inv_in).T
        NG[...] = jnp.zeros((T, D), F32)

        def back_gate(i, slot):
            NG[...] = NG[...] + mm(gate[:, lanes(i, CHUNK_N)], wcol[slot], NT)

        column_stream(wg_hbm, plan.gate_jobs, layer, back_gate)
        out_job(3)

        def gate_job(i):
            produce(first_job + plan.out_jobs + i, nT, 2 * h, lambda target: target * h, gate[:, lanes(i, CHUNK_N)])

        def diagonal(i):
            @pl.when(jnp.logical_and(place.seq < n_seq - 1, i == (n_seq - 1 - place.seq) * pairs // n_seq))
            def _():
                tiles(chunks, relay)

            at = lanes(i, LANES)
            scaled = mixed[:, at] * dtE[:, at]
            out_grad = V[:, at]
            l_tile = ldE[:, at]
            parts = []
            for side in range(2):
                column = l_tile[:, side * PS : side * PS + 1]
                row = ldT[pl.ds(2 * i + side, 1), :]
                decay = jnp.exp(jnp.minimum(row - column, 0.0))
                own_lanes = lane_low if side == 0 else jnp.logical_not(lane_low)
                pairing = mm(jnp.where(own_lanes, scaled, 0.0), out_grad, NT)
                dgT[...] = dgT[...] + decay * pairing
                parts.append(mm(gmT[...] * decay, out_grad))
            U[:, at] = jnp.where(lane_low, parts[0], parts[1])
            number = i // 2

            @pl.when(jnp.logical_and(i % 2 == 1, number < plan.gate_jobs))
            def _():
                gate_job(number)

            @pl.when(i % 2 == 1)
            def _():
                red.tick(base + plan.lead + plan.out_jobs + number)

        tiles(pairs, diagonal)
        masked = jnp.where(ti <= tj, dgT[...], 0.0)
        maps[:, 0:N] = mm(masked, c_map)
        maps[:, N:] = maps[:, N:] + mm(masked, b_map, TN)
        heads[...] = jnp.zeros((2, T, LANES), F32)
        rows[...] = jnp.zeros((8, LANES), F32)

        def back_heads(i):
            at = lanes(i, 256)
            select = head_matrix(LANES, 256, PS, i * 256)
            select32 = select.astype(F32)
            l_tile = ldE[:, at]
            heads_in = mixed[:, at]
            dt_tile = dtE[:, at]
            scaled = heads_in * dt_tile
            end_weight = jnp.exp(l_tile[T - 1 : T, :] - l_tile)
            skip = exact_right(head[2:3, :], select)
            out_grad = V[:, at]
            scaled_grad = U[:, at] + end_weight * mm(b_map, dS[li, :, at])
            maps[:, 0:N] = maps[:, 0:N] + mm(scaled * end_weight, dS[li, :, at], NT)
            decay = out_grad * (mo[:, at] - skip * heads_in) - scaled * scaled_grad
            heads[0] = heads[0] + mm(decay, select32, NT)
            heads[1] = heads[1] + mm(scaled_grad * heads_in, select32, NT)
            skip_sum = jnp.sum(out_grad * heads_in, axis=0, keepdims=True)
            end_sum = jnp.sum(dS[li, :, at] * sout[:, at], axis=0, keepdims=True)
            both = jnp.concatenate([skip_sum, end_sum, jnp.zeros((6, 256), F32)], axis=0)
            rows[...] = rows[...] + mm(both, select32, NT)
            U[:, at] = skip * out_grad + scaled_grad * dt_tile

        tiles(DI // 256, back_heads)
        red.tick(base + plan.lead + plan.early + plan.bubbles - 1)
        last_row = iota((T, LANES), 0) == T - 1
        decay_grad = heads[0] + jnp.where(last_row, rows[1:2, :], 0.0)
        rate_grad = exact(tri(T).astype(jnp.bfloat16), decay_grad, TN)
        step_grad = heads[1] - jnp.exp(head[0:1, :]) * rate_grad
        raw[:, CW:CX] = step_grad * sigmoid(raw_step + head[1:2, :])

        def back_conv(i):
            at = lanes(i, 256)
            taps, total = conv_value(at)
            sig = sigmoid(total)
            slope = sig * (1.0 + total * (1.0 - sig))

            def finish(upstream):
                pre = upstream * slope
                PG[0:T, at] = pre
                parts = [
                    jnp.sum(pre * ext[8 - K + 1 + k : 8 - K + 1 + k + T, at], axis=0, keepdims=True) for k in range(K)
                ]
                parts.append(jnp.sum(pre, axis=0, keepdims=True))
                parts.append(jnp.zeros((8 - K - 1, 256), F32))
                convg[li, :, at] = jnp.concatenate(parts, axis=0)

            @pl.when(i < DI // 256)
            def _():
                finish(U[:, lanes(jnp.minimum(i, DI // 256 - 1), 256)])

            @pl.when(i >= DI // 256)
            def _():
                finish(maps[...])

        tiles(CW // 256, back_conv)
        convg[li, :, CW:CX] = jnp.where(iota((8, LANES), 0) == 0, rows[0:1, :], 0.0)
        edge = remote(
            PG.at[pl.ds(0, 8)], edge_in.at[li], e_send.at[li], e_recv.at[li], place.dp, place.seq - 1
        )

        @pl.when(place.seq > 0)
        def _():
            edge.start()

        @pl.when(place.seq < n_seq - 1)
        def _():
            edge.wait_recv()
            PG[T : T + 8, :] = edge_in[li]

        def back_raw(i):
            at = lanes(i, 256)
            taps = conv_ref[pl.ds(pl.multiple_of(layer * 8, 8), 8), at]
            total = taps[K - 1 : K, :] * PG[0:T, at]
            for k in range(K - 1):
                total = total + taps[k : k + 1, :] * PG[K - 1 - k : K - 1 - k + T, at]
            raw[:, at] = total

        tiles(CW // 256, back_raw)

        def mix_job(i):
            produce(first_job + plan.early + i, nT, 2 * h, lambda target: target * h, raw[:, lanes(i, CHUNK_N)])
            red.tick(base + plan.lead + plan.early + plan.bubbles + i)

        def back_mix(i, slot):
            mix_job(i)
            NG[...] = NG[...] + mm(raw[:, lanes(i, CHUNK_N)], wcol[slot], NT)

        column_stream(wm_hbm, plan.mix_jobs, layer, back_mix)
        inner = jnp.sum(NG[...] * x[...], axis=-1, keepdims=True) / D
        grad[...] = grad[...] + inv_in * NG[...] - x[...] * (inner * (inv_in * inv_in * inv_in))

        @pl.when(place.seq > 0)
        def _():
            edge.wait_send()
            tiles(chunks, lambda c: relay_copy(c).wait_send())

        return carry

    lax.fori_loop(0, 2, layer_body, 0)
    hg_ref[...] = grad[...]
    base = 2 * plan.slots
    for e in range(plan.conv_jobs):
        job = 2 * plan.per_layer + e
        for block in range(plan.blocks_per_job):
            number = e * plan.blocks_per_job + block
            at = pl.ds(block * 8, 8)
            for o in range(n_dp):
                if number < plan.blocks:
                    li, c = divmod(number, plan.mix_jobs)
                    value = convg[li, :, c * CHUNK_N : (c + 1) * CHUNK_N]
                else:
                    value = jnp.zeros((8, CHUNK_N), F32)
                S[job % plan.s_ring, o, at] = value
                O[job % plan.o_ring, o, at] = value
        red.tick(base + e)
    tiles(max(plan.offsets), lambda i: red.tick(base + plan.conv_jobs + i))


def backward(cot, mask, conv, head, saved, n_dp, n_seq, dims):
    T, D, DI, CW, H, PS, N, K = dims
    plan = Plan(n_dp, n_seq, dims)
    any_spec = pl.BlockSpec(memory_space=pl.ANY)
    vmem = pl.BlockSpec(memory_space=pltpu.VMEM)
    CX = CW + LANES
    h, J = plan.h, plan.jobs
    sd = lambda *s: jax.ShapeDtypeStruct(s, F32)
    v = lambda *s: pltpu.VMEM(s, F32)
    dma = pltpu.SemaphoreType.DMA
    if plan.wide:
        received = [v(J, 2, h // 2, CHUNK_N), v(J, 2, h // 2, CHUNK_N), v(J, h // 2, CHUNK_N), v(J, h // 2, CHUNK_N),
                    v(J, h // 2, CHUNK_N), v(J, h // 4, CHUNK_N)]
    else:
        none = v(8, LANES)
        received = [v(J, n_dp - 1, h, CHUNK_N), none, none, none, v(J, max(plan.rounds, 1), h, CHUNK_N), none]
    return pl.pallas_call(
        functools.partial(backward_kernel, n_dp, n_seq, dims),
        out_shape=(
            sd(T, D), sd(2, 2 * h, CX), sd(2, 2 * h, DI), sd(2, 4 * h, D), sd(plan.conv_jobs, 2, h, CHUNK_N),
            sd(J, n_dp, h, CHUNK_N),
        ),
        in_specs=[vmem] * 4 + [any_spec] * 11,
        out_specs=(vmem,) + (any_spec,) * 5,
        scratch_shapes=[
            v(T, D), v(T, D), v(T, DI), v(T + 8, CW), v(T, LANES), v(T, DI), v(N, DI), v(N, DI),
            v(2, 256, D), v(2, D, CHUNK_N), v(T, DI), v(T, DI), v(T, CW), v(T, DI), v(T, DI), v(LANES, T), v(T, T),
            v(T, T), v(T + 8, CW), v(T, CX), v(D, T), v(DI, T), v(T, D), v(2, N, DI), v(N, DI), v(T, 2 * N),
            v(2, T, LANES), v(2, 8, CX), v(8, LANES),
            v(plan.s_ring, n_dp, h, CHUNK_N), v(plan.o_ring, n_dp, h, CHUNK_N), *received,
            v(plan.f_ring, h, CHUNK_N), v(plan.f_ring, h, CHUNK_N) if plan.wide else v(8, LANES), v(2, 8, CW),
            dma((J, plan.kinds + 1)), dma((J, plan.kinds + 1)), dma((plan.s_ring,)), dma((plan.f_ring,)), dma((7,)),
            dma((2,)), dma((2,)), dma((2,)), dma((2,)), dma((2, DI // 256)), dma((2, DI // 256)),
        ],
        compiler_params=pltpu.CompilerParams(
            collective_id=1, has_side_effects=True, vmem_limit_bytes=61 << 20
        ),
        name="backward",
    )(cot, mask, conv, head, *saved)


def on_device(hidden, cotangent, lengths, norm_gain, gate_weight, mix_weight, step_weight, conv_kernel, conv_bias,
              gated_gain, out_weight, skip_gain, log_rate, step_bias):
    n_dp, n_seq = lax.axis_size("dp"), lax.axis_size("seq")
    slots, T, D = hidden.shape
    DI, CW, H, K = gate_weight.shape[2], mix_weight.shape[2], skip_gain.shape[1], conv_kernel.shape[1]
    dims = (T, D, DI, CW, H, DI // H, (CW - DI) // 2, K)
    plan = Plan(n_dp, n_seq, dims)
    mask, conv, head, wm, wg, wo = prepare(
        hidden, lengths, norm_gain, gate_weight, mix_weight, step_weight, conv_kernel, conv_bias, gated_gain,
        out_weight, skip_gain, log_rate, step_bias, n_dp,
    )
    x = hidden[0]
    result, conv_full, *saved = forward(x, mask, conv, head, wm, wg, wo, n_dp, n_seq, dims)
    hidden_grad, gm, gg, go, gc, _ = backward(
        cotangent[0], mask, conv_full, head, (x, *saved), n_dp, n_seq, dims
    )
    gain = norm_gain[:, :, None]
    mix_grad = gm[:, :, :CW]
    step_grad = gm[:, :, CW : CW + H]
    norm_gain_grad = (
        jnp.sum(mix_grad * mix_weight, axis=2)
        + jnp.sum(gg * gate_weight, axis=2)
        + jnp.sum(step_grad * step_weight, axis=2)
    )
    gated_gain_grad = jnp.sum(go * out_weight, axis=2)
    blocks = gc[:, 0].reshape(-1, 8, CHUNK_N)[: plan.blocks]
    blocks = blocks.reshape(2, plan.mix_jobs, 8, CHUNK_N).transpose(0, 2, 1, 3).reshape(2, 8, CW + LANES)[::-1]
    shard = conv_bias.shape[1]
    own = lax.dynamic_slice(blocks, (0, 0, lax.axis_index("dp") * shard), (2, 8, shard))
    skip_grad = blocks[:, 0, CW : CW + H]
    return (
        result[None], hidden_grad[None], norm_gain_grad, gg * gain, mix_grad * gain, step_grad * gain, own[:, :K],
        own[:, K], gated_gain_grad, go * gated_gain[:, :, None], skip_grad,
    )


def solution(mesh):
    return jax.shard_map(
        on_device,
        mesh=mesh,
        in_specs=(
            P("dp", "seq", None), P("dp", "seq", None), P("dp"), P(None, "dp"), P(None, "dp", None),
            P(None, "dp", None), P(None, "dp", None), P(None, None, "dp"), P(None, "dp"), P(None, "dp"),
            P(None, "dp", None), P(), P(), P(),
        ),
        out_specs=(
            P("dp", "seq", None), P("dp", "seq", None), P(None, "dp"), P(None, "dp", None), P(None, "dp", None),
            P(None, "dp", None), P(None, None, "dp"), P(None, "dp"), P(None, "dp"), P(None, "dp", None), P(),
        ),
        check_vma=False,
    )
```

time: 1360 us -> 444 us (0.33)
  waiting for transfers between devices: 424 us -> 0 us
  Pallas kernels: 0 us -> 409 us
  matrix products: 247 us -> 0 us
  local copies, waits for them, and re-layouts: 189 us -> 8.42 us
  blocking collectives: 180 us -> 0 us
  starting transfers between devices: 175 us -> 0 us
  other arithmetic: 112 us -> 23.4 us
  between operations: 20.4 us -> 1.4 us
    pallas_call x0 -> x2, Pallas kernels: none -> 409 us  [the longest x1 255 us: backward(): pl.pallas_call(functools.partial(backward_kernel, n_dp, n_seq, dims), out...]
    dot_general x46 -> x0, matrix products: 243 us -> none  [the longest x22 136 us: matmul(): return jnp.dot(left, right, precision=HIGHEST)]
    ppermute x32 -> x0, waiting for transfers between devices: 214 us -> none  [from_behind(): lax.ppermute(value, axis, [(source, source + steps) for source in range(f...]
    ppermute x32 -> x0, starting transfers between devices: 174 us -> none  [from_behind(): lax.ppermute(value, axis, [(source, source + steps) for source in range(f...]
    psum x1 -> x0, waiting for transfers between devices: 128 us -> none  [on_device(): lax.psum((reduced[0], reduced[1], reduced[2], reduced[3], reduced[4], red...]
    all_gather x7 -> x0, blocking collectives: 91.8 us -> none  [the longest x2 36.4 us: on_device(): lax.all_gather(conv_kernel[layer_index], 'dp', axis=1, tiled=True)]
    slice x21 -> x5, local copies, waits for them, and re-layouts: 92.2 us -> 2.24 us  [the longest x1 0.91 us: on_device(): blocks = gc[:, 0].reshape(-1, 8, CHUNK_N)[:plan.blocks]]
    psum x2 -> x0, blocking collectives: 71.1 us -> none  [the longest x1 39.5 us: on_device(): skip_total = lax.psum(skip_grad, ('dp', 'seq'))]
  transfers between devices with their start and end apart: 49 -> 0, of which waited for: 33 -> 0; matrix products, arithmetic and copies ran while one was open for 38% -> 0% of each run, Pallas kernels for 0% -> 0%
where the time goes in v1:
time: 444 us; the launch traced here: 443 us
  Pallas kernels  409 us (92%)
  other arithmetic  23.4 us (5%)
  local copies, waits for them, and re-layouts  8.42 us (2%)
    pallas_call x1, Pallas kernels, backward(): pl.pallas_call(functools.partial(backward_kernel, n_dp, n_seq, dims), out...  255 us
    pallas_call x1, Pallas kernels, forward(): pl.pallas_call(functools.partial(forward_kernel, n_dp, n_seq, dims), out_...  154 us

profile of v1, /device:TPU:0, one launch (start us, length us, event | category | flops | bytes accessed | tf_op | source)
XLA Modules:
  0.0 442.6 jit_solution(12398357044266109612)
XLA Ops:
  0.6 0.0 copy-start.7
  1.3 0.7 copy.34
  2.0 1.3 select_maximum_fusion.2.refs_3_
  3.3 0.7 fusion.2
  4.1 0.5 dynamic_update_slice.3.refs_2_
  4.5 0.0 copy-start.5
  4.6 0.7 fusion.1.refs_1_
  5.2 0.9 copy.38
  6.2 0.0 copy-start.1
  6.2 3.4 broadcast_multiply_fusion.3.refs_5_
  9.6 0.0 copy-done.7
  9.6 0.0 copy-done.1
  9.6 0.0 copy-start
  9.6 0.0 copy-start.6
  9.6 1.6 broadcast_multiply_fusion.1.refs_6_
  11.3 0.0 copy-done.5
  11.3 1.0 copy-done
  12.2 0.0 copy-done.6
  12.3 1.9 fusion.refs_4_
  14.1 154.0 %forward.1 = (f32[256,768]{1,0:T(8,128)}, f32[16,1792]{1,0:T(8,128)}, f32[256,768]{1,0:T(8,128)}, f32[2,256,1536]{2,1,0:T(8,128)}, f32[2,264,1792]{2,1,0:T(8,128...) custom-call(f32[256,768]{1,0:T(8,128)} %bitcast.27, ...), custom_call_target="tpu_custom_call" | custom-call | tf_op jit(solution)/shard_map/forward/pallas_call | solution.py:545
  168.1 255.4 %backward.1 = (f32[256,768]{1,0:T(8,128)}, f32[2,192,1920]{2,1,0:T(8,128)}, f32[2,192,1536]{2,1,0:T(8,128)}, f32[2,384,768]{2,1,0:T(8,128)}, f32[1,2,96,384]{3,2,1,0:T(8,128)}, /*index=5*/f32[27,4,96,384]{3,2,1,0:T(8,128)}) custom-call(f32[256,768]{1,0:T(8,128)} %bitcast.31, f32[256,1]{1,0:T(8,128)} %fusion.1.refs_1_, f32[16,1792]{1,0:T(8,128)} %get-tuple-element.29.refs_2_, ...), custom_call_target="tpu_custom_call" | custom-call | tf_op jit(solution)/shard_map/backward/pallas_call | solution.py:1261
  423.5 1.1 slice_multiply_fusion.1
  424.7 3.7 slice_multiply_fusion
  428.3 0.7 copy.40
  429.1 0.0 copy-start.2
  429.1 4.2 broadcast_multiply_fusion.2
  433.3 0.6 add_add_fusion
  433.9 0.9 slice.26
  434.8 0.6 slice.30
  435.4 0.1 constant_dynamic-slice_fusion.1
  435.5 0.7 constant_dynamic-slice_fusion
  436.1 0.6 copy.43
  436.7 0.0 copy-done.2
  436.7 0.0 copy-start.3
  436.7 0.0 copy-start.4
  436.7 4.1 broadcast_multiply_fusion
  440.8 0.0 copy-done.3
  440.8 0.9 copy.48
  441.7 0.0 copy-done.4
  441.7 0.9 copy.49
  (3 shorter events, 0.0 us)
Async XLA Ops:
  0.6 9.0 %copy-start.7 = (f32[2,384]{1,0:T(2,128)S(1)}, f32[2,384]{1,0:T(2,128)}, u32[]{:S(2)}) copy-start(f32[2,384]{1,0:T(2,128)} %param.23) | copy-start | bytes 9220
  4.5 6.7 %copy-start.5 = (f32[16,1792]{1,0:T(8,128)}, f32[16,1792]{1,0:T(8,128)S(1)}, u32[]{:S(2)}) copy-start(f32[16,1792]{1,0:T(8,128)S(1)} %dynamic_update_slice.3.refs_2_) | copy-start | bytes 344068
  6.2 3.5 copy-start.1
  9.6 2.6 copy-start
  9.6 2.6 copy-start.6
  429.1 7.7 %copy-start.2 = (f32[2,384,768]{2,1,0:T(8,128)S(1)}, f32[2,384,768]{2,1,0:T(8,128)}, u32[]{:S(2)}) copy-start(f32[2,384,768]{2,1,0:T(8,128)} %param.24) | copy-start | bytes 7077892
  436.7 4.1 copy-start.3
  436.7 5.0 %copy-start.4 = (f32[256,768]{1,0:T(8,128)S(1)}, f32[256,768]{1,0:T(8,128)}, u32[]{:S(2)}) copy-start(f32[256,768]{1,0:T(8,128)} %get-tuple-element.40) | copy-start | bytes 2359300

commit v2 on v1

--- a/solution.py
+++ b/solution.py
@@ -323,7 +323,7 @@
     conv_in[place.dp] = conv_ref[...]
     first_in.wait()
     tiles(done_at, lambda i: tick(i + 1))
-    per_body = mix_pieces + 4 + H // 4 + gate_pieces + across
+    per_body = mix_pieces + 1 + (H // 2 + gate_pieces) // 3 + across
     ti, tj = iota((T, T), 0), iota((T, T), 1)
     lane_low = iota((T, LANES), 1) < PS
     CHUNK = 256
@@ -335,7 +335,7 @@
             (WM, wm_out), (WG, wg_out), (WO, wo_out),
         )
         return [
-            pltpu.make_async_copy(a.at[layer], b.at[layer], o_sem.at[layer * 9 + k + 1])
+            functools.partial(lambda a, b, k: pltpu.make_async_copy(a.at[layer], b.at[layer], o_sem.at[layer * 9 + k + 1]), a, b, k)
             for k, (a, b) in enumerate(saved)
         ]
 
@@ -367,11 +367,11 @@
 
         step[layer] = raw
         tick(base + mix_pieces - 1)
+        saved_copies(layer)[6]().start()
         dt = softplus(raw + head[1:2, :])
         rate = -jnp.exp(head[0:1, :]) * dt
         ld = exact(tri(T).astype(jnp.bfloat16), rate)
         ldT[...] = ld.T
-        tick(base + mix_pieces)
 
         def expand(i):
             select = head_matrix(LANES, 256, PS, i * 256)
@@ -379,7 +379,6 @@
             dtE[:, lanes(i, 256)] = exact_right(dt, select)
 
         tiles(DI // 256, expand)
-        tick(base + mix_pieces + 1)
 
         @pl.when(layer == 0)
         def _():
@@ -408,7 +407,7 @@
             mixed[:, at] = total * sigmoid(total)
 
         tiles(CW // 256, conv)
-        tick(base + mix_pieces + 2)
+        tick(base + mix_pieces)
         b_map = mixed[:, DI : DI + N]
         c_map = mixed[:, DI + N : DI + 2 * N]
         gm[...] = jnp.where(ti >= tj, mm(c_map, b_map, NT), 0.0)
@@ -420,7 +419,6 @@
             sout[layer, :, at] = mm(b_map, weighted, TN)
 
         tiles(DI // 256, local_state)
-        tick(base + mix_pieces + 3)
 
         def relay_copy(chunk):
             at = lanes(chunk, CHUNK)
@@ -448,11 +446,10 @@
 
         pairs = H // 2
 
+        items = pairs + gate_pieces
+        relay_from = place.seq * (items - chunks) // (n_seq - 1)
+
         def diagonal(i):
-            @pl.when(i == place.seq * pairs // n_seq)
-            def _():
-                tiles(chunks, relay)
-
             at = lanes(i, LANES)
             scaled = mixed[:, at] * dtE[:, at]
             l_tile = ldE[:, at]
@@ -464,19 +461,37 @@
                 parts.append(mm(weights, scaled))
             diag[:, at] = jnp.where(lane_low, parts[0], parts[1])
 
-            @pl.when(i % 2 == 1)
-            def _():
-                tick(base + mix_pieces + 4 + i // 2)
-
-        tiles(pairs, diagonal)
-
-        def skip_row(i):
-            return exact_right(head[2:3, :], head_matrix(LANES, 256, PS, i * 256))
 
         def gate_proj(i):
             at = lanes(i, PIECE)
             gate[layer, :, at] = mm(xs[layer] * inv, WG[layer, :, at])
-            tick(base + mix_pieces + 4 + H // 4 + i)
+
+        def work_item(i):
+            @pl.when(i < pairs)
+            def _():
+                diagonal(i)
+
+            @pl.when(i == pairs)
+            def _():
+                own_copy(1, layer).wait()
+
+            @pl.when(i >= pairs)
+            def _():
+                gate_proj(i - pairs)
+
+            @pl.when(jnp.logical_and(i >= relay_from, i < relay_from + chunks))
+            def _():
+                relay(i - relay_from)
+
+            @pl.when(i % 3 == 2)
+            def _():
+                tick(base + mix_pieces + 1 + i // 3)
+
+        tiles(items, work_item)
+        saved_copies(layer)[7]().start()
+
+        def skip_row(i):
+            return exact_right(head[2:3, :], head_matrix(LANES, 256, PS, i * 256))
 
         def off(i):
             at = lanes(i, 256)
@@ -485,8 +500,6 @@
             mo[layer, :, at] = out
 
         tiles(DI // 256, off)
-        own_copy(1, layer).wait()
-        tiles(gate_pieces, gate_proj)
 
         def gating(i, squares):
             at = lanes(i, LANES)
@@ -498,17 +511,18 @@
         squares = lax.fori_loop(0, DI // LANES, gating, jnp.zeros((T, LANES), F32))
         inv_out = lax.rsqrt(jnp.sum(squares, axis=-1, keepdims=True) / DI + EPSILON)
         own_copy(2, layer).wait()
+        tiles(across, lambda i: tick(base + mix_pieces + 1 + items // 3 + i))
 
         def project_out(i):
             at = lanes(i, PIECE)
-            tick(base + mix_pieces + 4 + H // 4 + gate_pieces + i)
             branch = mm(diag[...] * inv_out, WO[layer, :, at])
             nxt = xs[layer, :, at] + branch
             xs[layer + 1, :, at] = nxt
 
         tiles(across, project_out)
-        for copy in saved_copies(layer):
-            copy.start()
+        for number, copy in enumerate(saved_copies(layer)):
+            if number < 6 or number == 8:
+                copy().start()
         @pl.when(place.seq < n_seq - 1)
         def _():
             edge.wait_send()
@@ -528,7 +542,7 @@
         conv_copy(s).wait_send()
     for layer in range(layers):
         for copy in saved_copies(layer):
-            copy.wait()
+            copy().wait()
     last.wait()
 
 
@@ -605,9 +619,10 @@
         self.total_slots = 2 * self.slots + self.conv_jobs
         self.wide = n_dp == 4 and self.n_z == 4 and self.h % 32 == 0
         self.rounds = self.n_z.bit_length() - 1
-        self.offsets = (0, 1, 2, 4, 6, 8, 10, 12, 14, 15)
+        self.offsets = (0, 1, 2, 4, 6, 9, 12, 15, 18, 19)
         self.o_ring = self.offsets[4] + 1
         self.f_ring = max(self.offsets) + 1
+        self.r_ring = (self.jobs + 1) // 2
         self.s_ring = self.offsets[2] + 1
         self.kinds = 12 if self.wide else n_dp - 1 + self.rounds + 2
         self.sibling_kind = self.kinds - 1
@@ -654,6 +669,9 @@
         kind = self.plan.kinds - 2
         return self.copy(job, kind, self.S.at[ring], self.R.at[job], self.p.dp, self.p.sib)
 
+    def slot(self, job):
+        return lax.rem(job, self.plan.r_ring)
+
     def load(self, job):
         ring = lax.rem(job, self.plan.s_ring)
         return pltpu.make_async_copy(self.R.at[job], self.S.at[ring], self.loc.at[ring])
@@ -665,12 +683,12 @@
         p, half = self.p, self.plan.h // 2
         low, high = (0, half), (half, half)
         return {
-            0: lambda: self.copy(job, 0, self.own(job, p.dpx, *low), self.rx.at[job, 0], p.dpx, p.seq),
-            1: lambda: self.copy(job, 1, self.own(job, p.dpd, *low), self.rx.at[job, 1], p.dpx, p.seq),
-            2: lambda: self.copy(job, 2, self.own(job, p.dpy, *high), self.ry.at[job, 0], p.dpy, p.seq),
-            3: lambda: self.copy(job, 3, self.own(job, p.dpd, *high), self.ry.at[job, 1], p.dpy, p.seq),
-            4: lambda: self.copy(job, 4, self.own(job, p.dpy, *low), self.r2y.at[job], p.dpy, p.seq),
-            5: lambda: self.copy(job, 5, self.own(job, p.dpx, *high), self.r2x.at[job], p.dpx, p.seq),
+            0: lambda: self.copy(job, 0, self.own(job, p.dpx, *low), self.rx.at[self.slot(job), 0], p.dpx, p.seq),
+            1: lambda: self.copy(job, 1, self.own(job, p.dpd, *low), self.rx.at[self.slot(job), 1], p.dpx, p.seq),
+            2: lambda: self.copy(job, 2, self.own(job, p.dpy, *high), self.ry.at[self.slot(job), 0], p.dpy, p.seq),
+            3: lambda: self.copy(job, 3, self.own(job, p.dpd, *high), self.ry.at[self.slot(job), 1], p.dpy, p.seq),
+            4: lambda: self.copy(job, 4, self.own(job, p.dpy, *low), self.r2y.at[self.slot(job)], p.dpy, p.seq),
+            5: lambda: self.copy(job, 5, self.own(job, p.dpx, *high), self.r2x.at[self.slot(job)], p.dpx, p.seq),
         }[kind]()
 
     def keep(self):
@@ -682,10 +700,10 @@
     def zed(self, job, kind):
         p, h = self.p, self.plan.h
         if kind == 6:
-            return self.copy(job, 6, self.summed(job, (1 - p.parity) * (h // 2), h // 2), self.z1.at[job], p.dp, p.pair)
+            return self.copy(job, 6, self.summed(job, (1 - p.parity) * (h // 2), h // 2), self.z1.at[self.slot(job)], p.dp, p.pair)
         if kind == 7:
             start = self.keep() + (1 - p.z // 2) * (h // 4)
-            return self.copy(job, 7, self.summed(job, start, h // 4), self.z2.at[job], p.dp, self.z_peer(2))
+            return self.copy(job, 7, self.summed(job, start, h // 4), self.z2.at[self.slot(job)], p.dp, self.z_peer(2))
         if kind == 8:
             part = self.whole(job, self.quarter(), h // 4)
             return self.copy(job, 8, part, part, p.dp, self.z_peer(2))
@@ -699,14 +717,14 @@
     def direct(self, job, step):
         p, h = self.p, self.plan.h
         peer = lax.rem(p.dp + step, p.n_dp)
-        return self.copy(job, step - 1, self.own(job, peer, 0, h), self.rx.at[job, step - 1], peer, p.seq)
+        return self.copy(job, step - 1, self.own(job, peer, 0, h), self.rx.at[self.slot(job), step - 1], peer, p.seq)
 
     def butterfly(self, job, rnd):
         p, h = self.p, self.plan.h
         bit = (p.z // (1 << rnd)) % 2
         peer = (p.z + (1 << rnd) - 2 * bit * (1 << rnd)) * 2 + p.core
         kind = p.n_dp - 1 + rnd
-        return self.copy(job, kind, self.summed(job, 0, h), self.z1.at[job, rnd], p.dp, peer)
+        return self.copy(job, kind, self.summed(job, 0, h), self.z1.at[self.slot(job), rnd], p.dp, peer)
 
     def add(self, dst, src):
         dst[...] = dst[...] + src[...]
@@ -739,26 +757,24 @@
                     self.direct(job, step).start()
         elif number == 3:
             if plan.wide:
-                self.xy(job, 0).wait_recv()
-                self.xy(job, 1).wait_recv()
-                self.add(self.own(job, p.dpy, 0, half), self.rx.at[job, 1])
+                for kind in range(4):
+                    self.xy(job, kind).wait_recv()
+                self.add(self.own(job, p.dpy, 0, half), self.rx.at[self.slot(job), 1])
+                self.add(self.own(job, p.dpx, half, half), self.ry.at[self.slot(job), 1])
+                self.add(self.mine(job, 0, half), self.rx.at[self.slot(job), 0])
+                self.add(self.mine(job, half, half), self.ry.at[self.slot(job), 0])
                 self.xy(job, 4).start()
-                self.add(self.mine(job, 0, half), self.rx.at[job, 0])
-                self.xy(job, 2).wait_recv()
-                self.xy(job, 3).wait_recv()
-                self.add(self.own(job, p.dpx, half, half), self.ry.at[job, 1])
                 self.xy(job, 5).start()
-                self.add(self.mine(job, half, half), self.ry.at[job, 0])
             else:
                 for step in range(1, plan.n_dp):
                     self.direct(job, step).wait_recv()
-                    self.add(self.mine(job, 0, h), self.rx.at[job, step - 1])
+                    self.add(self.mine(job, 0, h), self.rx.at[self.slot(job), step - 1])
         elif number == 4:
             if plan.wide:
                 self.xy(job, 4).wait_recv()
-                self.summed(job, 0, half)[...] = self.mine(job, 0, half)[...] + self.r2y[job]
+                self.summed(job, 0, half)[...] = self.mine(job, 0, half)[...] + self.r2y[self.slot(job)]
                 self.xy(job, 5).wait_recv()
-                self.summed(job, half, half)[...] = self.mine(job, half, half)[...] + self.r2x[job]
+                self.summed(job, half, half)[...] = self.mine(job, half, half)[...] + self.r2x[self.slot(job)]
                 self.zed(job, 6).start()
                 for kind in range(6):
                     self.xy(job, kind).wait_send()
@@ -771,7 +787,7 @@
         elif number == 5:
             if plan.wide:
                 self.zed(job, 6).wait_recv()
-                self.add(self.summed(job, self.keep(), half), self.z1.at[job])
+                self.add(self.summed(job, self.keep(), half), self.z1.at[self.slot(job)])
                 self.zed(job, 7).start()
             else:
                 self.exchange(job, 0)
@@ -779,7 +795,7 @@
             if plan.wide:
                 self.zed(job, 7).wait_recv()
                 total = self.summed(job, self.quarter(), h // 4)
-                self.whole(job, self.quarter(), h // 4)[...] = total[...] + self.z2[job]
+                self.whole(job, self.quarter(), h // 4)[...] = total[...] + self.z2[self.slot(job)]
                 self.zed(job, 8).start()
             else:
                 self.exchange(job, 1)
@@ -806,7 +822,7 @@
         copy = self.butterfly(job, rnd)
         copy.wait_recv()
         copy.wait_send()
-        self.add(self.summed(job, 0, self.plan.h), self.z1.at[job, rnd])
+        self.add(self.summed(job, 0, self.plan.h), self.z1.at[self.slot(job), rnd])
         if rnd + 1 < self.plan.rounds:
             self.butterfly(job, rnd + 1).start()
 
@@ -891,18 +907,31 @@
     chunks = DI // CHUNK
     pairs = H // 2
 
-    def loads(layer, is_second):
-        items = ((mo_hbm, mo), (gate_hbm, gate), (step_hbm, step), (ext_hbm, ext), (sin_hbm, sin), (sout_hbm, sout))
-        return [pltpu.make_async_copy(a.at[layer], b, l_sem.at[k]) for k, (a, b) in enumerate(items)]
+    def load_of(layer, k):
+        source, target = (
+            (mo_hbm, mo), (gate_hbm, gate), (step_hbm, step), (ext_hbm, ext), (sin_hbm, sin), (sout_hbm, sout),
+            (wo_hbm, wrow),
+        )[k]
+        return pltpu.make_async_copy(source.at[layer], target, l_sem.at[k])
+
+    class Load:
+        def __init__(self, layer, k):
+            self.layer, self.k = layer, k
+
+        def wait(self):
+            load_of(self.layer, self.k).wait()
+
+    for k in range(7):
+        load_of(1, k).start()
 
     def load_x(layer_value, action):
         @pl.when(layer_value == 1)
         def _():
-            getattr(pltpu.make_async_copy(x1_hbm, x, l_sem.at[6]), action)()
+            getattr(pltpu.make_async_copy(x1_hbm, x, l_sem.at[7]), action)()
 
         @pl.when(layer_value == 0)
         def _():
-            getattr(pltpu.make_async_copy(x0_hbm, x, l_sem.at[6]), action)()
+            getattr(pltpu.make_async_copy(x0_hbm, x, l_sem.at[7]), action)()
 
     grad[...] = cot_ref[...] * mask_ref[...]
     PG[T : T + 8, :] = jnp.zeros((8, CW), F32)
@@ -926,35 +955,30 @@
             return pltpu.make_async_copy(hbm.at[layer, :, lanes(i, CHUNK_N)], wcol.at[slot], w_sem.at[slot])
 
         fetch(0, 0).start()
+        fetch(1, 1).start()
 
         def run(i):
-            slot = lax.rem(i, 2)
+            slot = lax.rem(i, 3)
             fetch(i, slot).wait()
 
-            @pl.when(i + 1 < count)
-            def _():
-                fetch(i + 1, 1 - slot).start()
+            @pl.when(i + 2 < count)
+            def _():
+                fetch(i + 2, lax.rem(i + 2, 3)).start()
 
             body(i, slot)
 
-        tiles(count, run)
+        return run
 
     def layer_body(li, carry):
         layer = 1 - li
         base = li * plan.slots
         first_job = li * plan.per_layer
         head = head_ref[layer]
-        items = loads(layer, li)
-        for copy in items:
-            copy.start()
+        loads = [Load(layer, k) for k in range(7)]
         load_x(layer, "start")
 
-        def fetch_row(i, slot):
-            return pltpu.make_async_copy(wo_hbm.at[layer, lanes(i, 256)], wrow.at[slot], v_sem.at[slot])
-
-        fetch_row(0, 0).start()
-        items[0].wait()
-        items[1].wait()
+        loads[0].wait()
+        loads[1].wait()
 
         def regate(i, squares):
             at = lanes(i, LANES)
@@ -966,17 +990,11 @@
         squares = lax.fori_loop(0, DI // LANES, regate, jnp.zeros((T, LANES), F32))
         inv_out = lax.rsqrt(jnp.sum(squares, axis=-1, keepdims=True) / DI + EPSILON)
         red.tick(base)
+        loads[6].wait()
 
         def back_out(i, sums):
-            slot = lax.rem(i, 2)
-            fetch_row(i, slot).wait()
-
-            @pl.when(i + 1 < DI // 256)
-            def _():
-                fetch_row(i + 1, 1 - slot).start()
-
             at = lanes(i, 256)
-            q = mm(grad[...], wrow[slot], NT)
+            q = mm(grad[...], wrow[at, :], NT)
             V[:, at] = q
             gated = U[:, at]
             gnT[at, :] = (gated * inv_out).T
@@ -988,11 +1006,18 @@
 
         red.tick(base + 1)
 
-        def out_job(i):
+        @pl.when(li == 0)
+        def _():
+            load_of(0, 6).start()
+
+        def out_piece(i):
             per_row = plan.out_jobs // 2
             part = i // per_row
             rhs = grad[:, lanes(i % per_row, CHUNK_N)]
             produce(first_job + i, gnT, 4 * h, lambda target: target * 2 * h + part * h, rhs)
+
+        def out_job(i):
+            out_piece(i)
             red.tick(base + plan.lead + i)
 
         def degate(i):
@@ -1007,7 +1032,7 @@
         out_job(0)
         load_x(layer, "wait")
         inv_in = lax.rsqrt(jnp.mean(x[...] * x[...], axis=-1, keepdims=True) + EPSILON)
-        for copy in items[2:]:
+        for copy in loads[2:6]:
             copy.wait()
         raw_step = step[...]
         dt = softplus(raw_step + head[1:2, :])
@@ -1071,28 +1096,20 @@
             def _():
                 relay_copy(chunk).start()
 
-        @pl.when(place.seq == n_seq - 1)
-        def _():
-            tiles(chunks, relay)
-
-        out_job(2)
+        items = pairs + plan.gate_jobs
+        relay_from = (n_seq - 1 - place.seq) * (items - chunks) // (n_seq - 1)
         nT[...] = (x[...] * inv_in).T
         NG[...] = jnp.zeros((T, D), F32)
 
         def back_gate(i, slot):
             NG[...] = NG[...] + mm(gate[:, lanes(i, CHUNK_N)], wcol[slot], NT)
 
-        column_stream(wg_hbm, plan.gate_jobs, layer, back_gate)
-        out_job(3)
+        gate_stream = column_stream(wg_hbm, plan.gate_jobs, layer, back_gate)
 
         def gate_job(i):
             produce(first_job + plan.out_jobs + i, nT, 2 * h, lambda target: target * h, gate[:, lanes(i, CHUNK_N)])
 
         def diagonal(i):
-            @pl.when(jnp.logical_and(place.seq < n_seq - 1, i == (n_seq - 1 - place.seq) * pairs // n_seq))
-            def _():
-                tiles(chunks, relay)
-
             at = lanes(i, LANES)
             scaled = mixed[:, at] * dtE[:, at]
             out_grad = V[:, at]
@@ -1107,17 +1124,36 @@
                 dgT[...] = dgT[...] + decay * pairing
                 parts.append(mm(gmT[...] * decay, out_grad))
             U[:, at] = jnp.where(lane_low, parts[0], parts[1])
-            number = i // 2
-
-            @pl.when(jnp.logical_and(i % 2 == 1, number < plan.gate_jobs))
-            def _():
-                gate_job(number)
+
+        def work_item(i):
+            @pl.when(i < pairs)
+            def _():
+                diagonal(i)
+
+            @pl.when(i >= pairs)
+            def _():
+                gate_stream(i - pairs)
+
+            @pl.when(jnp.logical_and(i >= relay_from, i < relay_from + chunks))
+            def _():
+                relay(i - relay_from)
+
+            number = i // 2 + 2
+
+            @pl.when(jnp.logical_and(i % 2 == 1, number < plan.out_jobs))
+            def _():
+                out_piece(number)
+
+            @pl.when(jnp.logical_and(i % 2 == 1, jnp.logical_and(number >= plan.out_jobs, number < plan.early)))
+            def _():
+                gate_job(number - plan.out_jobs)
 
             @pl.when(i % 2 == 1)
             def _():
-                red.tick(base + plan.lead + plan.out_jobs + number)
-
-        tiles(pairs, diagonal)
+                red.tick(base + plan.lead + number)
+
+        tiles(items, work_item)
+        mix_stream = column_stream(wm_hbm, plan.mix_jobs, layer, lambda i, slot: back_mix(i, slot))
         masked = jnp.where(ti <= tj, dgT[...], 0.0)
         maps[:, 0:N] = mm(masked, c_map)
         maps[:, N:] = maps[:, N:] + mm(masked, b_map, TN)
@@ -1180,6 +1216,12 @@
 
         tiles(CW // 256, back_conv)
         convg[li, :, CW:CX] = jnp.where(iota((8, LANES), 0) == 0, rows[0:1, :], 0.0)
+
+        @pl.when(li == 0)
+        def _():
+            for k in range(6):
+                load_of(0, k).start()
+
         edge = remote(
             PG.at[pl.ds(0, 8)], edge_in.at[li], e_send.at[li], e_recv.at[li], place.dp, place.seq - 1
         )
@@ -1211,7 +1253,7 @@
             mix_job(i)
             NG[...] = NG[...] + mm(raw[:, lanes(i, CHUNK_N)], wcol[slot], NT)
 
-        column_stream(wm_hbm, plan.mix_jobs, layer, back_mix)
+        tiles(plan.mix_jobs, mix_stream)
         inner = jnp.sum(NG[...] * x[...], axis=-1, keepdims=True) / D
         grad[...] = grad[...] + inv_in * NG[...] - x[...] * (inner * (inv_in * inv_in * inv_in))
 
@@ -1248,16 +1290,16 @@
     any_spec = pl.BlockSpec(memory_space=pl.ANY)
     vmem = pl.BlockSpec(memory_space=pltpu.VMEM)
     CX = CW + LANES
-    h, J = plan.h, plan.jobs
+    h, J, ring = plan.h, plan.jobs, plan.r_ring
     sd = lambda *s: jax.ShapeDtypeStruct(s, F32)
     v = lambda *s: pltpu.VMEM(s, F32)
     dma = pltpu.SemaphoreType.DMA
     if plan.wide:
-        received = [v(J, 2, h // 2, CHUNK_N), v(J, 2, h // 2, CHUNK_N), v(J, h // 2, CHUNK_N), v(J, h // 2, CHUNK_N),
-                    v(J, h // 2, CHUNK_N), v(J, h // 4, CHUNK_N)]
+        received = [v(ring, 2, h // 2, CHUNK_N), v(ring, 2, h // 2, CHUNK_N), v(ring, h // 2, CHUNK_N),
+                    v(ring, h // 2, CHUNK_N), v(ring, h // 2, CHUNK_N), v(ring, h // 4, CHUNK_N)]
     else:
         none = v(8, LANES)
-        received = [v(J, n_dp - 1, h, CHUNK_N), none, none, none, v(J, max(plan.rounds, 1), h, CHUNK_N), none]
+        received = [v(ring, n_dp - 1, h, CHUNK_N), none, none, none, v(ring, max(plan.rounds, 1), h, CHUNK_N), none]
     return pl.pallas_call(
         functools.partial(backward_kernel, n_dp, n_seq, dims),
         out_shape=(
@@ -1268,13 +1310,13 @@
         out_specs=(vmem,) + (any_spec,) * 5,
         scratch_shapes=[
             v(T, D), v(T, D), v(T, DI), v(T + 8, CW), v(T, LANES), v(T, DI), v(N, DI), v(N, DI),
-            v(2, 256, D), v(2, D, CHUNK_N), v(T, DI), v(T, DI), v(T, CW), v(T, DI), v(T, DI), v(LANES, T), v(T, T),
+            v(DI, D), v(3, D, CHUNK_N), v(T, DI), v(T, DI), v(T, CW), v(T, DI), v(T, DI), v(LANES, T), v(T, T),
             v(T, T), v(T + 8, CW), v(T, CX), v(D, T), v(DI, T), v(T, D), v(2, N, DI), v(N, DI), v(T, 2 * N),
             v(2, T, LANES), v(2, 8, CX), v(8, LANES),
             v(plan.s_ring, n_dp, h, CHUNK_N), v(plan.o_ring, n_dp, h, CHUNK_N), *received,
             v(plan.f_ring, h, CHUNK_N), v(plan.f_ring, h, CHUNK_N) if plan.wide else v(8, LANES), v(2, 8, CW),
-            dma((J, plan.kinds + 1)), dma((J, plan.kinds + 1)), dma((plan.s_ring,)), dma((plan.f_ring,)), dma((7,)),
-            dma((2,)), dma((2,)), dma((2,)), dma((2,)), dma((2, DI // 256)), dma((2, DI // 256)),
+            dma((J, plan.kinds + 1)), dma((J, plan.kinds + 1)), dma((plan.s_ring,)), dma((plan.f_ring,)), dma((8,)),
+            dma((3,)), dma((2,)), dma((2,)), dma((2,)), dma((2, DI // 256)), dma((2, DI // 256)),
         ],
         compiler_params=pltpu.CompilerParams(
             collective_id=1, has_side_effects=True, vmem_limit_bytes=61 << 20

time: 444 us -> 401 us (0.903)
  Pallas kernels: 409 us -> 367 us
    pallas_call x1, Pallas kernels: 255 us -> 225 us  [backward(): pl.pallas_call(functools.partial(backward_kernel, n_dp, n_seq, dims), out...]
    pallas_call x1, Pallas kernels: 154 us -> 143 us  [forward(): pl.pallas_call(functools.partial(forward_kernel, n_dp, n_seq, dims), out_...]
where the time goes in v2:
time: 401 us; the launch traced here: 400 us
  Pallas kernels  367 us (92%)
  other arithmetic  23.4 us (6%)
  local copies, waits for them, and re-layouts  8.42 us (2%)
    pallas_call x1, Pallas kernels, backward(): pl.pallas_call(functools.partial(backward_kernel, n_dp, n_seq, dims), out...  225 us
    pallas_call x1, Pallas kernels, forward(): pl.pallas_call(functools.partial(forward_kernel, n_dp, n_seq, dims), out_...  143 us

profile of v2, /device:TPU:0, one launch (start us, length us, event | category | flops | bytes accessed | tf_op | source)
XLA Modules:
  0.0 400.4 jit_solution(16134394730904794127)
XLA Ops:
  0.6 0.0 copy-start.7
  1.3 0.7 copy.34
  2.0 1.3 select_maximum_fusion.2.refs_3_
  3.3 0.7 fusion.2
  4.1 0.5 dynamic_update_slice.3.refs_2_
  4.5 0.0 copy-start.5
  4.6 0.7 fusion.1.refs_1_
  5.2 0.9 copy.38
  6.2 0.0 copy-start.1
  6.2 3.4 broadcast_multiply_fusion.3.refs_5_
  9.6 0.0 copy-done.7
  9.6 0.0 copy-done.1
  9.6 0.0 copy-start
  9.6 0.0 copy-start.6
  9.6 1.6 broadcast_multiply_fusion.1.refs_6_
  11.3 0.0 copy-done.5
  11.3 1.0 copy-done
  12.2 0.0 copy-done.6
  12.3 1.9 fusion.refs_4_
  14.1 142.6 %forward.1 = (f32[256,768]{1,0:T(8,128)}, f32[16,1792]{1,0:T(8,128)}, f32[256,768]{1,0:T(8,128)}, f32[2,256,1536]{2,1,0:T(8,128)}, f32[2,264,1792]{2,1,0:T(8,128...) custom-call(f32[256,768]{1,0:T(8,128)} %bitcast.27, ...), custom_call_target="tpu_custom_call" | custom-call | tf_op jit(solution)/shard_map/forward/pallas_call | solution.py:559
  156.7 224.7 %backward.1 = (f32[256,768]{1,0:T(8,128)}, f32[2,192,1920]{2,1,0:T(8,128)}, f32[2,192,1536]{2,1,0:T(8,128)}, f32[2,384,768]{2,1,0:T(8,128)}, f32[1,2,96,384]{3,2,1,0:T(8,128)}, /*index=5*/f32[27,4,96,384]{3,2,1,0:T(8,128)}) custom-call(f32[256,768]{1,0:T(8,128)} %bitcast.31, f32[256,1]{1,0:T(8,128)} %fusion.1.refs_1_, f32[16,1792]{1,0:T(8,128)} %get-tuple-element.29.refs_2_, ...), custom_call_target="tpu_custom_call" | custom-call | tf_op jit(solution)/shard_map/backward/pallas_call | solution.py:1303
  381.3 1.1 slice_multiply_fusion.1
  382.5 3.7 slice_multiply_fusion
  386.1 0.7 copy.40
  386.9 0.0 copy-start.2
  386.9 4.2 %broadcast_multiply_fusion.2 = (f32[2,192,1536]{2,1,0:T(8,128)}, f32[2,192]{1,0:T(2,128)S(1)}) fusion(f32[2,192,1536]{2,1,0:T(8,128)} %get-tuple-element.42, f32[2,192]{1,0:T(2,128)S(1)} %copy-done.6, f32[2,192,1536]{2,1,0:T(8,128)} %param.18), kind=kLoop, calls=%fused_computation.9 | loop fusion | flops 1769088 | bytes 7080960 | tf_op jit(solution)/shard_map/mul | solution.py:1359
  391.1 0.6 add_add_fusion
  391.7 0.9 slice.26
  392.6 0.6 slice.30
  393.2 0.1 constant_dynamic-slice_fusion.1
  393.3 0.7 constant_dynamic-slice_fusion
  393.9 0.6 copy.43
  394.5 0.0 copy-done.2
  394.5 0.0 copy-start.3
  394.5 0.0 copy-start.4
  394.5 4.1 %broadcast_multiply_fusion = (f32[2,384,768]{2,1,0:T(8,128)}, f32[2,384]{1,0:T(2,128)}) fusion(f32[2,384,768]{2,1,0:T(8,128)} %get-tuple-element.44, f32[2,384]{1,0:T(2,128)S(1)} %copy-done.7, f32[2,384,768]{2,1,0:T(8,128)S(1)} %copy-done.2), kind=kLoop, calls=%fused_computation.7 | loop fusion | flops 1768704 | bytes 7084032 | tf_op jit(solution)/shard_map/mul | solution.py:1360
  398.6 0.0 copy-done.3
  398.6 0.9 copy.48
  399.5 0.0 copy-done.4
  399.5 0.9 copy.49
  (3 shorter events, 0.0 us)
Async XLA Ops:
  0.6 9.0 %copy-start.7 = (f32[2,384]{1,0:T(2,128)S(1)}, f32[2,384]{1,0:T(2,128)}, u32[]{:S(2)}) copy-start(f32[2,384]{1,0:T(2,128)} %param.23) | copy-start | bytes 9220
  4.5 6.7 %copy-start.5 = (f32[16,1792]{1,0:T(8,128)}, f32[16,1792]{1,0:T(8,128)S(1)}, u32[]{:S(2)}) copy-start(f32[16,1792]{1,0:T(8,128)S(1)} %dynamic_update_slice.3.refs_2_) | copy-start | bytes 344068
  6.2 3.5 copy-start.1
  9.6 2.6 copy-start
  9.6 2.6 copy-start.6
  386.9 7.7 %copy-start.2 = (f32[2,384,768]{2,1,0:T(8,128)S(1)}, f32[2,384,768]{2,1,0:T(8,128)}, u32[]{:S(2)}) copy-start(f32[2,384,768]{2,1,0:T(8,128)} %param.24) | copy-start | bytes 7077892
  394.5 4.1 %copy-start.3 = (f32[256,768]{1,0:T(8,128)S(1)}, f32[256,768]{1,0:T(8,128)}, u32[]{:S(2)}) copy-start(f32[256,768]{1,0:T(8,128)} %get-tuple-element.28) | copy-start | bytes 2359300
  394.5 5.0 %copy-start.4 = (f32[256,768]{1,0:T(8,128)S(1)}, f32[256,768]{1,0:T(8,128)}, u32[]{:S(2)}) copy-start(f32[256,768]{1,0:T(8,128)} %get-tuple-element.40) | copy-start | bytes 2359300

commit v3 on v2

--- a/solution.py
+++ b/solution.py
@@ -147,8 +147,8 @@
 
 
 class Gather:
-    def __init__(self, place, own, dest, stride, row_of, columns, half, sems, index):
-        self.p, self.own, self.dest = place, own, dest
+    def __init__(self, place, dest, stride, row_of, columns, half, sems, index):
+        self.p, self.dest = place, dest
         self.stride, self.row_of, self.columns = stride, row_of, columns
         self.send, self.recv = sems
         self.index = index
@@ -164,8 +164,16 @@
         return remote(src, dst, self.send.at[self.index, kind], self.recv.at[self.index, kind], dp, seq)
 
     def own_part(self, offset, count):
-        start = self.row_of(self.p.core) + offset
-        return self.own.at[pl.ds(pl.multiple_of(start, 8), count), self.columns]
+        return self.at(self.p.dp, self.p.core, offset, count)
+
+    def scale(self, gain):
+        for core in range(2):
+            rows = self.at(self.p.dp, core, 0, self.half)
+            start = self.row_of(core)
+            if not isinstance(start, int):
+                start = pl.multiple_of(start, 8)
+            column = gain[pl.ds(start, self.half), :]
+            rows[...] = rows[...] * jnp.concatenate([column] * (PIECE // LANES), axis=1)
 
     def get(self, kind):
         p, t = self.p, self.third
@@ -256,7 +264,7 @@
 
 def forward_kernel(n_dp, n_seq, dims, *refs):
     (
-        x_hbm, mask_ref, conv_ref, head_ref, wm_own, wg_own, wo_own,
+        x_hbm, mask_ref, conv_ref, head_ref, norm_ref, gated_ref, wm_own, wg_own, wo_own, ws_own,
         result_ref, conv_full, xs_out, gate_out, ext_out, step_out, mo_out, sin_out, sout_out, wm_out, wg_out, wo_out,
         WM, WG, WO, xs, gate, ext, step, mo, sin, sout, conv_in, mixed, diag, ldE, dtE, ldT, gm,
         g_send, g_recv, g_local, c_send, c_recv, e_send, e_recv, r_send, r_recv, o_sem,
@@ -277,41 +285,51 @@
             layer, q = job // per_layer, job % per_layer
             inside = jnp.logical_and(job >= 0, job < 2 * per_layer)
 
-            def run(own, dest, stride, row_of, column, number=number, job=job, layer=layer):
-                piece = Gather(
-                    place, own.at[layer], dest.at[layer], stride, row_of, lanes(column, PIECE), h, (g_send, g_recv), job
-                )
+            def run(kind, dest, stride, row_of, column, number=number, job=job, layer=layer):
+                piece = Gather(place, dest.at[layer], stride, row_of, lanes(column, PIECE), h, (g_send, g_recv), job)
+                if number == 0:
+                    first = job == layer * per_layer + (0, mix_pieces, early)[kind]
+
+                    @pl.when(first)
+                    def _():
+                        own_copy(kind, layer).wait()
+                        if kind == 0:
+                            own_copy(3, layer).wait()
+
+                    piece.scale((norm_ref, norm_ref, gated_ref)[kind].at[layer])
                 piece.stage(number)
 
             @pl.when(jnp.logical_and(inside, q < mix_pieces))
             def _():
-                run(wm_own, WM, 2 * h, lambda core: core * h, q)
+                run(0, WM, 2 * h, lambda core: core * h, q)
 
             @pl.when(jnp.logical_and(inside, jnp.logical_and(q >= mix_pieces, q < early)))
             def _():
-                run(wg_own, WG, 2 * h, lambda core: core * h, q - mix_pieces)
+                run(1, WG, 2 * h, lambda core: core * h, q - mix_pieces)
 
             @pl.when(jnp.logical_and(inside, q >= early))
             def _():
                 part = (q - early) // across
-                run(wo_own, WO, 4 * h, lambda core: core * 2 * h + part * h, (q - early) % across)
+                run(2, WO, 4 * h, lambda core: core * 2 * h + part * h, (q - early) % across)
 
     def own_copy(kind, layer):
-        own, dest = ((wm_own, WM), (wg_own, WG), (wo_own, WO))[kind]
+        own, dest, start, count = (
+            (wm_own, WM, 0, CW), (wg_own, WG, 0, DI), (wo_own, WO, 0, D), (ws_own, WM, CW, LANES)
+        )[kind]
         rows = own.shape[1]
-        start = pl.multiple_of(place.dp * rows, 8)
-        return pltpu.make_async_copy(own.at[layer], dest.at[layer, pl.ds(start, rows)], g_local.at[layer * 3 + kind])
-
+        at = pl.ds(pl.multiple_of(place.dp * rows, 8), rows)
+        target = dest.at[layer, at, pl.ds(start, count)]
+        return pltpu.make_async_copy(own.at[layer], target, g_local.at[layer * 4 + kind])
+
+    for layer in range(layers):
+        for kind in (0, 3, 1, 2):
+            own_copy(kind, layer).start()
     first_in = pltpu.make_async_copy(x_hbm, xs.at[0], o_sem.at[0])
     first_in.start()
     ext[0, 0:8, :] = jnp.zeros((8, CW), F32)
     ext[1, 0:8, :] = jnp.zeros((8, CW), F32)
     entry_barrier(place)
     tick(0)
-    for layer in range(layers):
-        for kind in range(3):
-            own_copy(kind, layer).start()
-
     def conv_copy(step_index):
         peer = (place.dp + step_index) % n_dp
         return remote(
@@ -345,8 +363,6 @@
         diag[:, 0:D] = x_all * inv
         head = head_ref[layer]
         base = done_at + 1 + layer * per_body
-        own_copy(0, layer).wait()
-
         def project_mix(i):
             ext[layer, 8 : T + 8, lanes(i, PIECE)] = mm(diag[:, 0:D], WM[layer, :, lanes(i, PIECE)])
             tick(base + i)
@@ -471,10 +487,6 @@
             def _():
                 diagonal(i)
 
-            @pl.when(i == pairs)
-            def _():
-                own_copy(1, layer).wait()
-
             @pl.when(i >= pairs)
             def _():
                 gate_proj(i - pairs)
@@ -510,7 +522,6 @@
 
         squares = lax.fori_loop(0, DI // LANES, gating, jnp.zeros((T, LANES), F32))
         inv_out = lax.rsqrt(jnp.sum(squares, axis=-1, keepdims=True) / DI + EPSILON)
-        own_copy(2, layer).wait()
         tiles(across, lambda i: tick(base + mix_pieces + 1 + items // 3 + i))
 
         def project_out(i):
@@ -546,7 +557,7 @@
     last.wait()
 
 
-def forward(x, mask, conv, head, wm, wg, wo, n_dp, n_seq, dims):
+def forward(x, mask, conv, head, norm, gated, wm, wg, wo, ws, n_dp, n_seq, dims):
     T, D, DI, CW, H, PS, N, K = dims
     any_spec = pl.BlockSpec(memory_space=pl.ANY)
     vmem = pl.BlockSpec(memory_space=pltpu.VMEM)
@@ -562,20 +573,20 @@
             sd(T, D), sd(16, CW), sd(T, D), sd(2, T, DI), sd(2, T + 8, CW), sd(2, T, LANES), sd(2, T, DI), sd(2, N, DI),
             sd(2, N, DI), sd(2, D, CX), sd(2, D, DI), sd(2, DI, D),
         ),
-        in_specs=[any_spec, vmem, vmem, vmem, any_spec, any_spec, any_spec],
+        in_specs=[any_spec] + [vmem] * 5 + [any_spec] * 4,
         out_specs=(vmem, vmem) + (any_spec,) * 10,
         scratch_shapes=[
             v(2, D, CX), v(2, D, DI), v(2, DI, D), v(3, T, D), v(2, T, DI), v(2, T + 8, CW), v(2, T, LANES),
             v(2, T, DI), v(2, N, DI), v(2, N, DI), v(n_dp, 16, CW), v(T, CW), v(T, DI), v(T, DI), v(T, DI),
             v(LANES, T), v(T, T),
-            dma((PIECES, kinds)), dma((PIECES, kinds)), dma((6,)), dma((n_dp - 1,)), dma((n_dp - 1,)), dma((2,)), dma((2,)),
+            dma((PIECES, kinds)), dma((PIECES, kinds)), dma((8,)), dma((n_dp - 1,)), dma((n_dp - 1,)), dma((2,)), dma((2,)),
             dma((2, DI // 256)), dma((2, DI // 256)), dma((19,)),
         ],
         compiler_params=pltpu.CompilerParams(
             collective_id=0, has_side_effects=True, vmem_limit_bytes=61 << 20
         ),
         name="forward",
-    )(x, mask, conv, head, wm, wg, wo)
+    )(x, mask, conv, head, norm, gated, wm, wg, wo, ws)
 
 
 def prepare(hidden, lengths, norm_gain, gate_weight, mix_weight, step_weight, conv_kernel, conv_bias, gated_gain,
@@ -586,16 +597,14 @@
     CW = shard * n_dp
     position = lax.axis_index("seq") * T + lax.iota(jnp.int32, T)
     mask = (position < lengths[0]).astype(F32)[:, None]
-    gain = norm_gain[:, :, None]
     step_pad = jnp.pad(step_weight, ((0, 0), (0, 0), (0, LANES - H)))
-    wm = jnp.concatenate([mix_weight, step_pad], axis=2) * gain
-    wg = gate_weight * gain
-    wo = out_weight * gated_gain[:, :, None]
+    norm = jnp.broadcast_to(norm_gain[:, :, None], norm_gain.shape + (LANES,))
+    gated = jnp.broadcast_to(gated_gain[:, :, None], gated_gain.shape + (LANES,))
     head = jnp.pad(jnp.stack([log_rate, step_bias, skip_gain], axis=1), ((0, 0), (0, 5), (0, LANES - H)))
     own = jnp.concatenate([conv_kernel, conv_bias[:, None, :]], axis=1)
     own = jnp.pad(own, ((0, 0), (0, 8 - own.shape[1]), (0, 0))).reshape(16, shard)
     conv = lax.dynamic_update_slice(jnp.zeros((16, CW), F32), own, (0, lax.axis_index("dp") * shard))
-    return mask, conv, head, wm, wg, wo
+    return mask, conv, head, norm, gated, step_pad
 CHUNK_N = 384
 
 
@@ -619,11 +628,15 @@
         self.total_slots = 2 * self.slots + self.conv_jobs
         self.wide = n_dp == 4 and self.n_z == 4 and self.h % 32 == 0
         self.rounds = self.n_z.bit_length() - 1
-        self.offsets = (0, 1, 2, 4, 6, 9, 12, 15, 18, 19)
+        self.offsets = (0, 1, 1, 4, 6, 8, 10, 12, 15, 16)
         self.o_ring = self.offsets[4] + 1
         self.f_ring = max(self.offsets) + 1
-        self.r_ring = (self.jobs + 1) // 2
+        self.r_ring = self.offsets[4] - self.offsets[2] + 2
+        self.z_ring = self.offsets[8] - self.offsets[4] + 1
+        self.half_ring = self.offsets[7] - self.offsets[5] + 2
+        self.w_ring = self.offsets[8] - self.offsets[7] + 1
         self.s_ring = self.offsets[2] + 1
+        self.in_ring = self.offsets[2] + 2
         self.kinds = 12 if self.wide else n_dp - 1 + self.rounds + 2
         self.sibling_kind = self.kinds - 1
 
@@ -643,7 +656,7 @@
 class Reducer:
     def __init__(self, place, plan, refs, outs):
         self.p, self.plan = place, plan
-        self.S, self.O, self.R, self.rx, self.ry, self.r2x, self.r2y, self.z1, self.z2, self.G, self.F, self.send, self.recv, self.loc, self.fin = refs
+        self.S, self.O, self.R, self.rx, self.ry, self.r2x, self.r2y, self.z1, self.z2, self.G, self.F, self.W, self.gains, self.sums, self.weights, self.send, self.recv, self.loc, self.fin, self.wsem = refs
         self.outs = outs
 
     def copy(self, job, kind, src, dst, dp, seq):
@@ -667,17 +680,17 @@
     def to_sibling(self, job):
         ring = lax.rem(job, self.plan.s_ring)
         kind = self.plan.kinds - 2
-        return self.copy(job, kind, self.S.at[ring], self.R.at[job], self.p.dp, self.p.sib)
+        into = lax.rem(job, self.plan.in_ring)
+        return self.copy(job, kind, self.S.at[ring], self.R.at[into], self.p.dp, self.p.sib)
 
     def slot(self, job):
         return lax.rem(job, self.plan.r_ring)
 
-    def load(self, job):
-        ring = lax.rem(job, self.plan.s_ring)
-        return pltpu.make_async_copy(self.R.at[job], self.S.at[ring], self.loc.at[ring])
-
-    def z_peer(self, step):
-        return lax.rem(self.p.z + step, self.plan.n_z) * 2 + self.p.core
+    def z_slot(self, job):
+        return lax.rem(job, self.plan.z_ring)
+
+    def half_slot(self, job):
+        return lax.rem(job, self.plan.half_ring)
 
     def xy(self, job, kind):
         p, half = self.p, self.plan.h // 2
@@ -692,27 +705,30 @@
         }[kind]()
 
     def keep(self):
-        return self.p.parity * (self.plan.h // 2)
-
-    def quarter(self):
-        return self.keep() + (self.p.z // 2) * (self.plan.h // 4)
+        return (self.p.z - 1) * (self.plan.h // 2)
 
     def zed(self, job, kind):
         p, h = self.p, self.plan.h
+        across = (self.plan.n_z - 1 - p.z) * 2 + p.core
         if kind == 6:
-            return self.copy(job, 6, self.summed(job, (1 - p.parity) * (h // 2), h // 2), self.z1.at[self.slot(job)], p.dp, p.pair)
+            return self.copy(job, 6, self.summed(job, 0, h), self.z1.at[self.z_slot(job)], p.dp, p.pair)
         if kind == 7:
-            start = self.keep() + (1 - p.z // 2) * (h // 4)
-            return self.copy(job, 7, self.summed(job, start, h // 4), self.z2.at[self.slot(job)], p.dp, self.z_peer(2))
+            start = (2 - p.z) * (h // 2)
+            return self.copy(job, 7, self.summed(job, start, h // 2), self.z2.at[self.half_slot(job)], p.dp, across)
         if kind == 8:
-            part = self.whole(job, self.quarter(), h // 4)
-            return self.copy(job, 8, part, part, p.dp, self.z_peer(2))
-        part = self.whole(job, self.keep(), h // 2)
+            part = self.whole(job, self.keep(), h // 2)
+            return self.copy(job, 8, part, part, p.dp, across)
+        part = self.whole(job, 0, h)
         return self.copy(job, 9, part, part, p.dp, p.pair)
+
+    def inner(self):
+        return jnp.logical_and(self.p.z > 0, self.p.z < self.plan.n_z - 1)
 
     def whole(self, job, start, count):
         ring = lax.rem(job, self.plan.f_ring)
-        return self.F.at[ring, pl.ds(pl.multiple_of(start, 8), count)]
+        if not isinstance(start, int):
+            start = pl.multiple_of(start, 8)
+        return self.F.at[ring, pl.ds(start, count)]
 
     def direct(self, job, step):
         p, h = self.p, self.plan.h
@@ -724,7 +740,7 @@
         bit = (p.z // (1 << rnd)) % 2
         peer = (p.z + (1 << rnd) - 2 * bit * (1 << rnd)) * 2 + p.core
         kind = p.n_dp - 1 + rnd
-        return self.copy(job, kind, self.summed(job, 0, h), self.z1.at[self.slot(job), rnd], p.dp, peer)
+        return self.copy(job, kind, self.summed(job, 0, h), self.z1.at[self.z_slot(job), rnd], p.dp, peer)
 
     def add(self, dst, src):
         dst[...] = dst[...] + src[...]
@@ -736,17 +752,16 @@
         if number == 0:
             self.to_sibling(job).start()
         elif number == 1:
+            return
+        elif number == 2:
             copy = self.to_sibling(job)
             copy.wait_recv()
             copy.wait_send()
-            self.load(job).start()
-        elif number == 2:
-            self.load(job).wait()
-            ring = lax.rem(job, plan.s_ring)
+            ring = lax.rem(job, plan.in_ring)
             o_ring = lax.rem(job, plan.o_ring)
 
             def add_owner(o):
-                self.O[o_ring, o] = self.O[o_ring, o] + self.S[ring, o]
+                self.O[o_ring, o] = self.O[o_ring, o] + self.R[ring, o]
 
             tiles(plan.n_dp, add_owner)
             if plan.wide:
@@ -775,7 +790,11 @@
                 self.summed(job, 0, half)[...] = self.mine(job, 0, half)[...] + self.r2y[self.slot(job)]
                 self.xy(job, 5).wait_recv()
                 self.summed(job, half, half)[...] = self.mine(job, half, half)[...] + self.r2x[self.slot(job)]
-                self.zed(job, 6).start()
+
+                @pl.when(jnp.logical_not(self.inner()))
+                def _():
+                    self.zed(job, 6).start()
+
                 for kind in range(6):
                     self.xy(job, kind).wait_send()
             else:
@@ -786,35 +805,56 @@
                     self.butterfly(job, 0).start()
         elif number == 5:
             if plan.wide:
-                self.zed(job, 6).wait_recv()
-                self.add(self.summed(job, self.keep(), half), self.z1.at[self.slot(job)])
-                self.zed(job, 7).start()
+
+                @pl.when(self.inner())
+                def _():
+                    self.zed(job, 6).wait_recv()
+                    self.add(self.summed(job, 0, h), self.z1.at[self.z_slot(job)])
+                    self.zed(job, 7).start()
+
             else:
                 self.exchange(job, 0)
         elif number == 6:
             if plan.wide:
-                self.zed(job, 7).wait_recv()
-                total = self.summed(job, self.quarter(), h // 4)
-                self.whole(job, self.quarter(), h // 4)[...] = total[...] + self.z2[self.slot(job)]
-                self.zed(job, 8).start()
+
+                @pl.when(self.inner())
+                def _():
+                    self.zed(job, 7).wait_recv()
+                    part = self.summed(job, self.keep(), half)[...] + self.z2[self.half_slot(job)]
+                    self.whole(job, self.keep(), half)[...] = part
+                    self.zed(job, 8).start()
+
             else:
                 self.exchange(job, 1)
         elif number == 7:
+            self.weight(job, "start")
             if plan.wide:
-                self.zed(job, 8).wait_recv()
-                self.zed(job, 9).start()
+
+                @pl.when(self.inner())
+                def _():
+                    self.zed(job, 8).wait_recv()
+                    self.zed(job, 9).start()
+
         elif number == 8:
             if plan.wide:
-                self.zed(job, 9).wait_recv()
+
+                @pl.when(self.inner())
+                def _():
+                    for kind in (7, 8, 9):
+                        self.zed(job, kind).wait_send()
+
+                @pl.when(jnp.logical_not(self.inner()))
+                def _():
+                    self.zed(job, 9).wait_recv()
+                    self.zed(job, 6).wait_send()
+
             else:
                 for rnd in range(2, max(plan.rounds, 3)):
                     self.exchange(job, rnd)
+            self.scale(job)
             self.final(job, "start")
         else:
             self.final(job, "wait")
-            if plan.wide:
-                for kind in range(6, 10):
-                    self.zed(job, kind).wait_send()
 
     def exchange(self, job, rnd):
         if rnd >= self.plan.rounds:
@@ -822,59 +862,126 @@
         copy = self.butterfly(job, rnd)
         copy.wait_recv()
         copy.wait_send()
-        self.add(self.summed(job, 0, self.plan.h), self.z1.at[self.slot(job), rnd])
+        self.add(self.summed(job, 0, self.plan.h), self.z1.at[self.z_slot(job), rnd])
         if rnd + 1 < self.plan.rounds:
             self.butterfly(job, rnd + 1).start()
+
+    def kind_of(self, job):
+        plan = self.plan
+        second = job >= plan.per_layer
+        q = job - jnp.where(second, plan.per_layer, 0)
+        normal = job < 2 * plan.per_layer
+        layer = jnp.where(second, 0, 1)
+        is_out = jnp.logical_and(normal, q < plan.out_jobs)
+        is_gate = jnp.logical_and(normal, jnp.logical_and(q >= plan.out_jobs, q < plan.early))
+        is_mix = jnp.logical_and(normal, q >= plan.early)
+        return layer, q, normal, is_out, is_gate, is_mix
+
+    def total(self, job):
+        return self.whole(job, 0, self.plan.h) if self.plan.wide else self.summed(job, 0, self.plan.h)
+
+    def weight(self, job, what):
+        plan, p = self.plan, self.p
+        h = plan.h
+        layer, q, normal, is_out, is_gate, is_mix = self.kind_of(job)
+        wm, wg, wo = self.weights
+        slot = lax.rem(job, plan.w_ring)
+        per_row = plan.out_jobs // 2
+
+        def go_for(source, row, column):
+            at = (layer, pl.ds(pl.multiple_of(row, 8), h), lanes(column, CHUNK_N))
+            copy = pltpu.make_async_copy(source.at[at], self.W.at[slot], self.wsem.at[slot])
+            getattr(copy, what)()
+
+        pl.when(is_out)(
+            lambda: go_for(wo, p.dp * 4 * h + p.core * 2 * h + (q // per_row) * h, lax.rem(q, per_row))
+        )
+        pl.when(is_gate)(lambda: go_for(wg, p.dp * 2 * h + p.core * h, q - plan.out_jobs))
+        pl.when(is_mix)(lambda: go_for(wm, p.dp * 2 * h + p.core * h, q - plan.early))
+
+    def scale(self, job):
+        plan, p = self.plan, self.p
+        h = plan.h
+        layer, q, normal, is_out, is_gate, is_mix = self.kind_of(job)
+        norm, gated = self.gains
+        norm_sum, gated_sum = self.sums
+        slot = lax.rem(job, plan.w_ring)
+        total = self.total(job)
+        self.weight(job, "wait")
+
+        def apply(sums, gain):
+            value = total[...]
+            product = value * self.W[slot]
+            lane_sum = product[:, 0:LANES]
+            for part in range(1, CHUNK_N // LANES):
+                lane_sum = lane_sum + product[:, part * LANES : (part + 1) * LANES]
+            sums[...] = sums[...] + lane_sum
+            total[...] = value * jnp.concatenate([gain[...]] * (CHUNK_N // LANES), axis=1)
+
+        @pl.when(is_out)
+        def _():
+            part = q // (plan.out_jobs // 2)
+            rows = pl.ds(pl.multiple_of(p.core * 2 * h + part * h, 8), h)
+            apply(gated_sum.at[layer, pl.ds(pl.multiple_of(part * h, 8), h)], gated.at[layer, rows])
+
+        @pl.when(jnp.logical_or(is_gate, is_mix))
+        def _():
+            apply(norm_sum.at[layer], norm.at[layer, pl.ds(pl.multiple_of(p.core * h, 8), h)])
 
     def final(self, job, what):
         plan, p = self.plan, self.p
         h = plan.h
-        gm, gg, go, gc = self.outs
-        layer = 1 - job // plan.per_layer
-        q = lax.rem(job, plan.per_layer)
-        normal = job < 2 * plan.per_layer
-        src = self.whole(job, 0, h) if plan.wide else self.summed(job, 0, h)
+        gm, gs, gg, go, gc = self.outs
+        layer, q, normal, is_out, is_gate, is_mix = self.kind_of(job)
+        src = self.total(job)
+        per_row = plan.out_jobs // 2
+        last = plan.mix_jobs - 1
+        edge = gm.shape[2] - last * CHUNK_N
+        ring = lax.rem(job, plan.f_ring)
+        extra = plan.kinds
+
+        def rows(start):
+            return pl.ds(pl.multiple_of(start, 8), h)
 
         def put(core):
-            def rows(start):
-                return pl.ds(pl.multiple_of(start, 8), h)
-
-            per_row = plan.out_jobs // 2
+            at = rows(core * h)
             return (
+                (is_out, lambda: [(None, go.at[layer, rows(core * 2 * h + (q // per_row) * h), lanes(lax.rem(q, per_row), CHUNK_N)])]),
+                (is_gate, lambda: [(None, gg.at[layer, at, lanes(q - plan.out_jobs, CHUNK_N)])]),
                 (
-                    jnp.logical_and(normal, q < plan.out_jobs),
-                    lambda: go.at[layer, rows(core * 2 * h + (q // per_row) * h), lanes(lax.rem(q, per_row), CHUNK_N)],
+                    jnp.logical_and(is_mix, q - plan.early < last),
+                    lambda: [(None, gm.at[layer, at, lanes(q - plan.early, CHUNK_N)])],
                 ),
                 (
-                    jnp.logical_and(normal, jnp.logical_and(q >= plan.out_jobs, q < plan.early)),
-                    lambda: gg.at[layer, rows(core * h), lanes(q - plan.out_jobs, CHUNK_N)],
+                    jnp.logical_and(is_mix, q - plan.early == last),
+                    lambda: [
+                        ((0, edge), gm.at[layer, at, pl.ds(last * CHUNK_N, edge)]),
+                        ((edge, CHUNK_N - edge), gs.at[layer, at]),
+                    ],
                 ),
-                (
-                    jnp.logical_and(normal, q >= plan.early),
-                    lambda: gm.at[layer, rows(core * h), lanes(q - plan.early, CHUNK_N)],
-                ),
-                (jnp.logical_not(normal), lambda: gc.at[job - 2 * plan.per_layer, core]),
+                (jnp.logical_not(normal), lambda: [(None, gc.at[job - 2 * plan.per_layer, core])]),
             )
 
         def go_for(make, which):
-            local = pltpu.make_async_copy(src, make(), self.fin.at[lax.rem(job, plan.f_ring)])
-            away = self.copy(job, plan.sibling_kind, src, make(), p.dp, p.sib)
-            if which == "start":
-                local.start()
-                away.start()
-            else:
-                local.wait()
-                away.wait_send()
+            for number, (columns, target) in enumerate(make()):
+                part = src if columns is None else src.at[:, pl.ds(*columns)]
+                kind = plan.sibling_kind if number == 0 else extra
+                local = pltpu.make_async_copy(part, target, self.fin.at[number, ring])
+                away = self.copy(job, kind, part, target, p.dp, p.sib)
+                if which == "start":
+                    local.start()
+                    away.start()
+                elif which == "wait":
+                    local.wait()
+                    away.wait_send()
+                else:
+                    away.wait_recv()
 
         for when, make in put(p.core):
             pl.when(when)(functools.partial(go_for, make, what))
         if what == "wait":
             for when, make in put(1 - p.core):
-
-                def arrived(make=make):
-                    self.copy(job, plan.sibling_kind, src, make(), p.dp, p.sib).wait_recv()
-
-                pl.when(when)(arrived)
+                pl.when(when)(functools.partial(go_for, make, "arrived"))
 
     def tick(self, t):
         for number in reversed(range(len(self.plan.offsets))):
@@ -889,19 +996,27 @@
     T, D, DI, CW, H, PS, N, K = dims
     plan = Plan(n_dp, n_seq, dims)
     (
-        cot_ref, mask_ref, conv_ref, head_ref, x0_hbm, x1_hbm, gate_hbm, ext_hbm, step_hbm, mo_hbm, sin_hbm,
+        cot_ref, mask_ref, conv_ref, head_ref, norm_ref, gated_ref, x0_hbm, x1_hbm, gate_hbm, ext_hbm, step_hbm, mo_hbm, sin_hbm,
         sout_hbm, wm_hbm, wg_hbm, wo_hbm,
-        hg_ref, gm, gg, go, gc, R,
+        hg_ref, gm, gs, gg, go, gc, norm_out, gated_out,
         grad, x, gate, ext, step, mo, sin, sout, wrow, wcol, U, V, mixed, ldE, dtE, ldT, gmT, dgT, PG, raw, nT, gnT,
         NG, dS, dSin, maps, heads, convg, rows,
-        S, O, rx, ry, r2x, r2y, z1, z2, G, F, edge_in,
-        j_send, j_recv, s_loc, f_loc, l_sem, w_sem, v_sem, e_send, e_recv, r_send, r_recv,
+        S, R, O, rx, ry, r2x, r2y, z1, z2, G, F, edge_in, W, norm_sum, gated_sum,
+        j_send, j_recv, s_loc, f_loc, wt_sem, gain_sem, l_sem, w_sem, v_sem, e_send, e_recv, r_send, r_recv,
     ) = refs
     place = Place(n_dp, n_seq)
     h = plan.h
     red = Reducer(
-        place, plan, (S, O, R, rx, ry, r2x, r2y, z1, z2, G, F, j_send, j_recv, s_loc, f_loc), (gm, gg, go, gc)
+        place,
+        plan,
+        (
+            S, O, R, rx, ry, r2x, r2y, z1, z2, G, F, W, (norm_ref, gated_ref), (norm_sum, gated_sum),
+            (wm_hbm, wg_hbm, wo_hbm), j_send, j_recv, s_loc, f_loc, wt_sem,
+        ),
+        (gm, gs, gg, go, gc),
     )
+    norm_sum[...] = jnp.zeros(norm_sum.shape, F32)
+    gated_sum[...] = jnp.zeros(gated_sum.shape, F32)
     CX = CW + LANES
     CHUNK = 256
     chunks = DI // CHUNK
@@ -1160,9 +1275,50 @@
         heads[...] = jnp.zeros((2, T, LANES), F32)
         rows[...] = jnp.zeros((8, LANES), F32)
 
-        def back_heads(i):
-            at = lanes(i, 256)
-            select = head_matrix(LANES, 256, PS, i * 256)
+        groups = DI // CHUNK_N
+        late = base + plan.lead + plan.early + plan.bubbles
+
+        def conv_back(at, width, upstream):
+            taps, total = conv_value(at)
+            sig = sigmoid(total)
+            pre = upstream * (sig * (1.0 + total * (1.0 - sig)))
+            PG[0:T, at] = pre
+            parts = [jnp.sum(pre * ext[8 - K + 1 + k : 8 - K + 1 + k + T, at], axis=0, keepdims=True) for k in range(K)]
+            parts.append(jnp.sum(pre, axis=0, keepdims=True))
+            parts.append(jnp.zeros((8 - K - 1, width), F32))
+            convg[li, :, at] = jnp.concatenate(parts, axis=0)
+
+        def edge_copy(number, at):
+            return remote(
+                PG.at[pl.ds(0, 8), at], edge_in.at[li, :, at], e_send.at[li, number], e_recv.at[li, number],
+                place.dp, place.seq - 1,
+            )
+
+        def raw_back(number, at):
+            @pl.when(place.seq < n_seq - 1)
+            def _():
+                edge_copy(number, at).wait_recv()
+                PG[T : T + 8, at] = edge_in[li, :, at]
+
+            taps = conv_ref[pl.ds(pl.multiple_of(layer * 8, 8), 8), at]
+            total = taps[K - 1 : K, :] * PG[0:T, at]
+            for k in range(K - 1):
+                total = total + taps[k : k + 1, :] * PG[K - 1 - k : K - 1 - k + T, at]
+            raw[:, at] = total
+
+        def mix_piece(number):
+            produce(
+                first_job + plan.early + number, nT, 2 * h, lambda target: target * h, raw[:, lanes(number, CHUNK_N)]
+            )
+            red.tick(late + number)
+            mix_stream(number)
+
+        def back_mix(i, slot):
+            NG[...] = NG[...] + mm(raw[:, lanes(i, CHUNK_N)], wcol[slot], NT)
+
+        def back_group(g):
+            at = lanes(g, CHUNK_N)
+            select = head_matrix(LANES, CHUNK_N, PS, g * CHUNK_N)
             select32 = select.astype(F32)
             l_tile = ldE[:, at]
             heads_in = mixed[:, at]
@@ -1178,43 +1334,36 @@
             heads[1] = heads[1] + mm(scaled_grad * heads_in, select32, NT)
             skip_sum = jnp.sum(out_grad * heads_in, axis=0, keepdims=True)
             end_sum = jnp.sum(dS[li, :, at] * sout[:, at], axis=0, keepdims=True)
-            both = jnp.concatenate([skip_sum, end_sum, jnp.zeros((6, 256), F32)], axis=0)
+            both = jnp.concatenate([skip_sum, end_sum, jnp.zeros((6, CHUNK_N), F32)], axis=0)
             rows[...] = rows[...] + mm(both, select32, NT)
-            U[:, at] = skip * out_grad + scaled_grad * dt_tile
-
-        tiles(DI // 256, back_heads)
-        red.tick(base + plan.lead + plan.early + plan.bubbles - 1)
+            conv_back(at, CHUNK_N, skip * out_grad + scaled_grad * dt_tile)
+
+            @pl.when(place.seq > 0)
+            def _():
+                edge_copy(g, at).start()
+
+            @pl.when(g == 0)
+            def _():
+                red.tick(late - 1)
+
+            @pl.when(g > 0)
+            def _():
+                raw_back(g - 1, lanes(g - 1, CHUNK_N))
+                mix_piece(g - 1)
+
+        tiles(groups, back_group)
+        map_lanes = pl.ds(DI, CW - DI)
+        conv_back(map_lanes, CW - DI, maps[...])
+
+        @pl.when(place.seq > 0)
+        def _():
+            edge_copy(groups, map_lanes).start()
+
         last_row = iota((T, LANES), 0) == T - 1
         decay_grad = heads[0] + jnp.where(last_row, rows[1:2, :], 0.0)
         rate_grad = exact(tri(T).astype(jnp.bfloat16), decay_grad, TN)
         step_grad = heads[1] - jnp.exp(head[0:1, :]) * rate_grad
         raw[:, CW:CX] = step_grad * sigmoid(raw_step + head[1:2, :])
-
-        def back_conv(i):
-            at = lanes(i, 256)
-            taps, total = conv_value(at)
-            sig = sigmoid(total)
-            slope = sig * (1.0 + total * (1.0 - sig))
-
-            def finish(upstream):
-                pre = upstream * slope
-                PG[0:T, at] = pre
-                parts = [
-                    jnp.sum(pre * ext[8 - K + 1 + k : 8 - K + 1 + k + T, at], axis=0, keepdims=True) for k in range(K)
-                ]
-                parts.append(jnp.sum(pre, axis=0, keepdims=True))
-                parts.append(jnp.zeros((8 - K - 1, 256), F32))
-                convg[li, :, at] = jnp.concatenate(parts, axis=0)
-
-            @pl.when(i < DI // 256)
-            def _():
-                finish(U[:, lanes(jnp.minimum(i, DI // 256 - 1), 256)])
-
-            @pl.when(i >= DI // 256)
-            def _():
-                finish(maps[...])
-
-        tiles(CW // 256, back_conv)
         convg[li, :, CW:CX] = jnp.where(iota((8, LANES), 0) == 0, rows[0:1, :], 0.0)
 
         @pl.when(li == 0)
@@ -1222,44 +1371,25 @@
             for k in range(6):
                 load_of(0, k).start()
 
-        edge = remote(
-            PG.at[pl.ds(0, 8)], edge_in.at[li], e_send.at[li], e_recv.at[li], place.dp, place.seq - 1
-        )
+        def last_pieces(g):
+            @pl.when(g == groups - 1)
+            def _():
+                raw_back(g, lanes(groups - 1, CHUNK_N))
+
+            @pl.when(g == groups)
+            def _():
+                raw_back(g, map_lanes)
+
+            mix_piece(g)
+
+        lax.fori_loop(groups - 1, groups + 1, lambda g, c: (last_pieces(g), c)[1], 0)
+        inner = jnp.sum(NG[...] * x[...], axis=-1, keepdims=True) / D
+        grad[...] = grad[...] + inv_in * NG[...] - x[...] * (inner * (inv_in * inv_in * inv_in))
 
         @pl.when(place.seq > 0)
         def _():
-            edge.start()
-
-        @pl.when(place.seq < n_seq - 1)
-        def _():
-            edge.wait_recv()
-            PG[T : T + 8, :] = edge_in[li]
-
-        def back_raw(i):
-            at = lanes(i, 256)
-            taps = conv_ref[pl.ds(pl.multiple_of(layer * 8, 8), 8), at]
-            total = taps[K - 1 : K, :] * PG[0:T, at]
-            for k in range(K - 1):
-                total = total + taps[k : k + 1, :] * PG[K - 1 - k : K - 1 - k + T, at]
-            raw[:, at] = total
-
-        tiles(CW // 256, back_raw)
-
-        def mix_job(i):
-            produce(first_job + plan.early + i, nT, 2 * h, lambda target: target * h, raw[:, lanes(i, CHUNK_N)])
-            red.tick(base + plan.lead + plan.early + plan.bubbles + i)
-
-        def back_mix(i, slot):
-            mix_job(i)
-            NG[...] = NG[...] + mm(raw[:, lanes(i, CHUNK_N)], wcol[slot], NT)
-
-        tiles(plan.mix_jobs, mix_stream)
-        inner = jnp.sum(NG[...] * x[...], axis=-1, keepdims=True) / D
-        grad[...] = grad[...] + inv_in * NG[...] - x[...] * (inner * (inv_in * inv_in * inv_in))
-
-        @pl.when(place.seq > 0)
-        def _():
-            edge.wait_send()
+            tiles(groups, lambda g: edge_copy(g, lanes(g, CHUNK_N)).wait_send())
+            edge_copy(groups, map_lanes).wait_send()
             tiles(chunks, lambda c: relay_copy(c).wait_send())
 
         return carry
@@ -1283,8 +1413,21 @@
         red.tick(base + e)
     tiles(max(plan.offsets), lambda i: red.tick(base + plan.conv_jobs + i))
 
-
-def backward(cot, mask, conv, head, saved, n_dp, n_seq, dims):
+    copies = []
+    for number, (sums, out) in enumerate(((norm_sum, norm_out), (gated_sum, gated_out))):
+        local = pltpu.make_async_copy(sums, out.at[place.core], gain_sem.at[number])
+        away = remote(sums, out.at[place.core], gain_sem.at[2 + number], gain_sem.at[4 + number], place.dp, place.sib)
+        back = remote(sums, out.at[1 - place.core], gain_sem.at[2 + number], gain_sem.at[4 + number], place.dp, place.sib)
+        local.start()
+        away.start()
+        copies.append((local, away, back))
+    for local, away, back in copies:
+        local.wait()
+        away.wait_send()
+        back.wait_recv()
+
+
+def backward(cot, mask, conv, head, norm, gated, saved, n_dp, n_seq, dims):
     T, D, DI, CW, H, PS, N, K = dims
     plan = Plan(n_dp, n_seq, dims)
     any_spec = pl.BlockSpec(memory_space=pl.ANY)
@@ -1296,33 +1439,34 @@
     dma = pltpu.SemaphoreType.DMA
     if plan.wide:
         received = [v(ring, 2, h // 2, CHUNK_N), v(ring, 2, h // 2, CHUNK_N), v(ring, h // 2, CHUNK_N),
-                    v(ring, h // 2, CHUNK_N), v(ring, h // 2, CHUNK_N), v(ring, h // 4, CHUNK_N)]
+                    v(ring, h // 2, CHUNK_N), v(plan.z_ring, h, CHUNK_N), v(plan.half_ring, h // 2, CHUNK_N)]
     else:
         none = v(8, LANES)
-        received = [v(ring, n_dp - 1, h, CHUNK_N), none, none, none, v(ring, max(plan.rounds, 1), h, CHUNK_N), none]
+        received = [v(ring, n_dp - 1, h, CHUNK_N), none, none, none, v(plan.z_ring, max(plan.rounds, 1), h, CHUNK_N), none]
     return pl.pallas_call(
         functools.partial(backward_kernel, n_dp, n_seq, dims),
         out_shape=(
-            sd(T, D), sd(2, 2 * h, CX), sd(2, 2 * h, DI), sd(2, 4 * h, D), sd(plan.conv_jobs, 2, h, CHUNK_N),
-            sd(J, n_dp, h, CHUNK_N),
+            sd(T, D), sd(2, 2 * h, CW), sd(2, 2 * h, LANES), sd(2, 2 * h, DI), sd(2, 4 * h, D),
+            sd(plan.conv_jobs, 2, h, CHUNK_N), sd(2, 2, h, LANES), sd(2, 2, 2 * h, LANES),
         ),
-        in_specs=[vmem] * 4 + [any_spec] * 11,
-        out_specs=(vmem,) + (any_spec,) * 5,
+        in_specs=[vmem] * 6 + [any_spec] * 11,
+        out_specs=(vmem,) + (any_spec,) * 7,
         scratch_shapes=[
             v(T, D), v(T, D), v(T, DI), v(T + 8, CW), v(T, LANES), v(T, DI), v(N, DI), v(N, DI),
             v(DI, D), v(3, D, CHUNK_N), v(T, DI), v(T, DI), v(T, CW), v(T, DI), v(T, DI), v(LANES, T), v(T, T),
             v(T, T), v(T + 8, CW), v(T, CX), v(D, T), v(DI, T), v(T, D), v(2, N, DI), v(N, DI), v(T, 2 * N),
             v(2, T, LANES), v(2, 8, CX), v(8, LANES),
-            v(plan.s_ring, n_dp, h, CHUNK_N), v(plan.o_ring, n_dp, h, CHUNK_N), *received,
+            v(plan.s_ring, n_dp, h, CHUNK_N), v(plan.in_ring, n_dp, h, CHUNK_N), v(plan.o_ring, n_dp, h, CHUNK_N), *received,
             v(plan.f_ring, h, CHUNK_N), v(plan.f_ring, h, CHUNK_N) if plan.wide else v(8, LANES), v(2, 8, CW),
-            dma((J, plan.kinds + 1)), dma((J, plan.kinds + 1)), dma((plan.s_ring,)), dma((plan.f_ring,)), dma((8,)),
-            dma((3,)), dma((2,)), dma((2,)), dma((2,)), dma((2, DI // 256)), dma((2, DI // 256)),
+            v(plan.w_ring, h, CHUNK_N), v(2, h, LANES), v(2, 2 * h, LANES),
+            dma((J, plan.kinds + 1)), dma((J, plan.kinds + 1)), dma((plan.s_ring,)), dma((2, plan.f_ring)), dma((plan.w_ring,)), dma((6,)), dma((8,)),
+            dma((3,)), dma((2,)), dma((2, DI // CHUNK_N + 1)), dma((2, DI // CHUNK_N + 1)), dma((2, DI // 256)), dma((2, DI // 256)),
         ],
         compiler_params=pltpu.CompilerParams(
             collective_id=1, has_side_effects=True, vmem_limit_bytes=61 << 20
         ),
         name="backward",
-    )(cot, mask, conv, head, *saved)
+    )(cot, mask, conv, head, norm, gated, *saved)
 
 
 def on_device(hidden, cotangent, lengths, norm_gain, gate_weight, mix_weight, step_weight, conv_kernel, conv_bias,
@@ -1332,32 +1476,27 @@
     DI, CW, H, K = gate_weight.shape[2], mix_weight.shape[2], skip_gain.shape[1], conv_kernel.shape[1]
     dims = (T, D, DI, CW, H, DI // H, (CW - DI) // 2, K)
     plan = Plan(n_dp, n_seq, dims)
-    mask, conv, head, wm, wg, wo = prepare(
+    mask, conv, head, norm, gated, step_pad = prepare(
         hidden, lengths, norm_gain, gate_weight, mix_weight, step_weight, conv_kernel, conv_bias, gated_gain,
         out_weight, skip_gain, log_rate, step_bias, n_dp,
     )
     x = hidden[0]
-    result, conv_full, *saved = forward(x, mask, conv, head, wm, wg, wo, n_dp, n_seq, dims)
-    hidden_grad, gm, gg, go, gc, _ = backward(
-        cotangent[0], mask, conv_full, head, (x, *saved), n_dp, n_seq, dims
+    result, conv_full, *saved = forward(
+        x, mask, conv, head, norm, gated, mix_weight, gate_weight, out_weight, step_pad, n_dp, n_seq, dims
     )
-    gain = norm_gain[:, :, None]
-    mix_grad = gm[:, :, :CW]
-    step_grad = gm[:, :, CW : CW + H]
-    norm_gain_grad = (
-        jnp.sum(mix_grad * mix_weight, axis=2)
-        + jnp.sum(gg * gate_weight, axis=2)
-        + jnp.sum(step_grad * step_weight, axis=2)
+    hidden_grad, gm, gs, gg, go, gc, norm_sum, gated_sum = backward(
+        cotangent[0], mask, conv_full, head, norm, gated, (x, *saved), n_dp, n_seq, dims
     )
-    gated_gain_grad = jnp.sum(go * out_weight, axis=2)
+    norm_gain_grad = jnp.sum(norm_sum, axis=-1).transpose(1, 0, 2).reshape(norm_gain.shape) / norm_gain
+    gated_gain_grad = jnp.sum(gated_sum, axis=-1).transpose(1, 0, 2).reshape(gated_gain.shape) / gated_gain
     blocks = gc[:, 0].reshape(-1, 8, CHUNK_N)[: plan.blocks]
     blocks = blocks.reshape(2, plan.mix_jobs, 8, CHUNK_N).transpose(0, 2, 1, 3).reshape(2, 8, CW + LANES)[::-1]
     shard = conv_bias.shape[1]
     own = lax.dynamic_slice(blocks, (0, 0, lax.axis_index("dp") * shard), (2, 8, shard))
     skip_grad = blocks[:, 0, CW : CW + H]
     return (
-        result[None], hidden_grad[None], norm_gain_grad, gg * gain, mix_grad * gain, step_grad * gain, own[:, :K],
-        own[:, K], gated_gain_grad, go * gated_gain[:, :, None], skip_grad,
+        result[None], hidden_grad[None], norm_gain_grad, gg, gm, gs[:, :, :H], own[:, :K], own[:, K],
+        gated_gain_grad, go, skip_grad,
     )
 
 

time: 401 us -> 384 us (0.958)
  other arithmetic: 23.4 us -> 6.34 us
  Pallas kernels: 367 us -> 355 us
  local copies, waits for them, and re-layouts: 8.42 us -> 20.2 us
    mul x7 -> x0, other arithmetic: 20.1 us -> none  [the longest x1 4.23 us: on_device(): gg * gain]
    pallas_call x1, Pallas kernels: 225 us -> 213 us  [backward(): pl.pallas_call(functools.partial(backward_kernel, n_dp, n_seq, dims), out...]
    unnamed x21 -> x22, local copies, waits for them, and re-layouts: 5 us -> 12.8 us
where the time goes in v3:
time: 384 us; the launch traced here: 383 us
  Pallas kernels  355 us (92%)
  local copies, waits for them, and re-layouts  20.2 us (5%)
  other arithmetic  6.34 us (2%)
    pallas_call x1, Pallas kernels, backward(): pl.pallas_call(functools.partial(backward_kernel, n_dp, n_seq, dims), out...  213 us
    pallas_call x1, Pallas kernels, forward(): pl.pallas_call(functools.partial(forward_kernel, n_dp, n_seq, dims), out_...  143 us
    unnamed x22, local copies, waits for them, and re-layouts  12.8 us

profile of v3, /device:TPU:0, one launch (start us, length us, event | category | flops | bytes accessed | tf_op | source)
XLA Modules:
  0.0 383.1 jit_solution(9780837600849485050)
XLA Ops:
  1.3 0.7 copy.45
  2.0 1.3 select_maximum_fusion.1.refs_3_
  3.3 0.7 fusion.1
  4.1 0.5 dynamic_update_slice.3.refs_2_
  4.5 0.0 copy-start.4
  4.5 0.7 fusion.refs_1_
  5.2 1.5 broadcast_in_dim.27.refs_4_
  6.7 0.9 copy.49
  7.6 0.7 pad.14.refs_9_
  8.3 1.6 broadcast_in_dim.28.refs_5_
  9.9 0.0 copy-done.4
  9.9 142.7 %forward.1 = (f32[256,768]{1,0:T(8,128)}, f32[16,1792]{1,0:T(8,128)}, f32[256,768]{1,0:T(8,128)}, f32[2,256,1536]{2,1,0:T(8,128)}, f32[2,264,1792]{2,1,0:T(8,128...) custom-call(f32[256,768]{1,0:T(8,128)} %bitcast.30, ...), custom_call_target="tpu_custom_call" | custom-call | tf_op jit(solution)/shard_map/forward/pallas_call | solution.py:570
  152.6 0.0 copy-start.5
  152.6 0.0 copy-start.6
  152.6 0.0 copy-start.3
  152.6 212.5 %backward.1 = (f32[256,768]{1,0:T(8,128)}, f32[2,192,1792]{2,1,0:T(8,128)}, f32[2,192,128]{2,1,0:T(8,128)}, f32[2,192,1536]{2,1,0:T(8,128)}, f32[2,384,768]{2,1,...) custom-call(f32[256,768]{1,0:T(8,128)} %bitcast.34, ...), custom_call_target="tpu_custom_call" | custom-call | tf_op jit(solution)/shard_map/backward/pallas_call | solution.py:1446
  365.2 0.0 copy-start.2
  365.2 1.2 reduce_sum.18
  366.4 1.2 reduce_sum.19
  367.6 0.1 reshape.58
  367.7 0.0 copy-done.5
  367.7 0.6 div.7
  368.3 0.1 reshape.55
  368.4 0.0 copy-done.6
  368.4 0.6 div.6
  369.0 1.7 copy.52
  370.6 0.9 slice.22
  371.6 0.6 slice.26
  372.1 0.1 constant_dynamic-slice_fusion.1
  372.2 0.7 constant_dynamic-slice_fusion
  372.9 0.6 copy.55
  373.5 0.0 copy-done.3
  373.5 0.9 copy.63
  374.4 2.1 copy.64
  376.4 0.0 copy-done.2
  376.4 0.0 copy-start
  376.4 1.4 copy.65
  377.8 1.2 copy-done
  379.1 0.0 copy-start.1
  379.1 1.5 copy.66
  380.6 1.1 copy-done.1
  381.7 1.4 copy.67
  (5 shorter events, 0.0 us)
Async XLA Ops:
  4.5 5.4 %copy-start.4 = (f32[16,1792]{1,0:T(8,128)}, f32[16,1792]{1,0:T(8,128)S(1)}, u32[]{:S(2)}) copy-start(f32[16,1792]{1,0:T(8,128)S(1)} %dynamic_update_slice.3.refs_2_) | copy-start | bytes 344068
  152.6 215.1 %copy-start.5 = (f32[2,384]{1,0:T(2,128)S(1)}, f32[2,384]{1,0:T(2,128)}, u32[]{:S(2)}) copy-start(f32[2,384]{1,0:T(2,128)} %param.23) | copy-start | bytes 9220
  152.6 215.8 %copy-start.6 = (f32[2,192]{1,0:T(2,128)S(1)}, f32[2,192]{1,0:T(2,128)}, u32[]{:S(2)}) copy-start(f32[2,192]{1,0:T(2,128)} %param.17) | copy-start | bytes 4612
  152.6 220.9 %copy-start.3 = (f32[256,768]{1,0:T(8,128)S(1)}, f32[256,768]{1,0:T(8,128)}, u32[]{:S(2)}) copy-start(f32[256,768]{1,0:T(8,128)} %get-tuple-element.31) | copy-start | bytes 2359300
  365.2 11.3 %copy-start.2 = (f32[2,192,1536]{2,1,0:T(8,128)S(1)}, f32[2,192,1536]{2,1,0:T(8,128)}, u32[]{:S(2)}) copy-start(f32[2,192,1536]{2,1,0:T(8,128)} %get-tuple-element.109) | copy-start | bytes 7077892
  376.4 2.6 copy-start
  379.1 2.7 copy-start.1

commit v4 on v3

--- a/solution.py
+++ b/solution.py
@@ -265,7 +265,7 @@
 def forward_kernel(n_dp, n_seq, dims, *refs):
     (
         x_hbm, mask_ref, conv_ref, head_ref, norm_ref, gated_ref, wm_own, wg_own, wo_own, ws_own,
-        result_ref, conv_full, xs_out, gate_out, ext_out, step_out, mo_out, sin_out, sout_out, wm_out, wg_out, wo_out,
+        result_ref, conv_full, xs_out, gate_out, ext_out, step_out, mo_out, sin_out, sout_out, wm_out, wg_out, wo_out, lde_out, dte_out, mixed_out, ldt_out,
         WM, WG, WO, xs, gate, ext, step, mo, sin, sout, conv_in, mixed, diag, ldE, dtE, ldT, gm,
         g_send, g_recv, g_local, c_send, c_recv, e_send, e_recv, r_send, r_recv, o_sem,
     ) = refs
@@ -350,10 +350,14 @@
     def saved_copies(layer):
         saved = (
             (gate, gate_out), (ext, ext_out), (step, step_out), (mo, mo_out), (sin, sin_out), (sout, sout_out),
-            (WM, wm_out), (WG, wg_out), (WO, wo_out),
+            (WM, wm_out), (WG, wg_out), (WO, wo_out), (ldE, lde_out), (dtE, dte_out), (mixed, mixed_out),
+            (ldT, ldt_out),
         )
         return [
-            functools.partial(lambda a, b, k: pltpu.make_async_copy(a.at[layer], b.at[layer], o_sem.at[layer * 9 + k + 1]), a, b, k)
+            functools.partial(
+                lambda a, b, k: pltpu.make_async_copy(a.at[layer] if k < 9 else a, b.at[layer], o_sem.at[layer * 13 + k + 1]),
+                a, b, k,
+            )
             for k, (a, b) in enumerate(saved)
         ]
 
@@ -382,6 +386,12 @@
             edge.start()
 
         step[layer] = raw
+
+        @pl.when(layer > 0)
+        def _():
+            for copy in saved_copies(0)[9:]:
+                copy().wait()
+
         tick(base + mix_pieces - 1)
         saved_copies(layer)[6]().start()
         dt = softplus(raw + head[1:2, :])
@@ -435,6 +445,9 @@
             sout[layer, :, at] = mm(b_map, weighted, TN)
 
         tiles(DI // 256, local_state)
+
+        for copy in saved_copies(layer)[9:]:
+            copy().start()
 
         def relay_copy(chunk):
             at = lanes(chunk, CHUNK)
@@ -552,8 +565,9 @@
     for s in range(1, n_dp):
         conv_copy(s).wait_send()
     for layer in range(layers):
-        for copy in saved_copies(layer):
-            copy().wait()
+        for number, copy in enumerate(saved_copies(layer)):
+            if number < 9 or layer == layers - 1:
+                copy().wait()
     last.wait()
 
 
@@ -571,16 +585,16 @@
         functools.partial(forward_kernel, n_dp, n_seq, dims),
         out_shape=(
             sd(T, D), sd(16, CW), sd(T, D), sd(2, T, DI), sd(2, T + 8, CW), sd(2, T, LANES), sd(2, T, DI), sd(2, N, DI),
-            sd(2, N, DI), sd(2, D, CX), sd(2, D, DI), sd(2, DI, D),
+            sd(2, N, DI), sd(2, D, CX), sd(2, D, DI), sd(2, DI, D), sd(2, T, DI), sd(2, T, DI), sd(2, T, CW), sd(2, LANES, T),
         ),
         in_specs=[any_spec] + [vmem] * 5 + [any_spec] * 4,
-        out_specs=(vmem, vmem) + (any_spec,) * 10,
+        out_specs=(vmem, vmem) + (any_spec,) * 14,
         scratch_shapes=[
             v(2, D, CX), v(2, D, DI), v(2, DI, D), v(3, T, D), v(2, T, DI), v(2, T + 8, CW), v(2, T, LANES),
             v(2, T, DI), v(2, N, DI), v(2, N, DI), v(n_dp, 16, CW), v(T, CW), v(T, DI), v(T, DI), v(T, DI),
             v(LANES, T), v(T, T),
             dma((PIECES, kinds)), dma((PIECES, kinds)), dma((8,)), dma((n_dp - 1,)), dma((n_dp - 1,)), dma((2,)), dma((2,)),
-            dma((2, DI // 256)), dma((2, DI // 256)), dma((19,)),
+            dma((2, DI // 256)), dma((2, DI // 256)), dma((27,)),
         ],
         compiler_params=pltpu.CompilerParams(
             collective_id=0, has_side_effects=True, vmem_limit_bytes=61 << 20
@@ -628,7 +642,7 @@
         self.total_slots = 2 * self.slots + self.conv_jobs
         self.wide = n_dp == 4 and self.n_z == 4 and self.h % 32 == 0
         self.rounds = self.n_z.bit_length() - 1
-        self.offsets = (0, 1, 1, 4, 6, 8, 10, 12, 15, 16)
+        self.offsets = (0, 1, 1, 4, 7, 10, 13, 16, 19, 20)
         self.o_ring = self.offsets[4] + 1
         self.f_ring = max(self.offsets) + 1
         self.r_ring = self.offsets[4] - self.offsets[2] + 2
@@ -997,7 +1011,7 @@
     plan = Plan(n_dp, n_seq, dims)
     (
         cot_ref, mask_ref, conv_ref, head_ref, norm_ref, gated_ref, x0_hbm, x1_hbm, gate_hbm, ext_hbm, step_hbm, mo_hbm, sin_hbm,
-        sout_hbm, wm_hbm, wg_hbm, wo_hbm,
+        sout_hbm, wm_hbm, wg_hbm, wo_hbm, lde_hbm, dte_hbm, mixed_hbm, ldt_hbm,
         hg_ref, gm, gs, gg, go, gc, norm_out, gated_out,
         grad, x, gate, ext, step, mo, sin, sout, wrow, wcol, U, V, mixed, ldE, dtE, ldT, gmT, dgT, PG, raw, nT, gnT,
         NG, dS, dSin, maps, heads, convg, rows,
@@ -1025,7 +1039,7 @@
     def load_of(layer, k):
         source, target = (
             (mo_hbm, mo), (gate_hbm, gate), (step_hbm, step), (ext_hbm, ext), (sin_hbm, sin), (sout_hbm, sout),
-            (wo_hbm, wrow),
+            (wo_hbm, wrow), (lde_hbm, ldE), (dte_hbm, dtE), (mixed_hbm, mixed), (ldt_hbm, ldT),
         )[k]
         return pltpu.make_async_copy(source.at[layer], target, l_sem.at[k])
 
@@ -1036,17 +1050,17 @@
         def wait(self):
             load_of(self.layer, self.k).wait()
 
-    for k in range(7):
+    for k in (1, 0, 6, 7, 8, 9, 10, 2, 3, 4, 5):
         load_of(1, k).start()
 
     def load_x(layer_value, action):
         @pl.when(layer_value == 1)
         def _():
-            getattr(pltpu.make_async_copy(x1_hbm, x, l_sem.at[7]), action)()
+            getattr(pltpu.make_async_copy(x1_hbm, x, l_sem.at[11]), action)()
 
         @pl.when(layer_value == 0)
         def _():
-            getattr(pltpu.make_async_copy(x0_hbm, x, l_sem.at[7]), action)()
+            getattr(pltpu.make_async_copy(x0_hbm, x, l_sem.at[11]), action)()
 
     grad[...] = cot_ref[...] * mask_ref[...]
     PG[T : T + 8, :] = jnp.zeros((8, CW), F32)
@@ -1089,7 +1103,7 @@
         base = li * plan.slots
         first_job = li * plan.per_layer
         head = head_ref[layer]
-        loads = [Load(layer, k) for k in range(7)]
+        loads = [Load(layer, k) for k in range(11)]
         load_x(layer, "start")
 
         loads[0].wait()
@@ -1147,20 +1161,9 @@
         out_job(0)
         load_x(layer, "wait")
         inv_in = lax.rsqrt(jnp.mean(x[...] * x[...], axis=-1, keepdims=True) + EPSILON)
-        for copy in loads[2:6]:
+        for copy in loads[2:6] + loads[7:]:
             copy.wait()
         raw_step = step[...]
-        dt = softplus(raw_step + head[1:2, :])
-        ld = exact(tri(T).astype(jnp.bfloat16), -jnp.exp(head[0:1, :]) * dt)
-        ldT[...] = ld.T
-
-        def expand(i):
-            select = head_matrix(LANES, 256, PS, i * 256)
-            ldE[:, lanes(i, 256)] = exact_right(ld, select)
-            dtE[:, lanes(i, 256)] = exact_right(dt, select)
-
-        tiles(DI // 256, expand)
-
         def conv_value(at):
             taps = conv_ref[pl.ds(pl.multiple_of(layer * 8, 8), 8), at]
             total = taps[K : K + 1, :]
@@ -1168,12 +1171,6 @@
                 total = total + taps[k : k + 1, :] * ext[8 - K + 1 + k : 8 - K + 1 + k + T, at]
             return taps, total
 
-        def conv(i):
-            at = lanes(i, 256)
-            total = conv_value(at)[1]
-            mixed[:, at] = total * sigmoid(total)
-
-        tiles(CW // 256, conv)
         out_job(1)
         b_map = mixed[:, DI : DI + N]
         c_map = mixed[:, DI + N : DI + 2 * N]
@@ -1368,7 +1365,7 @@
 
         @pl.when(li == 0)
         def _():
-            for k in range(6):
+            for k in (1, 0, 7, 8, 9, 10, 2, 3, 4, 5):
                 load_of(0, k).start()
 
         def last_pieces(g):
@@ -1449,7 +1446,7 @@
             sd(T, D), sd(2, 2 * h, CW), sd(2, 2 * h, LANES), sd(2, 2 * h, DI), sd(2, 4 * h, D),
             sd(plan.conv_jobs, 2, h, CHUNK_N), sd(2, 2, h, LANES), sd(2, 2, 2 * h, LANES),
         ),
-        in_specs=[vmem] * 6 + [any_spec] * 11,
+        in_specs=[vmem] * 6 + [any_spec] * 15,
         out_specs=(vmem,) + (any_spec,) * 7,
         scratch_shapes=[
             v(T, D), v(T, D), v(T, DI), v(T + 8, CW), v(T, LANES), v(T, DI), v(N, DI), v(N, DI),
@@ -1459,7 +1456,7 @@
             v(plan.s_ring, n_dp, h, CHUNK_N), v(plan.in_ring, n_dp, h, CHUNK_N), v(plan.o_ring, n_dp, h, CHUNK_N), *received,
             v(plan.f_ring, h, CHUNK_N), v(plan.f_ring, h, CHUNK_N) if plan.wide else v(8, LANES), v(2, 8, CW),
             v(plan.w_ring, h, CHUNK_N), v(2, h, LANES), v(2, 2 * h, LANES),
-            dma((J, plan.kinds + 1)), dma((J, plan.kinds + 1)), dma((plan.s_ring,)), dma((2, plan.f_ring)), dma((plan.w_ring,)), dma((6,)), dma((8,)),
+            dma((J, plan.kinds + 1)), dma((J, plan.kinds + 1)), dma((plan.s_ring,)), dma((2, plan.f_ring)), dma((plan.w_ring,)), dma((6,)), dma((12,)),
             dma((3,)), dma((2,)), dma((2, DI // CHUNK_N + 1)), dma((2, DI // CHUNK_N + 1)), dma((2, DI // 256)), dma((2, DI // 256)),
         ],
         compiler_params=pltpu.CompilerParams(

time: 384 us -> 375 us (0.977)
  Pallas kernels: 355 us -> 347 us
    pallas_call x1, Pallas kernels: 213 us -> 204 us  [backward(): pl.pallas_call(functools.partial(backward_kernel, n_dp, n_seq, dims), out...]
where the time goes in v4:
time: 375 us
  Pallas kernels  347 us (93%)
  local copies, waits for them, and re-layouts  20.2 us (5%)
  other arithmetic  6.34 us (2%)
    pallas_call x1, Pallas kernels, backward(): pl.pallas_call(functools.partial(backward_kernel, n_dp, n_seq, dims), out...  204 us
    pallas_call x1, Pallas kernels, forward(): pl.pallas_call(functools.partial(forward_kernel, n_dp, n_seq, dims), out_...  143 us
    unnamed x22, local copies, waits for them, and re-layouts  12.8 us

profile of v4, /device:TPU:0, one launch (start us, length us, event | category | flops | bytes accessed | tf_op | source)
XLA Modules:
  0.0 374.7 jit_solution(476387643545745744)
XLA Ops:
  1.3 0.7 copy.45
  2.0 1.3 select_maximum_fusion.1.refs_3_
  3.3 0.7 fusion.1
  4.1 0.5 dynamic_update_slice.3.refs_2_
  4.5 0.0 copy-start.4
  4.5 0.7 fusion.refs_1_
  5.2 1.5 broadcast_in_dim.27.refs_4_
  6.7 0.9 copy.49
  7.6 0.7 pad.14.refs_9_
  8.3 1.6 broadcast_in_dim.28.refs_5_
  9.9 0.0 copy-done.4
  9.9 142.8 %forward.1 = (f32[256,768]{1,0:T(8,128)}, f32[16,1792]{1,0:T(8,128)}, f32[256,768]{1,0:T(8,128)}, f32[2,256,1536]{2,1,0:T(8,128)}, f32[2,264,1792]{2,1,0:T(8,128...) custom-call(f32[256,768]{1,0:T(8,128)} %bitcast.30, ...), custom_call_target="tpu_custom_call" | custom-call | tf_op jit(solution)/shard_map/forward/pallas_call | solution.py:584
  152.7 0.0 copy-start.5
  152.7 0.0 copy-start.6
  152.7 0.0 copy-start.3
  152.7 204.1 %backward.1 = (f32[256,768]{1,0:T(8,128)}, f32[2,192,1792]{2,1,0:T(8,128)}, f32[2,192,128]{2,1,0:T(8,128)}, f32[2,192,1536]{2,1,0:T(8,128)}, f32[2,384,768]{2,1,...) custom-call(f32[256,768]{1,0:T(8,128)} %bitcast.32, ...), custom_call_target="tpu_custom_call" | custom-call | tf_op jit(solution)/shard_map/backward/pallas_call | solution.py:1443
  356.8 0.0 copy-start.2
  356.8 1.2 reduce_sum.18
  358.0 1.2 reduce_sum.19
  359.2 0.1 reshape.58
  359.3 0.0 copy-done.5
  359.3 0.6 div.7
  359.9 0.1 reshape.55
  360.0 0.0 copy-done.6
  360.0 0.6 div.6
  360.6 1.7 copy.52
  362.2 0.9 slice.22
  363.2 0.6 slice.26
  363.7 0.1 constant_dynamic-slice_fusion.1
  363.8 0.7 constant_dynamic-slice_fusion
  364.5 0.6 copy.55
  365.1 0.0 copy-done.3
  365.1 0.9 copy.63
  366.0 2.1 copy.64
  368.0 0.0 copy-done.2
  368.0 0.0 copy-start
  368.0 1.4 copy.65
  369.4 1.2 copy-done
  370.7 0.0 copy-start.1
  370.7 1.5 copy.66
  372.2 1.1 copy-done.1
  373.3 1.4 copy.67
  (5 shorter events, 0.0 us)
Async XLA Ops:
  4.5 5.4 %copy-start.4 = (f32[16,1792]{1,0:T(8,128)}, f32[16,1792]{1,0:T(8,128)S(1)}, u32[]{:S(2)}) copy-start(f32[16,1792]{1,0:T(8,128)S(1)} %dynamic_update_slice.3.refs_2_) | copy-start | bytes 344068
  152.7 206.6 %copy-start.5 = (f32[2,384]{1,0:T(2,128)S(1)}, f32[2,384]{1,0:T(2,128)}, u32[]{:S(2)}) copy-start(f32[2,384]{1,0:T(2,128)} %param.23) | copy-start | bytes 9220
  152.7 207.3 %copy-start.6 = (f32[2,192]{1,0:T(2,128)S(1)}, f32[2,192]{1,0:T(2,128)}, u32[]{:S(2)}) copy-start(f32[2,192]{1,0:T(2,128)} %param.17) | copy-start | bytes 4612
  152.7 212.4 %copy-start.3 = (f32[256,768]{1,0:T(8,128)S(1)}, f32[256,768]{1,0:T(8,128)}, u32[]{:S(2)}) copy-start(f32[256,768]{1,0:T(8,128)} %get-tuple-element.35) | copy-start | bytes 2359300
  356.8 11.3 %copy-start.2 = (f32[2,192,1536]{2,1,0:T(8,128)S(1)}, f32[2,192,1536]{2,1,0:T(8,128)}, u32[]{:S(2)}) copy-start(f32[2,192,1536]{2,1,0:T(8,128)} %get-tuple-element.117) | copy-start | bytes 7077892
  368.0 2.6 copy-start
  370.7 2.7 copy-start.1
